TPU v7x, 32 devices: a whole 2x2x4 slice. The times are simulated.
32 devices in a mesh: dp: 8 (over y, x, core), tensor: 4 (over z).
Axes of the slice: x: 2, y: 2, z: 4, core: 2. Of those that a mesh axis runs over, the one named last changes fastest.
Arguments:
- inputs_short: bfloat16 [16, 512, 1024], P('dp', 'tensor'), may hold values from -6 to 6
- memory_short: bfloat16 [16, 512, 1024], P('dp', 'tensor'), may hold values from -6 to 6
- compressed_short: bfloat16 [16, 512, 1024], P('dp', 'tensor'), may hold values from -6 to 6
- offsets_short: int32 [16], P('dp'), may hold values from 0 to 1024, as said below
- inputs_long: bfloat16 [8, 1024, 1024], P('dp', 'tensor'), may hold values from -6 to 6
- memory_long: bfloat16 [8, 1024, 1024], P('dp', 'tensor'), may hold values from -6 to 6
- compressed_long: bfloat16 [8, 1024, 1024], P('dp', 'tensor'), may hold values from -6 to 6
- offsets_long: int32 [8], P('dp'), may hold values from 0 to 2048, as said below
- query_weight: bfloat16 [1024, 1024], P(None, 'tensor'), may hold values from -0.1875 to 0.1875
- key_weight: bfloat16 [1024, 1024], P(None, 'tensor'), may hold values from -0.1875 to 0.1875
- value_weight: bfloat16 [1024, 1024], P(None, 'tensor'), may hold values from -0.1875 to 0.1875
- out_weight: bfloat16 [1024, 1024], P('tensor'), may hold values from -4 to 4
- up_weight: bfloat16 [1024, 4096], P(None, 'tensor'), may hold values from -0.1875 to 0.1875
- down_weight: bfloat16 [4096, 1024], P('tensor'), may hold values from -0.09375 to 0.09375
- compress_weight: bfloat16 [3, 1024, 1024], P(None, None, 'tensor'), may hold values from -0.109375 to 0.109375
- attention_gain: float32 [1024], replicated, may hold values from 0.5 to 1.5
- feedforward_gain: float32 [1024], replicated, may hold values from 0.5 to 1.5
- cotangent_short: bfloat16 [16, 512, 1024], P('dp', 'tensor'), may hold values from -6 to 6
- cotangent_long: bfloat16 [8, 1024, 1024], P('dp', 'tensor'), may hold values from -6 to 6
Outputs:
- output_short: bfloat16 [16, 512, 1024], P('dp', 'tensor')
- output_long: bfloat16 [8, 1024, 1024], P('dp', 'tensor')
- grad_inputs_short: float32 [16, 512, 1024], P('dp', 'tensor')
- grad_inputs_long: float32 [8, 1024, 1024], P('dp', 'tensor')
- appended_short: bfloat16 [16, 170, 1024], P('dp', None, 'tensor')
- appended_long: bfloat16 [8, 341, 1024], P('dp', None, 'tensor')
- grad_query_weight: float32 [1024, 1024], P(None, 'tensor')
- grad_key_weight: float32 [1024, 1024], P(None, 'tensor')
- grad_value_weight: float32 [1024, 1024], P(None, 'tensor')
- grad_out_weight: float32 [1024, 1024], P('tensor')
- grad_up_weight: float32 [1024, 4096], P(None, 'tensor')
- grad_down_weight: float32 [4096, 1024], P('tensor')
- grad_compress_weight: float32 [3, 1024, 1024], P(None, None, 'tensor')
- grad_attention_gain: float32 [1024], replicated
- grad_feedforward_gain: float32 [1024], replicated
- rebuild_loss: float32 [], replicated
Inputs may be any that keep to these rules, and one draw needn't show every extreme that they name: `offsets_short`: number of leading rows without data in a short sequence; some sequence has none and some has all 1024. `offsets_long`: number of leading rows without data in a long sequence; some sequence has none and some has all 2048.
All inputs are finite; a program needn't handle non-finite values.
Results may differ from a plain program's by a relative error of at most 0.02.
Values may be sent and summed in bfloat16 or wider, within the bound.
A program may use at most 256 MiB of HBM per device.

v0:
```python
import jax
import jax.numpy as jnp
from jax import lax
from jax.sharding import PartitionSpec as P

HEAD_SIZE = 128


epsilon = 1e-05
rebuild_weight = 256.0
masked_value = -1e30


def for_sending(value):

    def short(part):
        return part.astype(jnp.bfloat16) if part.dtype == jnp.float32 else part

    return jax.tree.map(short, value)


def normalize(rows):
    mean = jnp.mean(rows, -1, keepdims=True)
    centred = rows - mean
    inverse = lax.rsqrt(jnp.mean(centred * centred, -1, keepdims=True) + epsilon)
    return (centred * inverse, inverse)


def norm_back(grad_out, gain, unit, inverse):
    scaled = grad_out * gain
    return inverse * (
        scaled
        - jnp.mean(scaled, -1, keepdims=True)
        - unit * jnp.mean(scaled * unit, -1, keepdims=True)
    )


def to_heads(array, heads):
    return array.reshape(array.shape[0], heads, HEAD_SIZE)


def scores_of(query, key, validity):
    scores = jnp.einsum(
        "qhd,khd->hqk", query, key, preferred_element_type=jnp.float32
    ) * HEAD_SIZE ** (-0.5)
    if validity is None:
        return scores
    return jnp.where(validity[None], scores, masked_value)


def attend(query, key, value, validity):
    scores = scores_of(query, key, validity)
    top = jnp.max(scores, -1, keepdims=True)
    shifted = jnp.exp(scores - top)
    total = jnp.sum(shifted, -1, keepdims=True)
    probs = shifted / total
    result = jnp.einsum(
        "hqk,khd->qhd", probs.astype(jnp.bfloat16), value, preferred_element_type=jnp.float32
    )
    return (result, (top + jnp.log(total))[..., 0])


def attend_back(query, key, value, validity, log_total, grad_result):
    scores = scores_of(query, key, validity)
    probs = jnp.exp(scores - log_total[..., None])
    grad_value = jnp.einsum(
        "hqk,qhd->khd", probs.astype(jnp.bfloat16), grad_result, preferred_element_type=jnp.float32
    )
    grad_probs = jnp.einsum("qhd,khd->hqk", grad_result, value, preferred_element_type=jnp.float32)
    grad_scores = (probs * (grad_probs - jnp.sum(grad_probs * probs, -1, keepdims=True))).astype(
        jnp.bfloat16
    )
    scale = HEAD_SIZE ** (-0.5)
    grad_query = (
        jnp.einsum("hqk,khd->qhd", grad_scores, key, preferred_element_type=jnp.float32) * scale
    )
    grad_key = (
        jnp.einsum("hqk,qhd->khd", grad_scores, query, preferred_element_type=jnp.float32) * scale
    )
    return (grad_query, grad_key, grad_value)


def group_layer(inputs, memory, older, offsets, cotangent, weights):
    (
        query_projection_weight,
        key_w,
        value_w,
        output_projection_weight,
        up_projection_weight,
        down_projection_weight,
        squeeze_w,
        attention_gain,
        feedforward_gain,
    ) = weights
    count = inputs.shape[0]
    width = inputs.shape[2]
    local_width = query_projection_weight.shape[1]
    heads = local_width // HEAD_SIZE
    unit_tokens, inverse_tokens = normalize(inputs.astype(jnp.float32))
    normed_tokens = (unit_tokens * attention_gain).astype(jnp.bfloat16)
    entire_tokens, whole_memory, whole_older = (
        lax.all_gather(normed_tokens, "tensor", axis=1, tiled=True),
        lax.all_gather(memory, "tensor", axis=1, tiled=True),
        lax.all_gather(older, "tensor", axis=1, tiled=True),
    )
    length = entire_tokens.shape[1]
    reduced = length // 3
    unit_memory = normalize(jnp.concatenate([whole_older, whole_memory], 1).astype(jnp.float32))[0]
    memory_rows = (unit_memory * attention_gain).astype(jnp.bfloat16)
    incoming_keys = jnp.concatenate([memory_rows, entire_tokens], 1)
    pairwise_weight = jnp.concatenate([key_w, value_w], 1)
    queries = jnp.einsum(
        "qfc,cp->qfp", entire_tokens, query_projection_weight, preferred_element_type=jnp.float32
    ).astype(jnp.bfloat16)
    pairs = jnp.einsum(
        "qfc,cp->qfp", incoming_keys, pairwise_weight, preferred_element_type=jnp.float32
    ).astype(jnp.bfloat16)
    stacked = whole_memory[:, : 3 * reduced].reshape(count, reduced, 3 * width)
    appended_local = jnp.einsum(
        "srk,ke->sre",
        stacked,
        squeeze_w.reshape(3 * width, local_width),
        preferred_element_type=jnp.float32,
    ).astype(jnp.bfloat16)
    appended_whole = lax.all_gather(appended_local, "tensor", axis=2, tiled=True)
    unit_added, inverse_added = normalize(appended_whole.astype(jnp.float32))
    added_rows = (unit_added * attention_gain).astype(jnp.bfloat16)
    added_pairs = jnp.einsum(
        "srd,de->sre", added_rows, pairwise_weight, preferred_element_type=jnp.float32
    ).astype(jnp.bfloat16)
    query_place = jnp.arange(length)[:, None]
    key_place = jnp.arange(3 * length)[None, :]
    attended = []
    saved = []
    square_sum = jnp.zeros((), jnp.float32)
    for index in range(count):
        validity = jnp.where(
            key_place < 2 * length,
            key_place >= offsets[index],
            key_place - 2 * length <= query_place,
        )
        query = to_heads(queries[index], heads)
        key = to_heads(pairs[index, :, :local_width], heads)
        value = to_heads(pairs[index, :, local_width:], heads)
        added_key = to_heads(added_pairs[index, :, :local_width], heads)
        added_value = to_heads(added_pairs[index, :, local_width:], heads)
        result, log_main = attend(query, key, value, validity)
        rebuilt_memory, log_memory = attend(
            query, key[length : 2 * length], value[length : 2 * length], None
        )
        rebuilt_added, log_added = attend(query, added_key, added_value, None)
        differ = rebuilt_memory - rebuilt_added
        square_sum = square_sum + jnp.sum(differ * differ)
        attended.append(result.astype(jnp.bfloat16).reshape(length, local_width))
        saved.append(
            (validity, query, key, value, added_key, added_value, log_main, log_added, differ)
        )
    attention_complete = jnp.stack(attended)
    branch = lax.psum_scatter(
        jnp.einsum(
            "owa,au->owu",
            attention_complete,
            output_projection_weight,
            preferred_element_type=jnp.float32,
        ).astype(jnp.bfloat16),
        "tensor",
        scatter_dimension=1,
        tiled=True,
    ).astype(jnp.float32)
    hidden_state = inputs.astype(jnp.float32) + branch
    unit_hidden, inverse_hidden = normalize(hidden_state)
    feedforward_entire = lax.all_gather(
        (unit_hidden * feedforward_gain).astype(jnp.bfloat16), "tensor", axis=1, tiled=True
    )
    preactivation = jnp.einsum(
        "urc,ch->urh", feedforward_entire, up_projection_weight, preferred_element_type=jnp.float32
    )
    activated, gelu_back = jax.vjp(jax.nn.gelu, preactivation)
    activated_reduced = activated.astype(jnp.bfloat16)
    feedforward = lax.psum_scatter(
        jnp.einsum(
            "qer,rz->qez",
            activated_reduced,
            down_projection_weight,
            preferred_element_type=jnp.float32,
        ).astype(jnp.bfloat16),
        "tensor",
        scatter_dimension=1,
        tiled=True,
    ).astype(jnp.float32)
    output = (hidden_state + feedforward).astype(jnp.bfloat16)
    cotangent_entire = lax.all_gather(cotangent, "tensor", axis=1, tiled=True)
    grad_down_w = jnp.einsum(
        "jkg,jki->gi", activated_reduced, cotangent_entire, preferred_element_type=jnp.float32
    )
    grad_activated = jnp.einsum(
        "vhr,mr->vhm", cotangent_entire, down_projection_weight, preferred_element_type=jnp.float32
    )
    grad_preactivation = gelu_back(grad_activated)[0].astype(jnp.bfloat16)
    grad_up_projection_weight = jnp.einsum(
        "aji,ajr->ir", feedforward_entire, grad_preactivation, preferred_element_type=jnp.float32
    )
    grad_ff = lax.psum_scatter(
        jnp.einsum(
            "zar,vr->zav",
            grad_preactivation,
            up_projection_weight,
            preferred_element_type=jnp.float32,
        ).astype(jnp.bfloat16),
        "tensor",
        scatter_dimension=1,
        tiled=True,
    ).astype(jnp.float32)
    feed_gain_part = jnp.sum(grad_ff * unit_hidden, (0, 1))
    grad_hidden = cotangent.astype(jnp.float32) + norm_back(
        grad_ff, feedforward_gain, unit_hidden, inverse_hidden
    )
    grad_hidden_low = grad_hidden.astype(jnp.bfloat16)
    branch_entire = lax.all_gather(grad_hidden_low, "tensor", axis=1, tiled=True)
    grad_out_w = jnp.einsum(
        "qnw,qny->wy", attention_complete, branch_entire, preferred_element_type=jnp.float32
    )
    grad_attention = jnp.einsum(
        "pcm,fm->pcf", branch_entire, output_projection_weight, preferred_element_type=jnp.float32
    ).astype(jnp.bfloat16)
    grad_queries = []
    grad_pairs = []
    grad_added = []
    for index in range(count):
        validity, query, key, value, added_key, added_value, log_main, log_added, differ = saved[
            index
        ]
        main_query, main_key, main_value = attend_back(
            query, key, value, validity, log_main, to_heads(grad_attention[index], heads)
        )
        pushed = -2.0 * rebuild_weight * differ
        unused_query, added_key_grad, added_value_grad = attend_back(
            query, added_key, added_value, None, log_added, pushed.astype(jnp.bfloat16)
        )
        grad_queries.append(main_query.astype(jnp.bfloat16).reshape(length, local_width))
        grad_pairs.append(
            jnp.concatenate(
                [
                    main_key.reshape(3 * length, local_width),
                    main_value.reshape(3 * length, local_width),
                ],
                1,
            ).astype(jnp.bfloat16)
        )
        grad_added.append(
            jnp.concatenate(
                [
                    added_key_grad.reshape(reduced, local_width),
                    added_value_grad.reshape(reduced, local_width),
                ],
                1,
            ).astype(jnp.bfloat16)
        )
    grad_query_complete = jnp.stack(grad_queries)
    grad_pair_complete = jnp.stack(grad_pairs)
    grad_added_all = jnp.stack(grad_added)
    grad_query_w = jnp.einsum(
        "pxv,pxf->vf", entire_tokens, grad_query_complete, preferred_element_type=jnp.float32
    )
    grad_pair_w = jnp.einsum(
        "pxv,pxf->vf", incoming_keys, grad_pair_complete, preferred_element_type=jnp.float32
    )
    grad_keys_in = jnp.einsum(
        "azr,pr->azp", grad_pair_complete, pairwise_weight, preferred_element_type=jnp.float32
    )
    grad_token_rows = grad_keys_in[:, 2 * length :] + jnp.einsum(
        "azr,pr->azp",
        grad_query_complete,
        query_projection_weight,
        preferred_element_type=jnp.float32,
    )
    attention_gain_part = jnp.sum(grad_keys_in[:, : 2 * length] * unit_memory, (0, 1))
    grad_added_norm = jnp.einsum(
        "sre,de->srd", grad_added_all, pairwise_weight, preferred_element_type=jnp.float32
    )
    added_full = lax.psum(grad_added_norm.astype(jnp.bfloat16), "tensor").astype(jnp.float32)
    grad_appended = norm_back(added_full, attention_gain, unit_added, inverse_added).astype(
        jnp.bfloat16
    )
    grad_appended_local = lax.dynamic_slice_in_dim(
        grad_appended, lax.axis_index("tensor") * local_width, local_width, 2
    )
    grad_squeeze_w = jnp.einsum(
        "srk,sre->ke", stacked, grad_appended_local, preferred_element_type=jnp.float32
    ).reshape(3, width, local_width)
    grad_token_norm = lax.psum_scatter(
        grad_token_rows.astype(jnp.bfloat16), "tensor", scatter_dimension=1, tiled=True
    ).astype(jnp.float32)
    attention_gain_part = attention_gain_part + jnp.sum(grad_token_norm * unit_tokens, (0, 1))
    grad_inputs = grad_hidden + norm_back(
        grad_token_norm, attention_gain, unit_tokens, inverse_tokens
    )
    grads = (
        grad_query_w,
        grad_pair_w[:, :local_width],
        grad_pair_w[:, local_width:],
        grad_out_w,
        grad_up_projection_weight,
        grad_down_w,
        grad_squeeze_w,
    )
    return (
        output,
        grad_inputs,
        appended_local,
        grads,
        attention_gain_part,
        feed_gain_part,
        square_sum,
        count * length,
    )


def per_device(
    inputs_short,
    memory_short,
    compressed_short,
    offsets_short,
    inputs_long,
    memory_long,
    compressed_long,
    offsets_long,
    query_weight,
    key_weight,
    value_weight,
    out_weight,
    up_weight,
    down_weight,
    compress_weight,
    attention_gain,
    feedforward_gain,
    cotangent_short,
    cotangent_long,
):
    weights = (
        query_weight,
        key_weight,
        value_weight,
        out_weight,
        up_weight,
        down_weight,
        compress_weight,
        attention_gain,
        feedforward_gain,
    )
    short_result = group_layer(
        inputs_short, memory_short, compressed_short, offsets_short, cotangent_short, weights
    )
    long_result = group_layer(
        inputs_long, memory_long, compressed_long, offsets_long, cotangent_long, weights
    )
    summed = jax.tree.map(jnp.add, short_result[3], long_result[3])
    summed = jax.tree.map(
        lambda part: part.astype(jnp.float32), lax.psum(for_sending(summed), "dp")
    )
    gain_one, gain_two, square_total = lax.psum(
        (
            short_result[4] + long_result[4],
            short_result[5] + long_result[5],
            short_result[6] + long_result[6],
        ),
        ("dp", "tensor"),
    )
    rows_all = (short_result[7] + long_result[7]) * lax.axis_size("dp")
    loss = square_total / rows_all
    return (
        short_result[0],
        long_result[0],
        short_result[1],
        long_result[1],
        short_result[2],
        long_result[2],
        summed[0],
        summed[1],
        summed[2],
        summed[3],
        summed[4],
        summed[5],
        summed[6],
        gain_one,
        gain_two,
        loss,
    )


def solution(mesh):
    in_specs = (
        P("dp", "tensor", None),
        P("dp", "tensor", None),
        P("dp", "tensor", None),
        P("dp"),
        P("dp", "tensor", None),
        P("dp", "tensor", None),
        P("dp", "tensor", None),
        P("dp"),
        P(None, "tensor"),
        P(None, "tensor"),
        P(None, "tensor"),
        P("tensor", None),
        P(None, "tensor"),
        P("tensor", None),
        P(None, None, "tensor"),
        P(),
        P(),
        P("dp", "tensor", None),
        P("dp", "tensor", None),
    )
    out_specs = (
        P("dp", "tensor", None),
        P("dp", "tensor", None),
        P("dp", "tensor", None),
        P("dp", "tensor", None),
        P("dp", None, "tensor"),
        P("dp", None, "tensor"),
        P(None, "tensor"),
        P(None, "tensor"),
        P(None, "tensor"),
        P("tensor", None),
        P(None, "tensor"),
        P("tensor", None),
        P(None, None, "tensor"),
        P(),
        P(),
        P(),
    )
    return jax.shard_map(
        per_device, mesh=mesh, in_specs=in_specs, out_specs=out_specs, check_vma=False
    )
```

profile of v0, /device:TPU:1, one launch (start us, length us, event | category | flops | bytes accessed | tf_op | source)
XLA Modules:
  0.0 1282.3 jit_solution(18263462736623742670)
XLA Ops:
  28.4 29.3 %all-gather.24.cloned.1.call-done = bf16[1,1024,1024]{2,1,0:T(8,128)(2,1)} async-done(((bf16[1,256,1024]{2,1,0:T(8,128)(2,1)}), bf16[1,1024,1024]{2,1,0:T(8,128)(2,1)}) %all-gather.24.cloned.1.call-update) | async-done | bytes 2097168 | tf_op jit(solution)/shard_map/all_gather | solution.py:103
  57.7 46.3 %all-gather.22.cloned.1.call-done = bf16[1,1024,1024]{2,1,0:T(8,128)(2,1)} async-done(((bf16[1,256,1024]{2,1,0:T(8,128)(2,1)}), bf16[1,1024,1024]{2,1,0:T(8,128)(2,1)}) %all-gather.22.cloned.1.call-update) | async-done | bytes 2097168 | tf_op jit(solution)/shard_map/all_gather | solution.py:104
  106.8 43.4 %all-gather.16.cloned.1.call-done = bf16[2,512,1024]{2,1,0:T(8,128)(2,1)} async-done(((bf16[2,128,1024]{2,1,0:T(8,128)(2,1)}), bf16[2,512,1024]{2,1,0:T(8,128)(2,1)}) %all-gather.16.cloned.1.call-update) | async-done | bytes 2097168 | tf_op jit(solution)/shard_map/all_gather | solution.py:103
  150.2 46.1 %all-gather.14.cloned.1.call-done = bf16[2,512,1024]{2,1,0:T(8,128)(2,1)} async-done(((bf16[2,128,1024]{2,1,0:T(8,128)(2,1)}), bf16[2,512,1024]{2,1,0:T(8,128)(2,1)}) %all-gather.14.cloned.1.call-update) | async-done | bytes 2097168 | tf_op jit(solution)/shard_map/all_gather | solution.py:104
  203.8 39.2 %all-gather.18.cloned.1.call-done = bf16[2,512,1024]{2,1,0:T(8,128)(2,1)} async-done(((bf16[2,128,1024]{2,1,0:T(8,128)(2,1)}), bf16[2,512,1024]{2,1,0:T(8,128)(2,1)}) %all-gather.18.cloned.1.call-update) | async-done | bytes 2097168 | tf_op jit(solution)/shard_map/all_gather | solution.py:102
  260.0 29.1 %all-gather.26.cloned.1.call-done = bf16[1,1024,1024]{2,1,0:T(8,128)(2,1)} async-done(((bf16[1,256,1024]{2,1,0:T(8,128)(2,1)}), bf16[1,1024,1024]{2,1,0:T(8,128)(2,1)}) %all-gather.26.cloned.1.call-update) | async-done | bytes 2097168 | tf_op jit(solution)/shard_map/all_gather | solution.py:102
  289.1 6.5 fusion.51
  322.6 13.3 %fusion.357 = (f32[2,1024]{1,0:T(2,128)S(1)}, f32[2,1024,3072]{2,1,0:T(8,128)}) fusion(bf16[1024,2,128]{0,2,1:T(8,128)(2,1)S(1)} %bitcast.327, bf16[3072,2,128]{0,2,1:T(8,128)(2,1)S(1)} %bitcast.353, pred[1024,3072]{1,0:T(8,128)(4,1)} %fusion.8), kind=kOutput, calls=%fused_computation.483 | convolution fusion | flops 1629485056 | bytes 30416896 | tf_op jit(solution)/shard_map/qhd,khd->hqk/dot_general | solution.py:43
  335.9 11.2 fusion.3
  347.2 10.9 fusion.160
  367.9 40.8 %reduce-scatter.13.cloned.1.call-done = bf16[1,256,1024]{2,1,0:T(8,128)(2,1)} async-done(((bf16[1,1024,1024]{2,1,0:T(8,128)(2,1)}), bf16[1,256,1024]{2,1,0:T(8,128)(2,1)}) %reduce-scatter.13.cloned.1.call-update) | async-done | bytes 524304 | tf_op jit(solution)/shard_map/reduce_scatter | solution.py:159
  423.1 27.2 %all_gather.54 = bf16[2,170,1024]{2,1,0:T(8,128)(2,1)S(1)} all-gather(bf16[2,170,256]{2,1,0:T(8,128)(2,1)S(1)} %convolution_convert_fusion.8), channel_id=1, replica_groups=mesh['dp'=8,'tensor'=4] {'tensor'}, dimensions={2}, use_global_device_ids=true | all-gather | bytes 870400 | tf_op jit(solution)/shard_map/all_gather | solution.py:125
  494.9 26.6 %all-gather = bf16[341,1024]{1,0:T(8,128)(2,1)S(1)} all-gather(bf16[341,256]{1,0:T(8,128)(2,1)S(1)} %convolution_convert_fusion.9), channel_id=2, replica_groups=mesh['dp'=8,'tensor'=4] {'tensor'}, dimensions={1}, use_global_device_ids=true | all-gather | bytes 872960 | tf_op jit(solution)/shard_map/all_gather | solution.py:125
  540.1 7.2 fusion.362
  549.6 4.5 fusion.50
  562.1 5.9 fusion.103
  568.0 7.9 fusion.37
  581.6 5.9 fusion.92
  587.5 30.1 %all-gather.34.cloned.1.call-done = bf16[1,1024,1024]{2,1,0:T(8,128)(2,1)} async-done(((bf16[1,256,1024]{2,1,0:T(8,128)(2,1)}), bf16[1,1024,1024]{2,1,0:T(8,128)(2,1)}) %all-gather.34.cloned.1.call-update) | async-done | bytes 2097168 | tf_op jit(solution)/shard_map/all_gather | solution.py:192
  617.6 8.0 fusion.44
  635.2 48.3 %all-reduce.8.cloned.1.call-done = (bf16[2,170,1024]{2,1,0:T(8,128)(2,1)}, bf16[1,341,1024]{2,1,0:T(8,128)(2,1)}) async-done(((bf16[2,170,1024]{2,1,0:T(8,128)(2,1)}, bf16[1,341,1024]{2,1,0:T(8,128)(2,1)}), (bf16[2,170,1024]{2,1,0:T(8,128)(2,1)}, bf16[1,341,1024]{2,1,0:T(8,128)(2,1)})) %all-reduce.8.cloned.1.call-update) | async-done | bytes 1394704 | tf_op jit(solution)/shard_map/psum | solution.py:281
  701.7 4.4 fusion.90
  706.1 23.3 %reduce-scatter.17.cloned.1.call-done = bf16[2,128,1024]{2,1,0:T(8,128)(2,1)} async-done(((bf16[2,512,1024]{2,1,0:T(8,128)(2,1)}), bf16[2,128,1024]{2,1,0:T(8,128)(2,1)}) %reduce-scatter.17.cloned.1.call-update) | async-done | bytes 524304 | tf_op jit(solution)/shard_map/reduce_scatter | solution.py:203
  734.3 7.5 fusion.48
  744.7 4.3 fusion.47
  749.1 25.8 %reduce-scatter.21.cloned.1.call-done = bf16[1,256,1024]{2,1,0:T(8,128)(2,1)} async-done(((bf16[1,1024,1024]{2,1,0:T(8,128)(2,1)}), bf16[1,256,1024]{2,1,0:T(8,128)(2,1)}) %reduce-scatter.21.cloned.1.call-update) | async-done | bytes 524304 | tf_op jit(solution)/shard_map/reduce_scatter | solution.py:203
  778.9 43.2 %all-gather.32.cloned.1.call-done = bf16[2,512,1024]{2,1,0:T(8,128)(2,1)} async-done(((bf16[2,128,1024]{2,1,0:T(8,128)(2,1)}), bf16[2,512,1024]{2,1,0:T(8,128)(2,1)}) %all-gather.32.cloned.1.call-update) | async-done | bytes 2097168 | tf_op jit(solution)/shard_map/all_gather | solution.py:219
  824.6 4.6 multiply_reduce_fusion.3
  845.3 23.6 %all-gather.36.cloned.1.call-done = bf16[1,1024,1024]{2,1,0:T(8,128)(2,1)} async-done(((bf16[1,256,1024]{2,1,0:T(8,128)(2,1)}), bf16[1,1024,1024]{2,1,0:T(8,128)(2,1)}) %all-gather.36.cloned.1.call-update) | async-done | bytes 2097168 | tf_op jit(solution)/shard_map/all_gather | solution.py:219
  871.2 11.9 fusion.56
  883.1 15.4 %multiply_reduce_fusion = (f32[2,1024]{1,0:T(2,128)S(1)}, f32[2,1024,3072]{2,1,0:T(8,128)}) fusion(f32[2,1024,3072]{2,1,0:T(8,128)} %get-tuple-element.121, f32[2,1024]{1,0:T(2,128)S(1)} %log_add_fusion.1, bf16[1024,2,128]{0,2,1:T(8,128)(2,1)S(1)} %bitcast.368, bf16[3072,2,128]{0,2,1:T(8,128)(2,1)S(1)} %bitcast.350), kind=kOutput, calls=%fused_computation.4 | convolution fusion | flops 1629485056 | bytes 52445184 | tf_op jit(solution)/shard_map/qhd,khd->hqk/dot_general | solution.py:69
  898.5 21.6 %multiply_convert_fusion = bf16[2,1024,3072]{2,1,0:T(8,128)(2,1)} fusion(f32[2,1024,3072]{2,1,0:T(8,128)} %get-tuple-element.123, f32[2,1024,3072]{2,1,0:T(8,128)} %get-tuple-element.121, f32[2,1024]{1,0:T(2,128)S(1)} %get-tuple-element.122, f32[2,1024]{1,0:T(2,128)S(1)} %log_add_fusion.1), kind=kLoop, calls=%fused_computation.3 | loop fusion | flops 25165824 | bytes 62930944 | tf_op jit(solution)/shard_map/convert_element_type | solution.py:70
  920.1 8.9 fusion.153
  929.0 6.4 fusion.55
  945.7 6.9 fusion.52
  964.9 5.4 fusion.218
  970.3 4.5 copy-done.23
  977.1 5.2 convolution_bitcast_fusion
  982.3 4.5 copy-done.24
  989.1 7.0 fusion.108
  996.5 6.3 convert_bitcast_fusion.1
  1005.7 5.6 fusion.21
  1015.6 70.8 %all-reduce.6.cloned.1.call-done = (bf16[3,1024,256]{1,2,0:T(8,128)(2,1)}, bf16[1024,256]{1,0:T(8,128)(2,1)}, bf16[1024,256]{1,0:T(8,128)(2,1)}, bf16[1024,256]{...) async-done(((bf16[3,1024,256]{1,2,0:T(8,128)(2,1)}, bf16[1024,256]{1,0:T(8,128)(2,1)}, ...) | async-done | bytes 7864336 | tf_op jit(solution)/shard_map/psum | solution.py:359
  1095.0 4.4 convert_element_type.499
  1101.9 30.9 %reduce-scatter.19.cloned.1.call-done = bf16[2,128,1024]{2,1,0:T(8,128)(2,1)} async-done(((bf16[2,512,1024]{2,1,0:T(8,128)(2,1)}), bf16[2,128,1024]{2,1,0:T(8,128)(2,1)}) %reduce-scatter.19.cloned.1.call-update) | async-done | bytes 524304 | tf_op jit(solution)/shard_map/reduce_scatter | solution.py:291
  1134.4 43.7 %reduce-scatter.23.cloned.1.call-done = bf16[1,256,1024]{2,1,0:T(8,128)(2,1)} async-done(((bf16[1,1024,1024]{2,1,0:T(8,128)(2,1)}), bf16[1,256,1024]{2,1,0:T(8,128)(2,1)}) %reduce-scatter.23.cloned.1.call-update) | async-done | bytes 524304 | tf_op jit(solution)/shard_map/reduce_scatter | solution.py:291
  1179.8 42.8 %all-reduce = (f32[1024]{0:T(1024)}, f32[1024]{0:T(1024)}, f32[]{:T(128)}) all-reduce(f32[1024]{0:T(1024)S(1)} %add_add_fusion, f32[1024]{0:T(1024)S(1)} %add.308, f32[]{:T(128)S(6)} %add.310), channel_id=1, replica_groups=mesh['dp'=8,'tensor'=4] {'dp','tensor'}, use_global_device_ids=true, to_apply=%region_73.74 | all-reduce | flops 2049 | bytes 16392 | tf_op jit(solution)/shard_map/psum | solution.py:361
  1228.6 41.6 %reduce-scatter.15.cloned.1.call-done = bf16[1,256,1024]{2,1,0:T(8,128)(2,1)} async-done(((bf16[1,1024,1024]{2,1,0:T(8,128)(2,1)}), bf16[1,256,1024]{2,1,0:T(8,128)(2,1)}) %reduce-scatter.15.cloned.1.call-update) | async-done | bytes 524304 | tf_op jit(solution)/shard_map/reduce_scatter | solution.py:180
  (545 shorter events, 292.9 us)
Async XLA Ops:
  7.2 554.9 %copy-start = (bf16[1024,1024]{1,0:T(8,128)(2,1)S(1)}, bf16[1024,1024]{1,0:T(8,128)(2,1)}, u32[]{:S(2)}) copy-start(bf16[1024,1024]{1,0:T(8,128)(2,1)} %param.31) | copy-start | bytes 6291460
  7.2 50.5 %all-gather.24.cloned.1.call-start = ((), (), s32[]{:S(2)}) async-start(), calls=%async_computation.15 | async-start | bytes 2621440 | tf_op jit(solution)/shard_map/all_gather | solution.py:103
  8.0 96.0 %all-gather.22.cloned.1.call-start = ((), (), s32[]{:S(2)}) async-start(), calls=%async_computation.14 | async-start | bytes 2621440 | tf_op jit(solution)/shard_map/all_gather | solution.py:104
  8.7 141.4 %all-gather.16.cloned.1.call-start = ((), (), s32[]{:S(2)}) async-start(), calls=%async_computation.9 | async-start | bytes 2621440 | tf_op jit(solution)/shard_map/all_gather | solution.py:103
  9.5 186.8 %all-gather.14.cloned.1.call-start = ((), (), s32[]{:S(2)}) async-start(), calls=%async_computation.8 | async-start | bytes 2621440 | tf_op jit(solution)/shard_map/all_gather | solution.py:104
  10.0 232.9 %all-gather.18.cloned.1.call-start = ((), (), s32[]{:S(2)}) async-start(), calls=%async_computation.10 | async-start | bytes 2621440 | tf_op jit(solution)/shard_map/all_gather | solution.py:102
  13.8 275.3 %all-gather.26.cloned.1.call-start = ((), (), s32[]{:S(2)}) async-start(), calls=%async_computation.16 | async-start | bytes 2621440 | tf_op jit(solution)/shard_map/all_gather | solution.py:102
  15.4 347.1 %reduce-scatter.9.cloned.1.call-start = ((), (), s32[]{:S(2)}) async-start(), calls=%async_computation.11 | async-start | bytes 2621440 | tf_op jit(solution)/shard_map/reduce_scatter | solution.py:159
  106.8 140.9 %copy-start.93 = (f32[2048]{0:T(1024)}, f32[2048]{0:T(1024)S(1)}, u32[]{:S(2)}) copy-start(f32[2048]{0:T(1024)S(1)} %broadcast_multiply_fusion) | copy-start | bytes 24580
  199.8 46.5 %copy-start.95 = (f32[2,1024]{1,0:T(2,128)}, f32[2,1024]{1,0:T(2,128)S(1)}, u32[]{:S(2)}) copy-start(f32[2,1024]{1,0:T(2,128)S(1)} %broadcast_multiply_fusion.1) | copy-start | bytes 24580
  203.7 44.0 %copy-start.103 = (f32[2048]{0:T(1024)}, f32[2048]{0:T(1024)S(1)}, u32[]{:S(2)}) copy-start(f32[2048]{0:T(1024)S(1)} %add_rsqrt_fusion) | copy-start | bytes 24580
  203.8 44.0 %copy-start.101 = (f32[2,1024]{1,0:T(2,128)}, f32[2,1024]{1,0:T(2,128)S(1)}, u32[]{:S(2)}) copy-start(f32[2,1024]{1,0:T(2,128)S(1)} %add_rsqrt_fusion.1) | copy-start | bytes 24580
  320.0 88.8 %reduce-scatter.13.cloned.1.call-start = ((), (), s32[]{:S(2)}) async-start(), calls=%async_computation.17 | async-start | bytes 2621440 | tf_op jit(solution)/shard_map/reduce_scatter | solution.py:159
  361.0 201.0 %all-gather.20.cloned.1.call-start = ((), (), s32[]{:S(2)}) async-start(), calls=%async_computation.12 | async-start | bytes 2621440 | tf_op jit(solution)/shard_map/all_gather | solution.py:172
  363.8 367.8 %copy-start.107 = (f32[2,128]{1,0:T(2,128)}, f32[2,128]{1,0:T(2,128)S(1)}, u32[]{:S(2)}) copy-start(f32[2,128]{1,0:T(2,128)S(1)} %broadcast_multiply_fusion.18) | copy-start | bytes 3076
  365.2 43.6 %copy-start.109 = (f32[2,128]{1,0:T(2,128)}, f32[2,128]{1,0:T(2,128)S(1)}, u32[]{:S(2)}) copy-start(f32[2,128]{1,0:T(2,128)S(1)} %add_rsqrt_fusion.6) | copy-start | bytes 3076
  367.3 200.7 %all-gather.30.cloned.1.call-start = ((), (), s32[]{:S(2)}) async-start(), calls=%async_computation.20 | async-start | bytes 2621440 | tf_op jit(solution)/shard_map/all_gather | solution.py:192
  367.9 213.7 %all-gather.28.cloned.1.call-start = ((), (), s32[]{:S(2)}) async-start(), calls=%async_computation.18 | async-start | bytes 2621440 | tf_op jit(solution)/shard_map/all_gather | solution.py:172
  413.5 204.1 %all-gather.34.cloned.1.call-start = ((), (), s32[]{:S(2)}) async-start(), calls=%async_computation.24 | async-start | bytes 2621440 | tf_op jit(solution)/shard_map/all_gather | solution.py:192
  414.1 269.4 %all-reduce.8.cloned.1.call-start = ((), (), s32[]{:S(2)}) async-start(), calls=%async_computation.29 | async-start | bytes 2850816 | tf_op jit(solution)/shard_map/psum | solution.py:281
  419.6 31.3 %copy-start.80 = (bf16[1024,256]{0,1:T(8,128)(2,1)S(1)}, bf16[1024,256]{0,1:T(8,128)(2,1)}, u32[]{:S(2)}) copy-start(bf16[1024,256]{0,1:T(8,128)(2,1)} %copy.99) | copy-start | bytes 1572868
  419.6 31.3 %copy-start.84 = (bf16[1024,256]{0,1:T(8,128)(2,1)S(1)}, bf16[1024,256]{0,1:T(8,128)(2,1)}, u32[]{:S(2)}) copy-start(bf16[1024,256]{0,1:T(8,128)(2,1)} %copy.100) | copy-start | bytes 1572868
  561.7 167.6 %reduce-scatter.17.cloned.1.call-start = ((), (), s32[]{:S(2)}) async-start(), calls=%async_computation.21 | async-start | bytes 2621440 | tf_op jit(solution)/shard_map/reduce_scatter | solution.py:203
  581.0 193.8 %reduce-scatter.21.cloned.1.call-start = ((), (), s32[]{:S(2)}) async-start(), calls=%async_computation.25 | async-start | bytes 2621440 | tf_op jit(solution)/shard_map/reduce_scatter | solution.py:203
  630.7 52.8 %copy-start.27 = (bf16[2,170,1024]{2,1,0:T(8,128)(2,1)S(1)}, bf16[2,170,1024]{2,1,0:T(8,128)(2,1)}, u32[]{:S(2)}) copy-start(bf16[2,170,1024]{2,1,0:T(8,128)(2,1)} %copy-done.26) | copy-start | bytes 2088964
  630.7 52.8 %copy-start.119 = (f32[2,170]{1,0:T(2,128)S(1)}, f32[2,170]{1,0:T(2,128)}, u32[]{:S(2)}) copy-start(f32[2,170]{1,0:T(2,128)} %copy-done.118) | copy-start | bytes 4084
  630.7 191.4 %all-gather.32.cloned.1.call-start = ((), (), s32[]{:S(2)}) async-start(), calls=%async_computation.22 | async-start | bytes 2621440 | tf_op jit(solution)/shard_map/all_gather | solution.py:219
  734.0 134.9 %all-gather.36.cloned.1.call-start = ((), (), s32[]{:S(2)}) async-start(), calls=%async_computation.26 | async-start | bytes 2621440 | tf_op jit(solution)/shard_map/all_gather | solution.py:219
  744.7 30.1 %copy-start.113 = (f32[256]{0:T(256)S(1)}, f32[256]{0:T(256)}, u32[]{:S(2)}) copy-start(f32[256]{0:T(256)} %copy-done.112) | copy-start | bytes 3076
  744.7 31.8 %copy-start.45 = (bf16[1,256,1024]{2,1,0:T(8,128)(2,1)S(1)}, bf16[1,256,1024]{2,1,0:T(8,128)(2,1)}, u32[]{:S(2)}) copy-start(bf16[1,256,1024]{2,1,0:T(8,128)(2,1)} %param.37) | copy-start | bytes 1572868
  749.1 73.1 %copy-start.60 = (bf16[256,1024]{1,0:T(8,128)(2,1)S(1)}, bf16[256,1024]{1,0:T(8,128)(2,1)}, u32[]{:S(2)}) copy-start(bf16[256,1024]{1,0:T(8,128)(2,1)} %param.30) | copy-start | bytes 1572868
  778.9 45.7 %copy-start.52 = (bf16[1,1536,256]{1,2,0:T(8,128)(2,1)S(1)}, bf16[1,1536,256]{1,2,0:T(8,128)(2,1)}, u32[]{:S(2)}) copy-start(bf16[1,1536,256]{1,2,0:T(8,128)(2,1)} %get-tuple-element.89) | copy-start | bytes 2359300
  778.9 307.5 %all-reduce.6.cloned.1.call-start = ((), (), s32[]{:S(2)}) async-start(), calls=%async_computation.28 | async-start | bytes 15728640 | tf_op jit(solution)/shard_map/psum | solution.py:359
  964.8 168.0 %reduce-scatter.19.cloned.1.call-start = ((), (), s32[]{:S(2)}) async-start(), calls=%async_computation.23 | async-start | bytes 2621440 | tf_op jit(solution)/shard_map/reduce_scatter | solution.py:291
  977.0 201.1 %reduce-scatter.23.cloned.1.call-start = ((), (), s32[]{:S(2)}) async-start(), calls=%async_computation.27 | async-start | bytes 2621440 | tf_op jit(solution)/shard_map/reduce_scatter | solution.py:291
  989.0 235.8 %reduce-scatter.11.cloned.1.call-start = ((), (), s32[]{:S(2)}) async-start(), calls=%async_computation.13 | async-start | bytes 2621440 | tf_op jit(solution)/shard_map/reduce_scatter | solution.py:180
  996.1 274.1 %reduce-scatter.15.cloned.1.call-start = ((), (), s32[]{:S(2)}) async-start(), calls=%async_computation.19 | async-start | bytes 2621440 | tf_op jit(solution)/shard_map/reduce_scatter | solution.py:180
  1099.4 33.5 %copy-start.6 = (bf16[2,128,1024]{2,1,0:T(8,128)(2,1)S(1)}, bf16[2,128,1024]{2,1,0:T(8,128)(2,1)}, u32[]{:S(2)}) copy-start(bf16[2,128,1024]{2,1,0:T(8,128)(2,1)} %param.19) | copy-start | bytes 1572868
  1099.4 33.5 %copy-start.88 = (f32[1024]{0:T(1024)S(1)}, f32[1024]{0:T(1024)}, u32[]{:S(2)}) copy-start(f32[1024]{0:T(1024)} %param.34) | copy-start | bytes 12292
  1099.4 33.5 %copy-start.117 = (f32[2,128]{1,0:T(2,128)S(1)}, f32[2,128]{1,0:T(2,128)}, u32[]{:S(2)}) copy-start(f32[2,128]{1,0:T(2,128)} %copy-done.116) | copy-start | bytes 3076
  1099.4 33.5 %copy-start.132 = (f32[2,128]{1,0:T(2,128)S(1)}, f32[2,128]{1,0:T(2,128)}, u32[]{:S(2)}) copy-start(f32[2,128]{1,0:T(2,128)} %copy-done.131) | copy-start | bytes 3076
  1099.4 78.8 %copy-start.115 = (f32[256]{0:T(256)S(1)}, f32[256]{0:T(256)}, u32[]{:S(2)}) copy-start(f32[256]{0:T(256)} %copy-done.114) | copy-start | bytes 3076
  1099.4 78.8 %copy-start.130 = (f32[256]{0:T(256)S(1)}, f32[256]{0:T(256)}, u32[]{:S(2)}) copy-start(f32[256]{0:T(256)} %copy-done.129) | copy-start | bytes 3076
  1099.4 125.4 %copy-start.108 = (f32[2,128]{1,0:T(2,128)S(1)}, f32[2,128]{1,0:T(2,128)}, u32[]{:S(2)}) copy-start(f32[2,128]{1,0:T(2,128)} %copy-done.107) | copy-start | bytes 3076
  1099.4 125.4 %copy-start.111 = (f32[2,128]{1,0:T(2,128)S(1)}, f32[2,128]{1,0:T(2,128)}, u32[]{:S(2)}) copy-start(f32[2,128]{1,0:T(2,128)} %copy-done.109) | copy-start | bytes 3076
  1099.4 125.4 %copy-start.134 = (f32[2,128]{1,0:T(2,128)S(1)}, f32[2,128]{1,0:T(2,128)}, u32[]{:S(2)}) copy-start(f32[2,128]{1,0:T(2,128)} %copy-done.133) | copy-start | bytes 3076
  1099.4 125.4 %copy-start.136 = (f32[2,128]{1,0:T(2,128)S(1)}, f32[2,128]{1,0:T(2,128)}, u32[]{:S(2)}) copy-start(f32[2,128]{1,0:T(2,128)} %copy-done.135) | copy-start | bytes 3076
  1224.8 49.1 %copy-start.1 = (bf16[1024,1024]{1,0:T(8,128)(2,1)S(1)}, bf16[1024,1024]{1,0:T(8,128)(2,1)}, u32[]{:S(2)}) copy-start(bf16[1024,1024]{1,0:T(8,128)(2,1)} %param.31) | copy-start | bytes 6291460
  (128 other events, 777.6 us)
Sparse Core Ops, SparseCore 0:
  9.6 48.0 all-gather.23
  59.3 44.6 all-gather.21
  105.5 44.6 all-gather.15
  151.6 44.6 all-gather.13
  198.3 44.6 all-gather.17
  244.4 44.6 all-gather.25
  320.1 42.3 reduce-scatter.8
  365.5 43.1 reduce-scatter.12
  410.9 56.8 all-gather.19
  469.2 55.9 all-gather.29
  526.8 44.7 all-gather.27
  572.9 44.6 all-gather.33
  620.7 62.7 all-reduce.7
  685.6 43.7 reduce-scatter.16
  731.6 43.1 reduce-scatter.20
  776.8 45.2 all-gather.31
  824.1 44.7 all-gather.35
  964.9 121.4 all-reduce.5
  1088.8 43.9 reduce-scatter.18
  1135.0 43.1 reduce-scatter.22
  1180.6 44.1 reduce-scatter.10
  1227.1 43.1 reduce-scatter.14
where the time goes:
time: 1300 us; the launch traced here: 1280 us
  waiting for transfers between devices  662 us (51%)
  matrix products  282 us (22%)
  other arithmetic  125 us (10%)
  blocking collectives  96.6 us (7%)
  local copies, waits for them, and re-layouts  92.9 us (7%)
  between operations  21.1 us (2%)
    all_gather x2, waiting for transfers between devices, group_layer(): lax.all_gather(older, 'tensor', axis=1, tiled=True)  92.4 us
    reduce_scatter x2, waiting for transfers between devices, group_layer(): lax.psum_scatter(grad_token_rows.astype(jnp.bfloat16), 'tensor', scatter_...  74.7 us
    all_gather x2, waiting for transfers between devices, group_layer(): lax.all_gather(memory, 'tensor', axis=1, tiled=True)  72.7 us
    psum x1, waiting for transfers between devices, per_device(): lax.psum(for_sending(summed), 'dp')  70.8 us
    all_gather x2, waiting for transfers between devices, group_layer(): lax.all_gather(normed_tokens, 'tensor', axis=1, tiled=True)  68.3 us
    all_gather x2, waiting for transfers between devices, group_layer(): lax.all_gather(grad_hidden_low, 'tensor', axis=1, tiled=True)  66.8 us
    all_gather x2, blocking collectives, group_layer(): lax.all_gather(appended_local, 'tensor', axis=2, tiled=True)  53.8 us
    reduce_scatter x2, waiting for transfers between devices, group_layer(): lax.psum_scatter(jnp.einsum('zar,vr->zav', grad_preactivation, up_project...  49 us
  transfers between devices with their start and end apart: 22, of which 19 were waited for; matrix products, arithmetic and copies ran while one was open for 27% of the time, Pallas kernels for 0%

commit v1 on v0

--- a/solution.py
+++ b/solution.py
@@ -10,13 +10,97 @@
 rebuild_weight = 256.0
 masked_value = -1e30
 
-
-def for_sending(value):
-
-    def short(part):
-        return part.astype(jnp.bfloat16) if part.dtype == jnp.float32 else part
-
-    return jax.tree.map(short, value)
+AXES = ("dp", "tensor")
+
+
+class Layout:
+    def __init__(self):
+        self.dp, self.tensor = lax.axis_size("dp"), lax.axis_size("tensor")
+        self.half = self.tensor // 2
+        self.columns = self.dp // 2
+        place, plane = lax.axis_index("dp"), lax.axis_index("tensor")
+        self.core, self.column = place % 2, place // 2
+        self.upper, self.lower = plane // self.half, plane % self.half
+        self.bits = [bit for bit in range(self.half.bit_length() - 1)]
+        self.shard = self.core * self.half + self.lower
+        self.groups = [[2 * c + core for c in range(self.columns)] for core in range(2)]
+
+    def permute(self, value, move):
+        pairs = []
+        for d in range(self.dp):
+            for t in range(self.tensor):
+                column, core, upper, lower = move(d // 2, d % 2, t // self.half, t % self.half)
+                pairs.append((d * self.tensor + t, (2 * column + core) * self.tensor + upper * self.half + lower))
+        return jax.tree.map(lambda part: lax.ppermute(part, AXES, pairs), value)
+
+    def swap(self, value):
+        return self.permute(value, lambda p, c, h, a: (p, h, c, a))
+
+    def flip_core(self, value):
+        return self.permute(value, lambda p, c, h, a: (p, 1 - c, h, a))
+
+    def flip_lower(self, value, bit):
+        return self.permute(value, lambda p, c, h, a: (p, c, h, a ^ (1 << bit)))
+
+    def gather(self, value, axis):
+        def join(own, other, second):
+            return jnp.where(
+                second, jnp.concatenate([other, own], axis), jnp.concatenate([own, other], axis)
+            )
+
+        for bit in self.bits:
+            value = join(value, self.flip_lower(value, bit), (self.lower >> bit) % 2 == 1)
+        return join(value, self.flip_core(value), self.core == 1)
+
+    def scatter(self, value, axis):
+        def part(value, index):
+            extent = value.shape[axis] // 2
+            return lax.dynamic_slice_in_dim(value, index * extent, extent, axis)
+
+        def step(value, index, exchange):
+            other = exchange(part(value, 1 - index).astype(jnp.bfloat16))
+            return part(value, index).astype(jnp.float32) + other.astype(jnp.float32)
+
+        value = step(value, self.core, self.flip_core)
+        for bit in reversed(self.bits):
+            value = step(value, (self.lower >> bit) % 2, lambda v, bit=bit: self.flip_lower(v, bit))
+        return value
+
+    def total(self, value):
+        for exchange in [self.flip_core] + [
+            lambda v, bit=bit: self.flip_lower(v, bit) for bit in self.bits
+        ]:
+            value = value.astype(jnp.bfloat16)
+            value = value.astype(jnp.float32) + exchange(value).astype(jnp.float32)
+        return value
+
+    def weight(self, value):
+        rows = value.shape[0] // self.columns
+        mine = lax.dynamic_slice_in_dim(value, self.column * rows, rows, 0)
+        return lax.all_gather(
+            self.swap(mine), "dp", axis=0, tiled=True, axis_index_groups=self.groups
+        )
+
+    def grad(self, value):
+        part = lax.psum_scatter(
+            value.astype(jnp.bfloat16),
+            "dp",
+            scatter_dimension=0,
+            tiled=True,
+            axis_index_groups=self.groups,
+        )
+        rows = part.shape[0] // 2
+
+        def eighth(index):
+            return lax.dynamic_slice_in_dim(part, index * rows, rows, 0)
+
+        other = self.permute(
+            eighth(1 - self.upper),
+            lambda p, c, h, a: (p, c, c, a) if c != h else (p, 1 - c, h, a),
+        )
+        own = self.permute(eighth(self.upper), lambda p, c, h, a: (p, h, c, a))
+        summed = (own.astype(jnp.float32) + other.astype(jnp.float32)).astype(jnp.bfloat16)
+        return lax.all_gather(summed, "dp", axis=0, tiled=True).astype(jnp.float32)
 
 
 def normalize(rows):
@@ -80,11 +164,13 @@
     return (grad_query, grad_key, grad_value)
 
 
-def group_layer(inputs, memory, older, offsets, cotangent, weights):
+def group_layer(layout, inputs, memory, older, offsets, cotangent, weights):
+    inputs, memory, older, offsets, cotangent = layout.swap(
+        (inputs, memory, older, offsets, cotangent)
+    )
     (
         query_projection_weight,
-        key_w,
-        value_w,
+        pairwise_weight,
         output_projection_weight,
         up_projection_weight,
         down_projection_weight,
@@ -99,16 +185,15 @@
     unit_tokens, inverse_tokens = normalize(inputs.astype(jnp.float32))
     normed_tokens = (unit_tokens * attention_gain).astype(jnp.bfloat16)
     entire_tokens, whole_memory, whole_older = (
-        lax.all_gather(normed_tokens, "tensor", axis=1, tiled=True),
-        lax.all_gather(memory, "tensor", axis=1, tiled=True),
-        lax.all_gather(older, "tensor", axis=1, tiled=True),
+        layout.gather(normed_tokens, 1),
+        layout.gather(memory, 1),
+        layout.gather(older, 1),
     )
     length = entire_tokens.shape[1]
     reduced = length // 3
     unit_memory = normalize(jnp.concatenate([whole_older, whole_memory], 1).astype(jnp.float32))[0]
     memory_rows = (unit_memory * attention_gain).astype(jnp.bfloat16)
     incoming_keys = jnp.concatenate([memory_rows, entire_tokens], 1)
-    pairwise_weight = jnp.concatenate([key_w, value_w], 1)
     queries = jnp.einsum(
         "qfc,cp->qfp", entire_tokens, query_projection_weight, preferred_element_type=jnp.float32
     ).astype(jnp.bfloat16)
@@ -119,10 +204,10 @@
     appended_local = jnp.einsum(
         "srk,ke->sre",
         stacked,
-        squeeze_w.reshape(3 * width, local_width),
+        squeeze_w,
         preferred_element_type=jnp.float32,
     ).astype(jnp.bfloat16)
-    appended_whole = lax.all_gather(appended_local, "tensor", axis=2, tiled=True)
+    appended_whole = layout.gather(appended_local, 2)
     unit_added, inverse_added = normalize(appended_whole.astype(jnp.float32))
     added_rows = (unit_added * attention_gain).astype(jnp.bfloat16)
     added_pairs = jnp.einsum(
@@ -156,40 +241,34 @@
             (validity, query, key, value, added_key, added_value, log_main, log_added, differ)
         )
     attention_complete = jnp.stack(attended)
-    branch = lax.psum_scatter(
+    branch = layout.scatter(
         jnp.einsum(
             "owa,au->owu",
             attention_complete,
             output_projection_weight,
             preferred_element_type=jnp.float32,
         ).astype(jnp.bfloat16),
-        "tensor",
-        scatter_dimension=1,
-        tiled=True,
-    ).astype(jnp.float32)
+        1,
+    )
     hidden_state = inputs.astype(jnp.float32) + branch
     unit_hidden, inverse_hidden = normalize(hidden_state)
-    feedforward_entire = lax.all_gather(
-        (unit_hidden * feedforward_gain).astype(jnp.bfloat16), "tensor", axis=1, tiled=True
-    )
+    feedforward_entire = layout.gather((unit_hidden * feedforward_gain).astype(jnp.bfloat16), 1)
     preactivation = jnp.einsum(
         "urc,ch->urh", feedforward_entire, up_projection_weight, preferred_element_type=jnp.float32
     )
     activated, gelu_back = jax.vjp(jax.nn.gelu, preactivation)
     activated_reduced = activated.astype(jnp.bfloat16)
-    feedforward = lax.psum_scatter(
+    feedforward = layout.scatter(
         jnp.einsum(
             "qer,rz->qez",
             activated_reduced,
             down_projection_weight,
             preferred_element_type=jnp.float32,
         ).astype(jnp.bfloat16),
-        "tensor",
-        scatter_dimension=1,
-        tiled=True,
-    ).astype(jnp.float32)
+        1,
+    )
     output = (hidden_state + feedforward).astype(jnp.bfloat16)
-    cotangent_entire = lax.all_gather(cotangent, "tensor", axis=1, tiled=True)
+    cotangent_entire = layout.gather(cotangent, 1)
     grad_down_w = jnp.einsum(
         "jkg,jki->gi", activated_reduced, cotangent_entire, preferred_element_type=jnp.float32
     )
@@ -200,23 +279,21 @@
     grad_up_projection_weight = jnp.einsum(
         "aji,ajr->ir", feedforward_entire, grad_preactivation, preferred_element_type=jnp.float32
     )
-    grad_ff = lax.psum_scatter(
+    grad_ff = layout.scatter(
         jnp.einsum(
             "zar,vr->zav",
             grad_preactivation,
             up_projection_weight,
             preferred_element_type=jnp.float32,
         ).astype(jnp.bfloat16),
-        "tensor",
-        scatter_dimension=1,
-        tiled=True,
-    ).astype(jnp.float32)
+        1,
+    )
     feed_gain_part = jnp.sum(grad_ff * unit_hidden, (0, 1))
     grad_hidden = cotangent.astype(jnp.float32) + norm_back(
         grad_ff, feedforward_gain, unit_hidden, inverse_hidden
     )
     grad_hidden_low = grad_hidden.astype(jnp.bfloat16)
-    branch_entire = lax.all_gather(grad_hidden_low, "tensor", axis=1, tiled=True)
+    branch_entire = layout.gather(grad_hidden_low, 1)
     grad_out_w = jnp.einsum(
         "qnw,qny->wy", attention_complete, branch_entire, preferred_element_type=jnp.float32
     )
@@ -278,35 +355,35 @@
     grad_added_norm = jnp.einsum(
         "sre,de->srd", grad_added_all, pairwise_weight, preferred_element_type=jnp.float32
     )
-    added_full = lax.psum(grad_added_norm.astype(jnp.bfloat16), "tensor").astype(jnp.float32)
+    added_full = layout.total(grad_added_norm)
     grad_appended = norm_back(added_full, attention_gain, unit_added, inverse_added).astype(
         jnp.bfloat16
     )
     grad_appended_local = lax.dynamic_slice_in_dim(
-        grad_appended, lax.axis_index("tensor") * local_width, local_width, 2
+        grad_appended, layout.shard * local_width, local_width, 2
     )
     grad_squeeze_w = jnp.einsum(
         "srk,sre->ke", stacked, grad_appended_local, preferred_element_type=jnp.float32
-    ).reshape(3, width, local_width)
-    grad_token_norm = lax.psum_scatter(
-        grad_token_rows.astype(jnp.bfloat16), "tensor", scatter_dimension=1, tiled=True
-    ).astype(jnp.float32)
+    )
+    grad_token_norm = layout.scatter(grad_token_rows.astype(jnp.bfloat16), 1)
     attention_gain_part = attention_gain_part + jnp.sum(grad_token_norm * unit_tokens, (0, 1))
     grad_inputs = grad_hidden + norm_back(
         grad_token_norm, attention_gain, unit_tokens, inverse_tokens
     )
     grads = (
         grad_query_w,
-        grad_pair_w[:, :local_width],
-        grad_pair_w[:, local_width:],
+        grad_pair_w,
         grad_out_w,
         grad_up_projection_weight,
         grad_down_w,
         grad_squeeze_w,
     )
+    output, grad_inputs, appended_local = layout.swap(
+        (output, grad_inputs.astype(jnp.bfloat16), appended_local)
+    )
     return (
         output,
-        grad_inputs,
+        grad_inputs.astype(jnp.float32),
         appended_local,
         grads,
         attention_gain_part,
@@ -337,26 +414,35 @@
     cotangent_short,
     cotangent_long,
 ):
+    layout = Layout()
+    width, local_width = query_weight.shape
+    qkv_weight = layout.weight(jnp.concatenate([query_weight, key_weight, value_weight], 1))
     weights = (
-        query_weight,
-        key_weight,
-        value_weight,
-        out_weight,
-        up_weight,
-        down_weight,
-        compress_weight,
+        qkv_weight[:, :local_width],
+        qkv_weight[:, local_width:],
+        layout.weight(out_weight),
+        layout.weight(up_weight),
+        layout.weight(down_weight),
+        layout.weight(compress_weight.reshape(3 * width, local_width)),
         attention_gain,
         feedforward_gain,
     )
     short_result = group_layer(
-        inputs_short, memory_short, compressed_short, offsets_short, cotangent_short, weights
+        layout, inputs_short, memory_short, compressed_short, offsets_short, cotangent_short, weights
     )
     long_result = group_layer(
-        inputs_long, memory_long, compressed_long, offsets_long, cotangent_long, weights
+        layout, inputs_long, memory_long, compressed_long, offsets_long, cotangent_long, weights
     )
     summed = jax.tree.map(jnp.add, short_result[3], long_result[3])
-    summed = jax.tree.map(
-        lambda part: part.astype(jnp.float32), lax.psum(for_sending(summed), "dp")
+    query_sum, pair_sum, out_sum, up_sum, down_sum, squeeze_sum = map(layout.grad, summed)
+    summed = (
+        query_sum,
+        pair_sum[:, :local_width],
+        pair_sum[:, local_width:],
+        out_sum,
+        up_sum,
+        down_sum,
+        squeeze_sum.reshape(3, width, local_width),
     )
     gain_one, gain_two, square_total = lax.psum(
         (

time: 1300 us -> 1000 us (0.77)
  waiting for transfers between devices: 662 us -> 270 us
  starting transfers between devices: 2.25 us -> 115 us
  other arithmetic: 125 us -> 171 us
  blocking collectives: 96.6 us -> 69.1 us
  local copies, waits for them, and re-layouts: 92.9 us -> 75.5 us
  matrix products: 282 us -> 269 us
    all_gather x12 -> x8, waiting for transfers between devices: 330 us -> 7.51 us  [the longest x4 7.49 us: grad(): return lax.all_gather(summed, 'dp', axis=0, tiled=True).astype(jnp.float32)]
    ppermute x0 -> x81, waiting for transfers between devices: none -> 262 us  [permute(): return jax.tree.map(lambda part: lax.ppermute(part, AXES, pairs), value)]
    reduce_scatter x8 -> x6, waiting for transfers between devices: 209 us -> 0.12 us  [grad(): lax.psum_scatter(value.astype(jnp.bfloat16), 'dp', scatter_dimension=0, t...]
    psum x2 -> x0, waiting for transfers between devices: 119 us -> none  [the longest x1 70.8 us: per_device(): lax.psum(for_sending(summed), 'dp')]
    ppermute x0 -> x81, starting transfers between devices: none -> 113 us  [permute(): return jax.tree.map(lambda part: lax.ppermute(part, AXES, pairs), value)]
    select_n x0 -> x26, other arithmetic: none -> 47.8 us  [join(): jnp.where(second, jnp.concatenate([other, own], axis), jnp.concatenate([o...]
    all_gather x2 -> x3, blocking collectives: 53.8 us -> 30.6 us  [the longest x2 20.5 us: grad(): return lax.all_gather(summed, 'dp', axis=0, tiled=True).astype(jnp.float32)]
    dynamic_slice x0 -> x18, local copies, waits for them, and re-layouts: none -> 15.3 us  [the longest x6 6.89 us: eighth(): return lax.dynamic_slice_in_dim(part, index * rows, rows, 0)]
  transfers between devices with their start and end apart: 22 -> 95, of which waited for: 19 -> 28; matrix products, arithmetic and copies ran while one was open for 27% -> 48% of each run, Pallas kernels for 0% -> 0%
where the time goes in v1:
time: 1000 us; the launch traced here: 991 us
  waiting for transfers between devices  270 us (27%)
  matrix products  269 us (27%)
  other arithmetic  171 us (17%)
  starting transfers between devices  115 us (12%)
  local copies, waits for them, and re-layouts  75.5 us (8%)
  blocking collectives  69.1 us (7%)
  between operations  21.3 us (2%)
    ppermute x81, waiting for transfers between devices, permute(): return jax.tree.map(lambda part: lax.ppermute(part, AXES, pairs), value)  262 us
    ppermute x81, starting transfers between devices, permute(): return jax.tree.map(lambda part: lax.ppermute(part, AXES, pairs), value)  113 us
    select_n x26, other arithmetic, join(): jnp.where(second, jnp.concatenate([other, own], axis), jnp.concatenate([o...  47.8 us
    psum x1, blocking collectives, per_device(): lax.psum((short_result[4] + long_result[4], short_result[5] + long_result...  38.5 us
    unnamed x305, local copies, waits for them, and re-layouts  31.3 us
    dot_general x9, matrix products, attend(): jnp.einsum('hqk,khd->qhd', probs.astype(jnp.bfloat16), value, preferred_e...  30.9 us
    dot_general x6, matrix products, attend_back(): jnp.einsum('qhd,khd->hqk', grad_result, value, preferred_element_type=jnp...  24.7 us
    convert_element_type x3, other arithmetic, attend_back(): (probs * (grad_probs - jnp.sum(grad_probs * probs, -1, keepdims=True))).a...  24.5 us
  transfers between devices with their start and end apart: 95, of which 28 were waited for; matrix products, arithmetic and copies ran while one was open for 48% of the time, Pallas kernels for 0%

profile of v1, /device:TPU:1, one launch (start us, length us, event | category | flops | bytes accessed | tf_op | source)
XLA Modules:
  0.0 990.6 jit_solution(3842123413774470060)
XLA Ops:
  12.9 5.6 collective-permute-start.9
  18.5 9.7 collective-permute-done.9
  32.0 12.3 %collective-permute-done.58 = bf16[768,256]{1,0:T(8,128)(2,1)S(1)} collective-permute-done((bf16[768,256]{1,0:T(8,128)(2,1)S(1)}, bf16[768,256]{1,0:T(8,128)(2,1)S(1)}, u32[]{:S(2)}, u32[]{:S(2)}) %collective-permute-start.58) | collective-permute-done | bytes 393248 | tf_op jit(solution)/shard_map/ppermute | solution.py:34
  68.4 21.1 %collective-permute-done.16 = bf16[256,1024]{1,0:T(8,128)(2,1)S(1)} collective-permute-done((bf16[256,1024]{1,0:T(8,128)(2,1)S(1)}, bf16[256,1024]{1,0:T(8,128)(2,1)S(1)}, u32[]{:S(2)}, u32[]{:S(2)}) %collective-permute-start.16) | collective-permute-done | bytes 524320 | tf_op jit(solution)/shard_map/ppermute | solution.py:34
  106.1 10.2 %all_gather.34 = bf16[256,1024]{1,0:T(8,128)(2,1)S(1)} all-gather(bf16[64,1024]{1,0:T(8,128)(2,1)S(1)} %collective-permute-done.11), channel_id=1, replica_groups={{0,8,16,24},{4,12,20,28},{1,9,17,25},{5,13,21,29},{2,10,18,26},{6,14,22..., dimensions={0}, use_global_device_ids=true | all-gather | bytes 655360 | tf_op jit(solution)/shard_map/all_gather | solution.py:80
  132.6 8.7 collective-permute-done.48
  143.7 8.8 collective-permute-done.25
  152.5 10.1 %collective-permute-done.22 = bf16[1,256,1024]{2,1,0:T(8,128)(2,1)S(1)} collective-permute-done((bf16[1,256,1024]{2,1,0:T(8,128)(2,1)}, bf16[1,256,1024]{2,1,0:T(8,128)(2,1)S(1)}, u32[]{:S(2)}, u32[]{:S(2)}) %collective-permute-start.22) | collective-permute-done | bytes 524320 | tf_op jit(solution)/shard_map/ppermute | solution.py:34
  168.5 9.4 collective-permute-done.49
  182.0 16.1 %collective-permute-done.23 = bf16[1,256,1024]{2,1,0:T(8,128)(2,1)} collective-permute-done((bf16[1,256,1024]{2,1,0:T(8,128)(2,1)S(1)}, bf16[1,256,1024]{2,1,0:T(8,128)(2,1)}, u32[]{:S(2)}, u32[]{:S(2)}) %collective-permute-start.23) | collective-permute-done | bytes 524320 | tf_op jit(solution)/shard_map/ppermute | solution.py:34
  257.0 6.5 fusion.51
  304.7 7.2 fusion.364
  311.9 12.9 %fusion.359 = (f32[2,1024]{1,0:T(2,128)S(1)}, f32[2,1024,3072]{2,1,0:T(8,128)}) fusion(bf16[1024,2,128]{0,2,1:T(8,128)(2,1)S(1)} %bitcast.311, bf16[3072,2,128]{0,2,1:T(8,128)(2,1)S(1)} %bitcast.337, pred[1024,3072]{1,0:T(8,128)(4,1)} %fusion.8), kind=kOutput, calls=%fused_computation.592 | convolution fusion | flops 1629485056 | bytes 30416896 | tf_op jit(solution)/shard_map/qhd,khd->hqk/dot_general | solution.py:127
  324.7 11.1 %fusion.3 = f32[2,1024]{1,0:T(2,128)S(1)} fusion(f32[2,1024,3072]{2,1,0:T(8,128)} %get-tuple-element.142, f32[2,1024]{1,0:T(2,128)S(1)} %get-tuple-element.141), kind=kLoop, calls=%fused_computation.9 | loop fusion | flops 12580864 | bytes 25182208 | tf_op jit(solution)/shard_map/reduce_sum | solution.py:139
  336.5 11.2 %fusion.120 = bf16[2,128,1024]{2,1,0:T(8,128)(2,1)S(1)} fusion(bf16[3072,2,128]{0,2,1:T(8,128)(2,1)S(1)} %bitcast.332, f32[2,1024,3072]{2,1,0:T(8,128)} %get-tuple-element.142, f32[2,1024]{1,0:T(2,128)S(1)} %fusion.3, f32[2,1024]{1,0:T(2,128)S(1)} %get-tuple-element.141), kind=kOutput, calls=%fused_computation.224 | convolution fusion | flops 1629749248 | bytes 27279360 | tf_op jit(solution)/shard_map/hqk,khd->qhd/dot_general | solution.py:141
  403.2 7.7 collective-permute-done.13
  411.8 10.3 %collective-permute-done.32 = bf16[1,256,1024]{2,1,0:T(8,128)(2,1)S(1)} collective-permute-done((bf16[1,256,1024]{2,1,0:T(8,128)(2,1)S(1)}, bf16[1,256,1024]{2,1,0:T(8,128)(2,1)S(1)}, u32[]{:S(2)}, u32[]{:S(2)}) %collective-permute-start.32) | collective-permute-done | bytes 524320 | tf_op jit(solution)/shard_map/ppermute | solution.py:34
  423.2 13.8 %collective-permute-done.74 = bf16[2,170,1024]{2,0,1:T(2,128)(2,1)S(1)} collective-permute-done((bf16[2,170,1024]{2,0,1:T(2,128)(2,1)S(1)}, bf16[2,170,1024]{2,0,1:T(2,128)(2,1)S(1)}, u32[]{:S(2)}, u32[]{:S(2)}) %collective-permute-start.74) | collective-permute-done | bytes 696352 | tf_op jit(solution)/shard_map/ppermute | solution.py:34
  438.0 25.4 %collective-permute-done.14 = bf16[2,128,1024]{2,1,0:T(8,128)(2,1)S(1)} collective-permute-done((bf16[2,128,1024]{2,1,0:T(8,128)(2,1)S(1)}, bf16[2,128,1024]{2,1,0:T(8,128)(2,1)S(1)}, u32[]{:S(2)}, u32[]{:S(2)}) %collective-permute-start.14) | collective-permute-done | bytes 524320 | tf_op jit(solution)/shard_map/ppermute | solution.py:34
  478.4 7.2 fusion.89
  485.6 5.7 fusion.94
  491.5 6.9 fusion.37
  506.8 8.3 fusion.44
  524.6 21.8 %collective-permute-done.42 = bf16[2,128,1024]{2,1,0:T(8,128)(2,1)S(1)} collective-permute-done((bf16[2,128,1024]{2,1,0:T(8,128)(2,1)S(1)}, bf16[2,128,1024]{2,1,0:T(8,128)(2,1)S(1)}, u32[]{:S(2)}, u32[]{:S(2)}) %collective-permute-start.42) | collective-permute-done | bytes 524320 | tf_op jit(solution)/shard_map/ppermute | solution.py:34
  551.2 6.4 collective-permute-done.52
  558.2 10.7 %collective-permute-done.43 = bf16[2,128,1024]{2,1,0:T(8,128)(2,1)S(1)} collective-permute-done((bf16[2,128,1024]{2,1,0:T(8,128)(2,1)S(1)}, bf16[2,128,1024]{2,1,0:T(8,128)(2,1)S(1)}, u32[]{:S(2)}, u32[]{:S(2)}) %collective-permute-start.43) | collective-permute-done | bytes 524320 | tf_op jit(solution)/shard_map/ppermute | solution.py:34
  571.6 8.5 collective-permute-done.36
  587.4 7.6 collective-permute-done.53
  620.6 15.4 %multiply_reduce_fusion = (f32[2,1024]{1,0:T(2,128)S(1)}, f32[2,1024,3072]{2,1,0:T(8,128)}) fusion(f32[2,1024,3072]{2,1,0:T(8,128)} %get-tuple-element.142, f32[2,1024]{1,0:T(2,128)S(1)} %copy-done.105, bf16[1024,2,128]{0,2,1:T(8,128)(2,1)S(1)} %bitcast.356, bf16[3072,2,128]{0,2,1:T(8,128)(2,1)S(1)} %bitcast.333), kind=kOutput, calls=%fused_computation.4 | convolution fusion | flops 1629485056 | bytes 52445184 | tf_op jit(solution)/shard_map/qhd,khd->hqk/dot_general | solution.py:153
  636.0 17.0 %multiply_convert_fusion = bf16[2,1024,3072]{2,1,0:T(8,128)(2,1)S(1)} fusion(f32[2,1024,3072]{2,1,0:T(8,128)} %get-tuple-element.148, f32[2,1024,3072]{2,1,0:T(8,128)} %get-tuple-element.142, f32[2,1024]{1,0:T(2,128)S(1)} %get-tuple-element.147, f32[2,1024]{1,0:T(2,128)S(1)} %copy-done.105), kind=kLoop, calls=%fused_computation.3 | loop fusion | flops 25165824 | bytes 62930944 | tf_op jit(solution)/shard_map/convert_element_type | solution.py:154
  657.6 6.1 multiply_convert_fusion.1
  675.0 8.2 fusion.53
  683.2 10.8 %fusion.57 = bf16[2,128,3072]{2,1,0:T(8,128)(2,1)S(1)} fusion(bf16[1024,2,128]{0,2,1:T(8,128)(2,1)S(1)} %bitcast.357, f32[2,1024,3072]{2,1,0:T(8,128)} %get-tuple-element.142, f32[2,1024]{1,0:T(2,128)S(1)} %copy-done.105), kind=kOutput, calls=%fused_computation.99 | convolution fusion | flops 1623982080 | bytes 27271168 | tf_op jit(solution)/shard_map/hqk,qhd->khd/dot_general | solution.py:150
  695.1 6.1 fusion.83
  701.5 5.6 fusion.232
  707.1 5.6 fusion.48
  712.8 6.8 fusion.229
  719.7 6.5 fusion.47
  732.9 9.8 fusion.119
  756.9 8.8 collective-permute-done.79
  790.3 20.4 %collective-permute-done.59 = bf16[2,170,256]{2,1,0:T(8,128)(2,1)S(1)} collective-permute-done((bf16[2,170,256]{2,1,0:T(8,128)(2,1)}, bf16[2,170,256]{2,1,0:T(8,128)(2,1)S(1)}, u32[]{:S(2)}, u32[]{:S(2)}) %collective-permute-start.59) | collective-permute-done | bytes 174112 | tf_op jit(solution)/shard_map/ppermute | solution.py:34
  816.9 9.8 fusion.175
  860.8 7.3 collective-permute-done.69
  875.9 5.4 collective-permute-start.61
  884.9 10.3 %all_gather.40 = bf16[256,1024]{1,0:T(8,128)(2,1)S(1)} all-gather(bf16[32,1024]{1,0:T(8,128)(2,1)S(1)} %add_convert_fusion.8), channel_id=1, replica_groups=mesh['dp'=8,'tensor'=4] {'dp'}, dimensions={0}, use_global_device_ids=true | all-gather | bytes 589824 | tf_op jit(solution)/shard_map/all_gather | solution.py:103
  905.1 10.1 %all_gather.38 = bf16[1024,256]{1,0:T(8,128)(2,1)S(1)} all-gather(bf16[128,256]{1,0:T(8,128)(2,1)S(1)} %add_convert_fusion.9), channel_id=1, replica_groups=mesh['dp'=8,'tensor'=4] {'dp'}, dimensions={0}, use_global_device_ids=true | all-gather | bytes 589824 | tf_op jit(solution)/shard_map/all_gather | solution.py:103
  916.3 38.5 %all-reduce = (f32[1024]{0:T(1024)}, f32[1024]{0:T(1024)}, f32[]{:T(128)}) all-reduce(f32[1024]{0:T(1024)S(1)} %add_add_fusion, f32[1024]{0:T(1024)S(1)} %add.526, f32[]{:T(128)S(6)} %add.528), channel_id=1, replica_groups=mesh['dp'=8,'tensor'=4] {'dp','tensor'}, use_global_device_ids=true, to_apply=%region_62.63 | all-reduce | flops 2049 | bytes 16392 | tf_op jit(solution)/shard_map/psum | solution.py:447
  967.7 7.5 all-gather.21.cloned.1.call-done
  (747 shorter events, 452.1 us)
Async XLA Ops:
  7.2 249.8 %all-gather.9.cloned.1.call-start = ((), (), s32[]{:S(2)}) async-start(), calls=%async_computation.6 | async-start | bytes 1966080 | tf_op jit(solution)/shard_map/all_gather | solution.py:80
  28.9 248.0 %all-gather.15.cloned.1.call-start = ((), (), s32[]{:S(2)}) async-start(), calls=%async_computation.9 | async-start | bytes 1966080 | tf_op jit(solution)/shard_map/all_gather | solution.py:80
  45.1 433.3 %all-gather.11.cloned.1.call-start = ((), (), s32[]{:S(2)}) async-start(), calls=%async_computation.7 | async-start | bytes 2621440 | tf_op jit(solution)/shard_map/all_gather | solution.py:80
  45.1 50.5 %collective-permute-start.10 = (s32[2]{0:T(128)S(1)}, s32[2]{0:T(128)S(1)}, u32[]{:S(2)}, u32[]{:S(2)}) collective-permute-start(s32[2]{0:T(128)S(1)} %copy-done.132), channel_id=1, source_target_pairs={{0,0},{1,1},{2,4},{3,5},{4,2},{5,3},{6,6},{7,7},{8,8},{9,9},{10,12... | collective-permute-start | bytes 32 | tf_op jit(solution)/shard_map/ppermute | solution.py:34
  52.6 51.7 %collective-permute-start.11 = (bf16[64,1024]{1,0:T(8,128)(2,1)S(1)}, bf16[64,1024]{1,0:T(8,128)(2,1)S(1)}, u32[]{:S(2)}, u32[]{:S(2)}) collective-permute-start(bf16[64,1024]{1,0:T(8,128)(2,1)S(1)} %constant_dynamic-slice_fusion.20), channel_id=1, source_target_pairs={{0,0},{1,1},{2,4},{3,5},{4,2},{5,3},{6,6},{7,7},{8,8},{9,9},{10,12... | collective-permute-start | bytes 393224 | tf_op jit(solution)/shard_map/ppermute | solution.py:34
  55.3 72.8 %collective-permute-start.17 = (bf16[256,1024]{1,0:T(8,128)(2,1)}, bf16[256,1024]{1,0:T(8,128)(2,1)S(1)}, u32[]{:S(2)}, u32[]{:S(2)}) collective-permute-start(bf16[256,1024]{1,0:T(8,128)(2,1)} %constant_dynamic-slice_fusion.17), channel_id=1, source_target_pairs={{0,0},{1,1},{2,4},{3,5},{4,2},{5,3},{6,6},{7,7},{8,8},{9,9},{10,12... | collective-permute-start | bytes 1572872 | tf_op jit(solution)/shard_map/ppermute | solution.py:34
  63.2 61.6 %collective-permute-start = (bf16[2,128,1024]{2,1,0:T(8,128)(2,1)}, bf16[2,128,1024]{2,1,0:T(8,128)(2,1)S(1)}, u32[]{:S(2)}, u32[]{:S(2)}) collective-permute-start(bf16[2,128,1024]{2,1,0:T(8,128)(2,1)} %param.19), channel_id=1, source_target_pairs={{0,0},{1,1},{2,4},{3,5},{4,2},{5,3},{6,6},{7,7},{8,8},{9,9},{10,12... | collective-permute-start | bytes 1572872 | tf_op jit(solution)/shard_map/ppermute | solution.py:34
  89.5 42.7 %collective-permute-start.4 = (bf16[2,128,1024]{2,1,0:T(8,128)(2,1)}, bf16[2,128,1024]{2,1,0:T(8,128)(2,1)}, u32[]{:S(2)}, u32[]{:S(2)}) collective-permute-start(bf16[2,128,1024]{2,1,0:T(8,128)(2,1)} %param.20), channel_id=1, source_target_pairs={{0,0},{1,1},{2,4},{3,5},{4,2},{5,3},{6,6},{7,7},{8,8},{9,9},{10,12... | collective-permute-start | bytes 1572872 | tf_op jit(solution)/shard_map/ppermute | solution.py:34
  91.5 394.2 %all-gather.13.cloned.1.call-start = ((), (), s32[]{:S(2)}) async-start(), calls=%async_computation.8 | async-start | bytes 2621440 | tf_op jit(solution)/shard_map/all_gather | solution.py:80
  104.2 37.1 %collective-permute-start.1 = (bf16[2,128,1024]{2,1,0:T(8,128)(2,1)}, bf16[2,128,1024]{2,1,0:T(8,128)(2,1)}, u32[]{:S(2)}, u32[]{:S(2)}) collective-permute-start(bf16[2,128,1024]{2,1,0:T(8,128)(2,1)} %param.21), channel_id=1, source_target_pairs={{0,0},{1,1},{2,4},{3,5},{4,2},{5,3},{6,6},{7,7},{8,8},{9,9},{10,12... | collective-permute-start | bytes 1572872 | tf_op jit(solution)/shard_map/ppermute | solution.py:34
  128.9 33.7 %collective-permute-start.22 = (bf16[1,256,1024]{2,1,0:T(8,128)(2,1)}, bf16[1,256,1024]{2,1,0:T(8,128)(2,1)S(1)}, u32[]{:S(2)}, u32[]{:S(2)}) collective-permute-start(bf16[1,256,1024]{2,1,0:T(8,128)(2,1)} %param.25), channel_id=1, source_target_pairs={{0,0},{1,1},{2,4},{3,5},{4,2},{5,3},{6,6},{7,7},{8,8},{9,9},{10,12... | collective-permute-start | bytes 1572872 | tf_op jit(solution)/shard_map/ppermute | solution.py:34
  132.2 31.7 %collective-permute-start.28 = (bf16[1,256,1024]{2,1,0:T(8,128)(2,1)}, bf16[1,256,1024]{2,1,0:T(8,128)(2,1)}, u32[]{:S(2)}, u32[]{:S(2)}) collective-permute-start(bf16[1,256,1024]{2,1,0:T(8,128)(2,1)} %fusion.157), channel_id=1, source_target_pairs={{0,1},{1,0},{2,3},{3,2},{4,5},{5,4},{6,7},{7,6},{8,9},{9,8},{10,11... | collective-permute-start | bytes 1572872 | tf_op jit(solution)/shard_map/ppermute | solution.py:34
  141.3 36.6 %collective-permute-start.49 = (bf16[1,256,1024]{2,1,0:T(8,128)(2,1)S(1)}, bf16[1,256,1024]{2,1,0:T(8,128)(2,1)}, u32[]{:S(2)}, u32[]{:S(2)}) collective-permute-start(bf16[1,256,1024]{2,1,0:T(8,128)(2,1)S(1)} %collective-permute-done.48), channel_id=1, source_target_pairs={{0,1},{1,0},{2,3},{3,2},{4,5},{5,4},{6,7},{7,6},{8,9},{9,8},{10,11... | collective-permute-start | bytes 1572872 | tf_op jit(solution)/shard_map/ppermute | solution.py:34
  141.3 39.2 %collective-permute-start.38 = (bf16[2,128,1024]{2,1,0:T(8,128)(2,1)}, bf16[2,128,1024]{2,1,0:T(8,128)(2,1)}, u32[]{:S(2)}, u32[]{:S(2)}) collective-permute-start(bf16[2,128,1024]{2,1,0:T(8,128)(2,1)} %param.36), channel_id=1, source_target_pairs={{0,0},{1,1},{2,4},{3,5},{4,2},{5,3},{6,6},{7,7},{8,8},{9,9},{10,12... | collective-permute-start | bytes 1572872 | tf_op jit(solution)/shard_map/ppermute | solution.py:34
  152.5 47.3 %collective-permute-start.2 = (bf16[2,128,1024]{2,1,0:T(8,128)(2,1)}, bf16[2,128,1024]{2,1,0:T(8,128)(2,1)}, u32[]{:S(2)}, u32[]{:S(2)}) collective-permute-start(bf16[2,128,1024]{2,1,0:T(8,128)(2,1)} %collective-permute-done.1), channel_id=1, source_target_pairs={{0,1},{1,0},{2,3},{3,2},{4,5},{5,4},{6,7},{7,6},{8,9},{9,8},{10,11... | collective-permute-start | bytes 1572872 | tf_op jit(solution)/shard_map/ppermute | solution.py:34
  162.6 35.6 %collective-permute-start.23 = (bf16[1,256,1024]{2,1,0:T(8,128)(2,1)S(1)}, bf16[1,256,1024]{2,1,0:T(8,128)(2,1)}, u32[]{:S(2)}, u32[]{:S(2)}) collective-permute-start(bf16[1,256,1024]{2,1,0:T(8,128)(2,1)S(1)} %collective-permute-done.22), channel_id=1, source_target_pairs={{0,1},{1,0},{2,3},{3,2},{4,5},{5,4},{6,7},{7,6},{8,9},{9,8},{10,11... | collective-permute-start | bytes 1572872 | tf_op jit(solution)/shard_map/ppermute | solution.py:34
  163.7 590.1 %reduce-scatter.17.cloned.1.call-start = ((), (), s32[]{:S(2)}) async-start(), calls=%async_computation.18 | async-start | bytes 1966080 | tf_op jit(solution)/shard_map/reduce_scatter | solution.py:85
  164.0 39.4 %collective-permute-start.5 = (bf16[2,128,1024]{2,1,0:T(8,128)(2,1)}, bf16[2,128,1024]{2,1,0:T(8,128)(2,1)S(1)}, u32[]{:S(2)}, u32[]{:S(2)}) collective-permute-start(bf16[2,128,1024]{2,1,0:T(8,128)(2,1)} %collective-permute-done.4), channel_id=1, source_target_pairs={{0,1},{1,0},{2,3},{3,2},{4,5},{5,4},{6,7},{7,6},{8,9},{9,8},{10,11... | collective-permute-start | bytes 1572872 | tf_op jit(solution)/shard_map/ppermute | solution.py:34
  177.9 31.1 %collective-permute-start.26 = (bf16[1,256,1024]{2,1,0:T(8,128)(2,1)S(1)}, bf16[1,256,1024]{2,1,0:T(8,128)(2,1)S(1)}, u32[]{:S(2)}, u32[]{:S(2)}) collective-permute-start(bf16[1,256,1024]{2,1,0:T(8,128)(2,1)S(1)} %collective-permute-done.25), channel_id=1, source_target_pairs={{0,1},{1,0},{2,3},{3,2},{4,5},{5,4},{6,7},{7,6},{8,9},{9,8},{10,11... | collective-permute-start | bytes 1572872 | tf_op jit(solution)/shard_map/ppermute | solution.py:34
  180.5 36.4 %collective-permute-start.7 = (bf16[2,128,1024]{2,1,0:T(8,128)(2,1)}, bf16[2,128,1024]{2,1,0:T(8,128)(2,1)S(1)}, u32[]{:S(2)}, u32[]{:S(2)}) collective-permute-start(bf16[2,128,1024]{2,1,0:T(8,128)(2,1)} %fusion.165), channel_id=1, source_target_pairs={{0,1},{1,0},{2,3},{3,2},{4,5},{5,4},{6,7},{7,6},{8,9},{9,8},{10,11... | collective-permute-start | bytes 1572872 | tf_op jit(solution)/shard_map/ppermute | solution.py:34
  220.2 286.6 %collective-permute-start.50 = (bf16[1,512,1024]{2,1,0:T(8,128)(2,1)}, bf16[1,512,1024]{2,1,0:T(8,128)(2,1)}, u32[]{:S(2)}, u32[]{:S(2)}) collective-permute-start(bf16[1,512,1024]{2,1,0:T(8,128)(2,1)} %maximum_select_fusion.27), channel_id=1, source_target_pairs={{0,4},{1,5},{2,6},{3,7},{4,0},{5,1},{6,2},{7,3},{8,12},{9,13},{10,... | collective-permute-start | bytes 3145736 | tf_op jit(solution)/shard_map/ppermute | solution.py:34
  222.9 268.6 %collective-permute-start.40 = (bf16[2,256,1024]{2,1,0:T(8,128)(2,1)}, bf16[2,256,1024]{2,1,0:T(8,128)(2,1)}, u32[]{:S(2)}, u32[]{:S(2)}) collective-permute-start(bf16[2,256,1024]{2,1,0:T(8,128)(2,1)} %maximum_select_fusion.25), channel_id=1, source_target_pairs={{0,4},{1,5},{2,6},{3,7},{4,0},{5,1},{6,2},{7,3},{8,12},{9,13},{10,... | collective-permute-start | bytes 3145736 | tf_op jit(solution)/shard_map/ppermute | solution.py:34
  280.6 77.0 %collective-permute-start.75 = (bf16[1,341,256]{2,1,0:T(8,128)(2,1)}, bf16[1,341,256]{2,1,0:T(8,128)(2,1)}, u32[]{:S(2)}, u32[]{:S(2)}) collective-permute-start(bf16[1,341,256]{2,1,0:T(8,128)(2,1)} %bitcast.80), channel_id=1, source_target_pairs={{0,1},{1,0},{2,3},{3,2},{4,5},{5,4},{6,7},{7,6},{8,9},{9,8},{10,11... | collective-permute-start | bytes 523784 | tf_op jit(solution)/shard_map/ppermute | solution.py:34
  282.0 73.2 %collective-permute-start.71 = (bf16[2,170,256]{2,1,0:T(8,128)(2,1)}, bf16[2,170,256]{2,1,0:T(8,128)(2,1)}, u32[]{:S(2)}, u32[]{:S(2)}) collective-permute-start(bf16[2,170,256]{2,1,0:T(8,128)(2,1)} %fusion.140), channel_id=1, source_target_pairs={{0,1},{1,0},{2,3},{3,2},{4,5},{5,4},{6,7},{7,6},{8,9},{9,8},{10,11... | collective-permute-start | bytes 522248 | tf_op jit(solution)/shard_map/ppermute | solution.py:34
  301.6 93.4 %collective-permute-start.12 = (bf16[2,256,1024]{2,1,0:T(8,128)(2,1)}, bf16[2,256,1024]{2,1,0:T(8,128)(2,1)}, u32[]{:S(2)}, u32[]{:S(2)}) collective-permute-start(bf16[2,256,1024]{2,1,0:T(8,128)(2,1)} %constant_dynamic-slice_fusion.19), channel_id=1, source_target_pairs={{0,4},{1,5},{2,6},{3,7},{4,0},{5,1},{6,2},{7,3},{8,12},{9,13},{10,... | collective-permute-start | bytes 3145736 | tf_op jit(solution)/shard_map/ppermute | solution.py:34
  357.6 39.7 %collective-permute-start.31 = (bf16[1,512,1024]{2,1,0:T(8,128)(2,1)}, bf16[1,512,1024]{2,1,0:T(8,128)(2,1)}, u32[]{:S(2)}, u32[]{:S(2)}) collective-permute-start(bf16[1,512,1024]{2,1,0:T(8,128)(2,1)} %dynamic-slice_bitcast_fusion.2), channel_id=1, source_target_pairs={{0,4},{1,5},{2,6},{3,7},{4,0},{5,1},{6,2},{7,3},{8,12},{9,13},{10,... | collective-permute-start | bytes 3145736 | tf_op jit(solution)/shard_map/ppermute | solution.py:34
  402.8 34.3 %collective-permute-start.74 = (bf16[2,170,1024]{2,0,1:T(2,128)(2,1)S(1)}, bf16[2,170,1024]{2,0,1:T(2,128)(2,1)S(1)}, u32[]{:S(2)}, u32[]{:S(2)}) collective-permute-start(bf16[2,170,1024]{2,0,1:T(2,128)(2,1)S(1)} %copy.228), channel_id=1, source_target_pairs={{0,1},{1,0},{2,3},{3,2},{4,5},{5,4},{6,7},{7,6},{8,9},{9,8},{10,11... | collective-permute-start | bytes 2088968 | tf_op jit(solution)/shard_map/ppermute | solution.py:34
  410.9 58.1 %collective-permute-start.78 = (bf16[1,341,1024]{2,1,0:T(8,128)(2,1)S(1)}, bf16[1,341,1024]{2,1,0:T(8,128)(2,1)S(1)}, u32[]{:S(2)}, u32[]{:S(2)}) collective-permute-start(bf16[1,341,1024]{2,1,0:T(8,128)(2,1)S(1)} %add_convert_fusion.1), channel_id=1, source_target_pairs={{0,1},{1,0},{2,3},{3,2},{4,5},{5,4},{6,7},{7,6},{8,9},{9,8},{10,11... | collective-permute-start | bytes 2095112 | tf_op jit(solution)/shard_map/ppermute | solution.py:34
  422.1 41.3 %collective-permute-start.14 = (bf16[2,128,1024]{2,1,0:T(8,128)(2,1)S(1)}, bf16[2,128,1024]{2,1,0:T(8,128)(2,1)S(1)}, u32[]{:S(2)}, u32[]{:S(2)}) collective-permute-start(bf16[2,128,1024]{2,1,0:T(8,128)(2,1)S(1)} %multiply_convert_fusion.17), channel_id=1, source_target_pairs={{0,1},{1,0},{2,3},{3,2},{4,5},{5,4},{6,7},{7,6},{8,9},{9,8},{10,11... | collective-permute-start | bytes 1572872 | tf_op jit(solution)/shard_map/ppermute | solution.py:34
  437.1 37.6 %collective-permute-start.33 = (bf16[1,256,1024]{2,1,0:T(8,128)(2,1)S(1)}, bf16[1,256,1024]{2,1,0:T(8,128)(2,1)S(1)}, u32[]{:S(2)}, u32[]{:S(2)}) collective-permute-start(bf16[1,256,1024]{2,1,0:T(8,128)(2,1)S(1)} %multiply_convert_fusion.16), channel_id=1, source_target_pairs={{0,1},{1,0},{2,3},{3,2},{4,5},{5,4},{6,7},{7,6},{8,9},{9,8},{10,11... | collective-permute-start | bytes 1572872 | tf_op jit(solution)/shard_map/ppermute | solution.py:34
  524.1 33.5 %collective-permute-start.52 = (bf16[1,256,1024]{2,1,0:T(8,128)(2,1)S(1)}, bf16[1,256,1024]{2,1,0:T(8,128)(2,1)S(1)}, u32[]{:S(2)}, u32[]{:S(2)}) collective-permute-start(bf16[1,256,1024]{2,1,0:T(8,128)(2,1)S(1)} %dynamic-slice_convert_fusion.1), channel_id=1, source_target_pairs={{0,1},{1,0},{2,3},{3,2},{4,5},{5,4},{6,7},{7,6},{8,9},{9,8},{10,11... | collective-permute-start | bytes 1572872 | tf_op jit(solution)/shard_map/ppermute | solution.py:34
  549.7 30.4 %collective-permute-start.36 = (bf16[1,256,1024]{2,1,0:T(8,128)(2,1)S(1)}, bf16[1,256,1024]{2,1,0:T(8,128)(2,1)S(1)}, u32[]{:S(2)}, u32[]{:S(2)}) collective-permute-start(bf16[1,256,1024]{2,1,0:T(8,128)(2,1)S(1)} %dynamic-slice_convert_fusion.4), channel_id=1, source_target_pairs={{0,1},{1,0},{2,3},{3,2},{4,5},{5,4},{6,7},{7,6},{8,9},{9,8},{10,11... | collective-permute-start | bytes 1572872 | tf_op jit(solution)/shard_map/ppermute | solution.py:34
  570.3 29.9 %collective-permute-start.44 = (bf16[2,256,1024]{2,1,0:T(8,128)(2,1)}, bf16[2,256,1024]{2,1,0:T(8,128)(2,1)}, u32[]{:S(2)}, u32[]{:S(2)}) collective-permute-start(bf16[2,256,1024]{2,1,0:T(8,128)(2,1)} %maximum_select_fusion.26), channel_id=1, source_target_pairs={{0,4},{1,5},{2,6},{3,7},{4,0},{5,1},{6,2},{7,3},{8,12},{9,13},{10,... | collective-permute-start | bytes 3145736 | tf_op jit(solution)/shard_map/ppermute | solution.py:34
  587.0 179.6 %reduce-scatter.9.cloned.1.call-start = ((), (), s32[]{:S(2)}) async-start(), calls=%async_computation.11 | async-start | bytes 1310720 | tf_op jit(solution)/shard_map/reduce_scatter | solution.py:85
  701.2 112.2 %reduce-scatter.13.cloned.1.call-start = ((), (), s32[]{:S(2)}) async-start(), calls=%async_computation.14 | async-start | bytes 2621440 | tf_op jit(solution)/shard_map/reduce_scatter | solution.py:85
  712.7 140.4 %reduce-scatter.15.cloned.1.call-start = ((), (), s32[]{:S(2)}) async-start(), calls=%async_computation.16 | async-start | bytes 2621440 | tf_op jit(solution)/shard_map/reduce_scatter | solution.py:85
  726.2 142.7 %reduce-scatter.11.cloned.1.call-start = ((), (), s32[]{:S(2)}) async-start(), calls=%async_computation.13 | async-start | bytes 655360 | tf_op jit(solution)/shard_map/reduce_scatter | solution.py:85
  742.7 132.3 %reduce-scatter.7.cloned.1.call-start = ((), (), s32[]{:S(2)}) async-start(), calls=%async_computation.10 | async-start | bytes 655360 | tf_op jit(solution)/shard_map/reduce_scatter | solution.py:85
  753.7 201.8 %all-gather.23.cloned.1.call-start = ((), (), s32[]{:S(2)}) async-start(), calls=%async_computation.19 | async-start | bytes 1769472 | tf_op jit(solution)/shard_map/all_gather | solution.py:103
  766.5 194.4 %all-gather.17.cloned.1.call-start = ((), (), s32[]{:S(2)}) async-start(), calls=%async_computation.12 | async-start | bytes 1179648 | tf_op jit(solution)/shard_map/all_gather | solution.py:103
  777.2 186.4 %all-gather.19.cloned.1.call-start = ((), (), s32[]{:S(2)}) async-start(), calls=%async_computation.15 | async-start | bytes 2359296 | tf_op jit(solution)/shard_map/all_gather | solution.py:103
  777.3 36.1 %collective-permute-start.20 = (bf16[2,128,1024]{2,1,0:T(8,128)(2,1)}, bf16[2,128,1024]{2,1,0:T(8,128)(2,1)S(1)}, u32[]{:S(2)}, u32[]{:S(2)}) collective-permute-start(bf16[2,128,1024]{2,1,0:T(8,128)(2,1)} %get-tuple-element.108), channel_id=1, source_target_pairs={{0,0},{1,1},{2,4},{3,5},{4,2},{5,3},{6,6},{7,7},{8,8},{9,9},{10,12... | collective-permute-start | bytes 1572872 | tf_op jit(solution)/shard_map/ppermute | solution.py:34
  780.4 33.0 %collective-permute-start.37 = (bf16[1,256,1024]{2,1,0:T(8,128)(2,1)}, bf16[1,256,1024]{2,1,0:T(8,128)(2,1)}, u32[]{:S(2)}, u32[]{:S(2)}) collective-permute-start(bf16[1,256,1024]{2,1,0:T(8,128)(2,1)} %get-tuple-element.107), channel_id=1, source_target_pairs={{0,0},{1,1},{2,4},{3,5},{4,2},{5,3},{6,6},{7,7},{8,8},{9,9},{10,12... | collective-permute-start | bytes 1572872 | tf_op jit(solution)/shard_map/ppermute | solution.py:34
  828.3 146.9 %all-gather.21.cloned.1.call-start = ((), (), s32[]{:S(2)}) async-start(), calls=%async_computation.17 | async-start | bytes 2359296 | tf_op jit(solution)/shard_map/all_gather | solution.py:103
  848.9 32.5 %collective-permute-start.55 = (bf16[1,512,1024]{2,1,0:T(8,128)(2,1)}, bf16[1,512,1024]{2,1,0:T(8,128)(2,1)}, u32[]{:S(2)}, u32[]{:S(2)}) collective-permute-start(bf16[1,512,1024]{2,1,0:T(8,128)(2,1)} %constant_dynamic-slice_fusion.13), channel_id=1, source_target_pairs={{0,4},{1,5},{2,6},{3,7},{4,0},{5,1},{6,2},{7,3},{8,12},{9,13},{10,... | collective-permute-start | bytes 3145736 | tf_op jit(solution)/shard_map/ppermute | solution.py:34
  858.2 38.1 %collective-permute-start.46 = (bf16[2,128,1024]{2,1,0:T(8,128)(2,1)S(1)}, bf16[2,128,1024]{2,1,0:T(8,128)(2,1)S(1)}, u32[]{:S(2)}, u32[]{:S(2)}) collective-permute-start(bf16[2,128,1024]{2,1,0:T(8,128)(2,1)S(1)} %dynamic-slice_convert_fusion.2), channel_id=1, source_target_pairs={{0,1},{1,0},{2,3},{3,2},{4,5},{5,4},{6,7},{7,6},{8,9},{9,8},{10,11... | collective-permute-start | bytes 1572872 | tf_op jit(solution)/shard_map/ppermute | solution.py:34
  897.4 61.3 %collective-permute-start.47 = (bf16[2,128,1024]{2,1,0:T(8,128)(2,1)S(1)}, bf16[2,128,1024]{2,1,0:T(8,128)(2,1)S(1)}, u32[]{:S(2)}, u32[]{:S(2)}) collective-permute-start(bf16[2,128,1024]{2,1,0:T(8,128)(2,1)S(1)} %fusion.170), channel_id=1, source_target_pairs={{0,0},{1,1},{2,4},{3,5},{4,2},{5,3},{6,6},{7,7},{8,8},{9,9},{10,12... | collective-permute-start | bytes 1572872 | tf_op jit(solution)/shard_map/ppermute | solution.py:34
  900.7 59.1 %collective-permute-start.57 = (bf16[1,256,1024]{2,1,0:T(8,128)(2,1)S(1)}, bf16[1,256,1024]{2,1,0:T(8,128)(2,1)S(1)}, u32[]{:S(2)}, u32[]{:S(2)}) collective-permute-start(bf16[1,256,1024]{2,1,0:T(8,128)(2,1)S(1)} %fusion.162), channel_id=1, source_target_pairs={{0,0},{1,1},{2,4},{3,5},{4,2},{5,3},{6,6},{7,7},{8,8},{9,9},{10,12... | collective-permute-start | bytes 1572872 | tf_op jit(solution)/shard_map/ppermute | solution.py:34
  (194 other events, 2587.0 us)
Sparse Core Ops, SparseCore 0:
  29.1 33.6 all-gather.8
  64.6 31.1 all-gather.14
  97.6 36.7 all-gather.10
  163.8 34.5 all-gather.12
  587.1 28.4 reduce-scatter.16
  701.3 24.4 reduce-scatter.8
  729.6 35.1 reduce-scatter.12
  768.4 35.1 reduce-scatter.14
  807.3 24.6 reduce-scatter.10
  835.2 24.7 reduce-scatter.6
  862.7 26.2 all-gather.22
  890.8 24.8 all-gather.16
  917.8 27.4 all-gather.18
  947.1 27.9 all-gather.20

commit v2 on v1

v2 whole, which is shorter than its diff:
```python
import functools

import jax
import jax.numpy as jnp
from jax import lax
from jax.experimental import pallas as pl
from jax.experimental.pallas import tpu as pltpu
from jax.sharding import PartitionSpec as P

HEAD_SIZE = 128
SCALE = HEAD_SIZE**-0.5
AXES = ("dp", "tensor")
NT = (((1,), (1,)), ((), ()))
TN = (((0,), (0,)), ((), ()))

epsilon = 1e-05
rebuild_weight = 256.0
masked_value = -1e30


class Layout:
    def __init__(self):
        self.dp, self.tensor = lax.axis_size("dp"), lax.axis_size("tensor")
        self.half = self.tensor // 2
        self.columns = self.dp // 2
        place, plane = lax.axis_index("dp"), lax.axis_index("tensor")
        self.core, self.column = place % 2, place // 2
        self.upper, self.lower = plane // self.half, plane % self.half
        self.shard = self.core * self.half + self.lower
        self.groups = [[2 * c + core for c in range(self.columns)] for core in range(2)]

    def permute(self, value, move):
        pairs = []
        for d in range(self.dp):
            for t in range(self.tensor):
                column, core, upper, lower = move(d // 2, d % 2, t // self.half, t % self.half)
                pairs.append(
                    (
                        d * self.tensor + t,
                        (2 * column + core) * self.tensor + upper * self.half + lower,
                    )
                )
        return jax.tree.map(lambda part: lax.ppermute(part, AXES, pairs), value)

    def swap(self, value):
        return self.permute(value, lambda p, c, h, a: (p, h, c, a))

    def flip(self, value, bit):
        if bit == self.half:
            return self.permute(value, lambda p, c, h, a: (p, 1 - c, h, a))
        return self.permute(value, lambda p, c, h, a: (p, c, h, a ^ bit))

    def gather(self, value):
        value = value[None]
        bit = 1
        while bit < self.tensor:
            value = jnp.concatenate([value, self.flip(value, bit)], 0)
            bit *= 2
        return value

    def scatter(self, value):
        bit = self.half
        while bit:
            value = value.astype(jnp.bfloat16)
            other = self.flip(value[bit:], bit)
            value = value[:bit].astype(jnp.float32) + other.astype(jnp.float32)
            bit //= 2
        return value[0]

    def total(self, value):
        bit = self.half
        while bit:
            value = value.astype(jnp.bfloat16)
            value = value.astype(jnp.float32) + self.flip(value, bit).astype(jnp.float32)
            bit //= 2
        return value

    def ordered(self, pieces, axis):
        return jnp.concatenate(
            [
                lax.dynamic_index_in_dim(pieces, self.shard ^ s, 0, False)
                for s in range(self.tensor)
            ],
            axis,
        )

    def weight(self, value):
        rows = value.shape[0] // self.columns
        mine = lax.dynamic_slice_in_dim(value, self.column * rows, rows, 0)
        return lax.all_gather(
            self.swap(mine), "dp", axis=0, tiled=True, axis_index_groups=self.groups
        )

    def grad(self, value):
        part = lax.psum_scatter(
            value.astype(jnp.bfloat16),
            "dp",
            scatter_dimension=0,
            tiled=True,
            axis_index_groups=self.groups,
        )
        rows = part.shape[0] // 2

        def eighth(index):
            return lax.dynamic_slice_in_dim(part, index * rows, rows, 0)

        other = self.permute(
            eighth(1 - self.upper),
            lambda p, c, h, a: (p, c, c, a) if c != h else (p, 1 - c, h, a),
        )
        own = self.permute(eighth(self.upper), lambda p, c, h, a: (p, h, c, a))
        summed = (own.astype(jnp.float32) + other.astype(jnp.float32)).astype(jnp.bfloat16)
        return lax.all_gather(summed, "dp", axis=0, tiled=True).astype(jnp.float32)


def normalize(rows):
    mean = jnp.mean(rows, -1, keepdims=True)
    centred = rows - mean
    inverse = lax.rsqrt(jnp.mean(centred * centred, -1, keepdims=True) + epsilon)
    return (centred * inverse, inverse)


def normed(rows, gain):
    return (normalize(rows.astype(jnp.float32))[0] * gain).astype(jnp.bfloat16)


def norm_back(grad_out, gain, unit, inverse):
    scaled = grad_out * gain
    return inverse * (
        scaled
        - jnp.mean(scaled, -1, keepdims=True)
        - unit * jnp.mean(scaled * unit, -1, keepdims=True)
    )


def matmul(left, right):
    return jnp.einsum("...k,kn->...n", left, right, preferred_element_type=jnp.float32)


def matmul_back(left, right):
    return jnp.einsum("...n,kn->...k", left, right, preferred_element_type=jnp.float32)


def outer(left, right):
    rows = left.reshape(-1, left.shape[-1])
    columns = right.reshape(-1, right.shape[-1])
    return jnp.einsum("rk,rn->kn", rows, columns, preferred_element_type=jnp.float32)


def dot(left, right, dims=(((1,), (0,)), ((), ()))):
    return lax.dot_general(left, right, dims, preferred_element_type=jnp.float32)


class Tiles:
    def __init__(self, me, pieces, rows, many):
        self.me, self.pieces, self.rows, self.many = me, pieces, rows, many

    def load(self, ref, tile, *where):
        parts = [ref[(self.me ^ (tile * self.many + i), *where)] for i in range(self.many)]
        return parts[0] if self.many == 1 else jnp.concatenate(parts, 0)

    def store(self, ref, tile, value, *where, add=False):
        for i in range(self.many):
            index = (self.me ^ (tile * self.many + i), *where)
            part = value[i * self.rows : (i + 1) * self.rows]
            ref[index] = ref[index] + part if add else part

    def chunks(self, ref):
        for first in range(0, self.pieces, self.many):
            part = ref[first : first + self.many, 0]
            yield first, part.reshape(self.many * self.rows, part.shape[-1])

    def place(self, first, axis):
        extent = self.many * self.rows
        index = lax.broadcasted_iota(jnp.int32, (1, extent) if axis else (extent, 1), axis)
        piece = lax.bitwise_xor(self.me, first + index // self.rows)
        return piece * self.rows + index % self.rows


def attend_kernel(
    reduced,
    many,
    me_ref,
    offsets_ref,
    q_ref,
    kx_ref,
    vx_ref,
    km_ref,
    vm_ref,
    kc_ref,
    vc_ref,
    ka_ref,
    va_ref,
    o_ref,
    push_ref,
    lse_ref,
    alse_ref,
    square_ref,
):
    seq, head, block = pl.program_id(0), pl.program_id(1), pl.program_id(2)
    pieces, _, rows, _ = q_ref.shape
    length, tile = pieces * rows, many * rows
    tiles = Tiles(me_ref[0], pieces, rows, many)
    offset = offsets_ref[seq]
    q = tiles.load(q_ref, block, 0)

    def fold(carry, scores, values):
        top, total, acc = carry
        fresh = jnp.maximum(top, jnp.max(scores, 1, keepdims=True))
        probs = jnp.exp(scores - fresh)
        keep = jnp.exp(top - fresh)
        total = total * keep + jnp.sum(probs, 1, keepdims=True)
        acc = acc * keep + dot(probs.astype(jnp.bfloat16), values)
        return fresh, total, acc

    def empty():
        return (
            jnp.full((tile, 1), masked_value, jnp.float32),
            jnp.zeros((tile, 1), jnp.float32),
            jnp.zeros((tile, HEAD_SIZE), jnp.float32),
        )

    main, memory = empty(), empty()
    for base, keys_ref, values_ref in ((0, kc_ref, vc_ref), (length, km_ref, vm_ref)):
        for (first, keys), (_, values) in zip(tiles.chunks(keys_ref), tiles.chunks(values_ref)):
            scores = dot(q, keys, NT) * SCALE
            if base:
                memory = fold(memory, scores, values)
            allowed = tiles.place(first, 1) + base >= offset
            main = fold(main, jnp.where(allowed, scores, masked_value), values)

    def below(index, carry):
        keys, values = tiles.load(kx_ref, index, 0), tiles.load(vx_ref, index, 0)
        return fold(carry, dot(q, keys, NT) * SCALE, values)

    main = lax.fori_loop(0, block, below, main)
    scores = dot(q, tiles.load(kx_ref, block, 0), NT) * SCALE
    causal = lax.broadcasted_iota(jnp.int32, (tile, tile), 1) <= lax.broadcasted_iota(
        jnp.int32, (tile, tile), 0
    )
    top, total, acc = fold(
        main, jnp.where(causal, scores, masked_value), tiles.load(vx_ref, block, 0)
    )
    tiles.store(o_ref, block, (acc / total).astype(jnp.bfloat16), 0)

    scores = dot(q, ka_ref[0], NT) * SCALE
    place = lax.broadcasted_iota(jnp.int32, (1, ka_ref.shape[1]), 1)
    atop, atotal, aacc = fold(
        empty(), jnp.where(place < reduced, scores, masked_value), va_ref[0]
    )
    differ = memory[2] / memory[1] - aacc / atotal
    tiles.store(push_ref, block, (-2.0 * rebuild_weight * differ).astype(jnp.bfloat16), 0)

    @pl.when((seq == 0) & (head == 0) & (block == 0))
    def _():
        square_ref[...] = jnp.zeros_like(square_ref)

    square_ref[...] += jnp.sum((differ * differ).reshape(tile // 8, 8, HEAD_SIZE), 0)

    def row(column):
        return jnp.transpose(jnp.broadcast_to(column, (tile, HEAD_SIZE)))[:1]

    lse_ref[0] = row(top + jnp.log(total))
    alse_ref[0] = row(atop + jnp.log(atotal))


def attention_specs(pieces, rows, heads, padded, tile):
    def whole(shift):
        return pl.BlockSpec(
            (pieces, 1, rows, HEAD_SIZE), lambda s, h, b, *_: (0, s, 0, h + shift * heads)
        )

    def added(shift):
        return pl.BlockSpec((1, padded, HEAD_SIZE), lambda s, h, b, *_: (s, 0, h + shift * heads))

    stat = pl.BlockSpec((1, 1, tile), lambda s, h, b, *_: (s * heads + h, 0, b))
    keys = [whole(0), whole(1), whole(2)] + [whole(0), whole(1)] * 2 + [added(0), added(1)]
    return whole, stat, keys


def tile_pieces(pieces, rows):
    return min(pieces, max(1, 512 // rows))


def attend(me, offsets, triples, memory, older, added, reduced):
    pieces, count, rows, _ = triples.shape
    heads = memory.shape[-1] // (2 * HEAD_SIZE)
    padded, length = added.shape[1], pieces * rows
    many = tile_pieces(pieces, rows)
    whole, stat, keys = attention_specs(pieces, rows, heads, padded, many * rows)
    tokens = jax.ShapeDtypeStruct((pieces, count, rows, heads * HEAD_SIZE), jnp.bfloat16)
    stats = jax.ShapeDtypeStruct((count * heads, 1, length), jnp.float32)
    work = count * heads * length * (3 * length + padded)
    return pl.pallas_call(
        functools.partial(attend_kernel, reduced, many),
        grid_spec=pltpu.PrefetchScalarGridSpec(
            num_scalar_prefetch=2,
            grid=(count, heads, pieces // many),
            in_specs=keys,
            out_specs=[
                whole(0),
                whole(0),
                stat,
                stat,
                pl.BlockSpec((8, HEAD_SIZE), lambda *_: (0, 0)),
            ],
        ),
        out_shape=[tokens, tokens, stats, stats, jax.ShapeDtypeStruct((8, HEAD_SIZE), jnp.float32)],
        cost_estimate=pl.CostEstimate(
            flops=work * 4 * HEAD_SIZE * 2, bytes_accessed=work // 64, transcendentals=work
        ),
        name="attend",
    )(me, offsets, triples, triples, triples, memory, memory, older, older, added, added)


def attend_back_kernel(
    reduced,
    many,
    heads,
    me_ref,
    offsets_ref,
    q_ref,
    kx_ref,
    vx_ref,
    km_ref,
    vm_ref,
    kc_ref,
    vc_ref,
    ka_ref,
    va_ref,
    o_ref,
    do_ref,
    push_ref,
    lse_ref,
    alse_ref,
    dx_ref,
    dm_ref,
    dc_ref,
    da_ref,
    kx_acc,
    vx_acc,
    km_acc,
    vm_acc,
    kc_acc,
    vc_acc,
    ka_acc,
    va_acc,
):
    seq, head, block = pl.program_id(0), pl.program_id(1), pl.program_id(2)
    pieces, _, rows, _ = q_ref.shape
    length, tile = pieces * rows, many * rows
    tiles = Tiles(me_ref[0], pieces, rows, many)
    offset = offsets_ref[seq]
    q, grad = tiles.load(q_ref, block, 0), tiles.load(do_ref, block, 0)

    @pl.when(block == 0)
    def _():
        for ref in (kx_acc, vx_acc, km_acc, vm_acc, kc_acc, vc_acc, ka_acc, va_acc):
            ref[...] = jnp.zeros_like(ref)

    lse = lse_ref[0]
    both = grad.astype(jnp.float32) * tiles.load(o_ref, block, 0).astype(jnp.float32)
    delta = jnp.sum(jnp.transpose(both), 0, keepdims=True)

    def piece(keys, values, allowed):
        scores = dot(keys, q, NT) * SCALE
        if allowed is not None:
            scores = jnp.where(allowed, scores, masked_value)
        probs = jnp.exp(scores - lse)
        dv = dot(probs.astype(jnp.bfloat16), grad)
        dp = dot(values, grad, NT)
        ds = (probs * (dp - delta)).astype(jnp.bfloat16)
        return dot(ds, q), dv, dot(ds, keys, TN)

    dq = jnp.zeros((tile, HEAD_SIZE), jnp.float32)
    for base, keys_ref, values_ref, k_acc, v_acc in (
        (0, kc_ref, vc_ref, kc_acc, vc_acc),
        (length, km_ref, vm_ref, km_acc, vm_acc),
    ):
        for (first, keys), (_, values) in zip(tiles.chunks(keys_ref), tiles.chunks(values_ref)):
            dk, dv, part = piece(keys, values, tiles.place(first, 0) + base >= offset)
            k_acc[first : first + many] += dk.reshape(many, rows, HEAD_SIZE)
            v_acc[first : first + many] += dv.reshape(many, rows, HEAD_SIZE)
            dq += part

    def token_tile(index, allowed, dq):
        dk, dv, part = piece(tiles.load(kx_ref, index, 0), tiles.load(vx_ref, index, 0), allowed)
        tiles.store(kx_acc, index, dk, add=True)
        tiles.store(vx_acc, index, dv, add=True)
        return dq + part

    dq = lax.fori_loop(0, block, lambda index, dq: token_tile(index, None, dq), dq)
    causal = lax.broadcasted_iota(jnp.int32, (tile, tile), 0) <= lax.broadcasted_iota(
        jnp.int32, (tile, tile), 1
    )
    dq = token_tile(block, causal, dq)

    def columns(kind):
        return pl.ds(pl.multiple_of((kind * heads + head) * HEAD_SIZE, HEAD_SIZE), HEAD_SIZE)

    tiles.store(dx_ref, block, (dq * SCALE).astype(jnp.bfloat16), 0, slice(None), columns(0))

    push = tiles.load(push_ref, block, 0)
    place = lax.broadcasted_iota(jnp.int32, (ka_ref.shape[1], 1), 0)
    scores = jnp.where(place < reduced, dot(ka_ref[0], q, NT) * SCALE, masked_value)
    probs = jnp.exp(scores - alse_ref[0])
    va_acc[...] += dot(probs.astype(jnp.bfloat16), push)
    dp = dot(va_ref[0], push, NT)
    shift = jnp.sum(probs * dp, 0, keepdims=True)
    ka_acc[...] += dot((probs * (dp - shift)).astype(jnp.bfloat16), q)

    @pl.when(block == pl.num_programs(2) - 1)
    def _():
        dx_ref[:, 0, :, columns(1)] = (kx_acc[...] * SCALE).astype(jnp.bfloat16)
        dx_ref[:, 0, :, columns(2)] = vx_acc[...].astype(jnp.bfloat16)
        dm_ref[:, 0, :, columns(0)] = (km_acc[...] * SCALE).astype(jnp.bfloat16)
        dm_ref[:, 0, :, columns(1)] = vm_acc[...].astype(jnp.bfloat16)
        dc_ref[:, 0, :, columns(0)] = (kc_acc[...] * SCALE).astype(jnp.bfloat16)
        dc_ref[:, 0, :, columns(1)] = vc_acc[...].astype(jnp.bfloat16)
        da_ref[0, :, columns(0)] = (ka_acc[...] * SCALE).astype(jnp.bfloat16)
        da_ref[0, :, columns(1)] = va_acc[...].astype(jnp.bfloat16)


def attend_back(
    me, offsets, triples, memory, older, added, out, grad, push, lse, alse, reduced
):
    pieces, count, rows, _ = triples.shape
    heads = memory.shape[-1] // (2 * HEAD_SIZE)
    padded, length = added.shape[1], pieces * rows
    many = tile_pieces(pieces, rows)
    whole, stat, keys = attention_specs(pieces, rows, heads, padded, many * rows)

    def result(like):
        if like.ndim == 3:
            return pl.BlockSpec((1, *like.shape[1:]), lambda s, h, b, *_: (s, 0, 0))
        return pl.BlockSpec((pieces, 1, rows, like.shape[-1]), lambda s, h, b, *_: (0, s, 0, 0))

    outputs = [triples, memory, older, added]
    work = count * heads * length * (3 * length + padded)
    return pl.pallas_call(
        functools.partial(attend_back_kernel, reduced, many, heads),
        grid_spec=pltpu.PrefetchScalarGridSpec(
            num_scalar_prefetch=2,
            grid=(count, heads, pieces // many),
            in_specs=keys + [whole(0)] * 3 + [stat, stat],
            out_specs=[result(like) for like in outputs],
            scratch_shapes=[pltpu.VMEM((pieces, rows, HEAD_SIZE), jnp.float32)] * 6
            + [pltpu.VMEM((padded, HEAD_SIZE), jnp.float32)] * 2,
        ),
        out_shape=[jax.ShapeDtypeStruct(like.shape, jnp.bfloat16) for like in outputs],
        cost_estimate=pl.CostEstimate(
            flops=work * 10 * HEAD_SIZE * 2, bytes_accessed=work // 32, transcendentals=work
        ),
        name="attend_back",
    )(
        me,
        offsets,
        triples,
        triples,
        triples,
        memory,
        memory,
        older,
        older,
        added,
        added,
        out,
        grad,
        push,
        lse,
        alse,
    )


def feedforward_kernel(chunk, rows_ref, grad_ref, up_ref, down_ref, *refs):
    if len(refs) > 4:
        up_in, down_in, out_ref, back_ref, gup_ref, gdown_ref, up_acc, down_acc = refs
    else:
        out_ref, back_ref, up_acc, down_acc = refs
    width, hidden = up_ref.shape
    rows, grad = rows_ref[...].reshape(-1, width), grad_ref[...].reshape(-1, width)
    out = back = None

    @pl.when(pl.program_id(0) == 0)
    def _():
        if len(refs) > 4:
            up_acc[...] = up_in[...]
            down_acc[...] = down_in[...]
        else:
            up_acc[...] = jnp.zeros_like(up_acc)
            down_acc[...] = jnp.zeros_like(down_acc)

    for start in range(0, hidden, chunk):
        part = slice(start, start + chunk)
        up, down = up_ref[:, part], down_ref[part]
        u = dot(rows, up)
        root, cube = 0.7978845608028654, 0.044715
        square = u * u
        bend = jnp.tanh(root * (u + cube * (square * u)))
        half = 0.5 * (1.0 + bend)
        active = (u * half).astype(jnp.bfloat16)
        slope = half + 0.5 * u * (1.0 - bend * bend) * (root * (1.0 + 3.0 * cube * square))
        pre = (dot(grad, down, NT) * slope).astype(jnp.bfloat16)
        fresh = dot(active, down)
        out = fresh if out is None else out + fresh
        fresh = dot(pre, up, NT)
        back = fresh if back is None else back + fresh
        down_acc[part] += dot(active, grad, TN)
        up_acc[:, part] += dot(rows, pre, TN)
    out_ref[...] = out.astype(jnp.bfloat16).reshape(out_ref.shape)
    back_ref[...] = back.astype(jnp.bfloat16).reshape(back_ref.shape)
    if len(refs) > 4:

        @pl.when(pl.program_id(0) == pl.num_programs(0) - 1)
        def _():
            gup_ref[...] = up_acc[...].astype(gup_ref.dtype)
            gdown_ref[...] = down_acc[...].astype(gdown_ref.dtype)


def feedforward(rows, grad, up, down, before):
    pieces, count, each, width = rows.shape
    hidden = up.shape[1]
    many = min(pieces, max(1, 512 // (count * each)))
    block = pl.BlockSpec((many, count, each, width), lambda s: (s, 0, 0, 0))

    def whole(like):
        return pl.BlockSpec(like.shape, lambda s: (0, 0), pipeline_mode=pl.Buffered(1))

    kind = jnp.bfloat16 if before else jnp.float32
    total = pieces * count * each
    return pl.pallas_call(
        functools.partial(feedforward_kernel, min(512, hidden)),
        grid=(pieces // many,),
        in_specs=[block, block, whole(up), whole(down)] + [whole(up), whole(down)] * bool(before),
        out_specs=[block, block, whole(up), whole(down)],
        scratch_shapes=[
            pltpu.VMEM(up.shape, jnp.float32),
            pltpu.VMEM(down.shape, jnp.float32),
        ]
        * bool(before),
        out_shape=[jax.ShapeDtypeStruct(rows.shape, jnp.bfloat16)] * 2
        + [jax.ShapeDtypeStruct(up.shape, kind), jax.ShapeDtypeStruct(down.shape, kind)],
        cost_estimate=pl.CostEstimate(
            flops=12 * total * width * hidden,
            bytes_accessed=8 * total * width + 12 * width * hidden,
            transcendentals=total * hidden,
        ),
        name="feedforward",
    )(rows, grad, up, down, *before)


def stack_kernel(reduced, me_ref, memory_ref, stacked_ref, rows_acc):
    pieces, _, rows, width = memory_ref.shape
    blocks, extent, lanes = rows_acc.shape
    padded = stacked_ref.shape[1]
    keep = lax.broadcasted_iota(jnp.int32, (padded, 1), 0) < reduced
    for block in range(blocks):
        columns = slice(block * lanes, (block + 1) * lanes)
        for piece in range(pieces):
            start = pl.multiple_of((me_ref[0] ^ piece) * rows, rows)
            rows_acc[block, pl.ds(start, rows)] = memory_ref[piece, 0, :, columns].astype(
                jnp.float32
            )
        rows_acc[block, pieces * rows :] = jnp.zeros((extent - pieces * rows, lanes), jnp.float32)
        for tap in range(3):
            taken = rows_acc[block, pl.ds(tap, padded, stride=3)]
            start = tap * width + block * lanes
            stacked_ref[0, :, start : start + lanes] = jnp.where(keep, taken, 0.0).astype(
                jnp.bfloat16
            )


def stack(me, memory, reduced, padded):
    pieces, count, rows, width = memory.shape
    return pl.pallas_call(
        functools.partial(stack_kernel, reduced),
        grid_spec=pltpu.PrefetchScalarGridSpec(
            num_scalar_prefetch=1,
            grid=(count,),
            in_specs=[pl.BlockSpec((pieces, 1, rows, width), lambda s, *_: (0, s, 0, 0))],
            out_specs=pl.BlockSpec((1, padded, 3 * width), lambda s, *_: (s, 0, 0)),
            scratch_shapes=[pltpu.VMEM((width // 128, 3 * padded, 128), jnp.float32)],
        ),
        out_shape=jax.ShapeDtypeStruct((count, padded, 3 * width), jnp.bfloat16),
        cost_estimate=pl.CostEstimate(
            flops=0, bytes_accessed=4 * memory.size, transcendentals=0
        ),
        name="stack_memory",
    )(me, memory)


class Group:
    def __init__(self, layout, inputs, memory, older, offsets, cotangent):
        self.layout, self.offsets = layout, layout.swap(offsets)
        self.me = layout.shard.reshape(1).astype(jnp.int32)
        self.count = inputs.shape[0]
        self.length = inputs.shape[1] * layout.tensor
        self.reduced = self.length // 3
        self.padded = -(-self.reduced // 128) * 128
        self.raw = layout.swap(jnp.stack([inputs, memory]))
        self.older = layout.swap(older)
        self.cotangent = layout.swap(cotangent)

    def enter(self, gain):
        layout = self.layout
        whole = layout.gather(self.raw)
        self.memory_rows = whole[:, 1]
        self.token_z = normed(whole[:, 0], gain)
        self.memory_z = normed(whole[:, 1], gain)
        self.older_z = normed(layout.gather(self.older), gain)
        self.stacked = stack(self.me, self.memory_rows, self.reduced, self.padded)

    def compress(self, squeeze, pair_weight, gain):
        layout = self.layout
        self.appended = matmul(self.stacked, squeeze).astype(jnp.bfloat16)
        whole = layout.ordered(layout.gather(self.appended), -1)
        self.added_unit, self.added_inverse = normalize(whole.astype(jnp.float32))
        rows = (self.added_unit * gain).astype(jnp.bfloat16)
        self.added = matmul(rows, pair_weight).astype(jnp.bfloat16)

    def attend(self, triple_weight, pair_weight):
        self.triples = matmul(self.token_z, triple_weight).astype(jnp.bfloat16)
        self.memory_pairs = matmul(self.memory_z, pair_weight).astype(jnp.bfloat16)
        self.older_pairs = matmul(self.older_z, pair_weight).astype(jnp.bfloat16)
        self.attention, self.push, self.lse, self.added_lse, squares = attend(
            self.me,
            self.offsets,
            self.triples,
            self.memory_pairs,
            self.older_pairs,
            self.added,
            self.reduced,
        )
        self.squares = jnp.sum(squares)

    def middle(self, out_weight, gain):
        layout = self.layout
        branch = layout.scatter(matmul(self.attention, out_weight))
        self.hidden = self.raw[0].astype(jnp.float32) + branch
        self.hidden_unit, self.hidden_inverse = normalize(self.hidden)
        self.feed_rows = layout.gather((self.hidden_unit * gain).astype(jnp.bfloat16))
        self.grad_rows = layout.gather(self.cotangent)

    def feed(self, up_weight, down_weight, before):
        out, back, grad_up, grad_down = feedforward(
            self.feed_rows, self.grad_rows, up_weight, down_weight, before
        )
        self.feed_out, self.feed_back = out, back
        return grad_up, grad_down

    def leave(self):
        layout = self.layout
        return layout.swap((self.hidden + layout.scatter(self.feed_out)).astype(jnp.bfloat16))

    def middle_back(self, gain, out_weight):
        layout = self.layout
        grad = layout.scatter(self.feed_back)
        self.feed_gain = jnp.sum(grad * self.hidden_unit, (0, 1))
        self.grad_hidden = self.cotangent.astype(jnp.float32) + norm_back(
            grad, gain, self.hidden_unit, self.hidden_inverse
        )
        whole = layout.gather(self.grad_hidden.astype(jnp.bfloat16))
        self.grad_attention = matmul_back(whole, out_weight).astype(jnp.bfloat16)
        return outer(self.attention, whole)

    def attend_back(self):
        self.grad_triples, self.grad_memory, self.grad_older, self.grad_added = attend_back(
            self.me,
            self.offsets,
            self.triples,
            self.memory_pairs,
            self.older_pairs,
            self.added,
            self.attention,
            self.grad_attention,
            self.push,
            self.lse,
            self.added_lse,
            self.reduced,
        )

    def compress_back(self, pair_weight, gain):
        layout = self.layout
        grad = layout.total(matmul_back(self.grad_added, pair_weight))
        grad = norm_back(grad, gain, self.added_unit, self.added_inverse).astype(jnp.bfloat16)
        extent = self.appended.shape[2]
        mine = lax.dynamic_slice_in_dim(grad, layout.shard * extent, extent, 2)
        return outer(self.stacked, mine)

    def enter_back(self, triple_weight, gain):
        layout = self.layout
        grad = layout.scatter(matmul_back(self.grad_triples, triple_weight))
        unit, inverse = normalize(self.raw[0].astype(jnp.float32))
        full = self.grad_hidden + norm_back(grad, gain, unit, inverse)
        return layout.swap(full.astype(jnp.bfloat16)).astype(jnp.float32)

    def projection_grads(self):
        width = self.grad_triples.shape[-1] // 3
        triple = outer(self.token_z, self.grad_triples)
        pair = outer(self.memory_z, self.grad_memory) + outer(self.older_z, self.grad_older)
        return triple + jnp.pad(pair, ((0, 0), (width, 0)))

    def leave_appended(self):
        return self.layout.swap(self.appended)[:, : self.reduced]


def per_device(
    inputs_short,
    memory_short,
    compressed_short,
    offsets_short,
    inputs_long,
    memory_long,
    compressed_long,
    offsets_long,
    query_weight,
    key_weight,
    value_weight,
    out_weight,
    up_weight,
    down_weight,
    compress_weight,
    attention_gain,
    feedforward_gain,
    cotangent_short,
    cotangent_long,
):
    layout = Layout()
    width, local_width = query_weight.shape
    short = Group(
        layout, inputs_short, memory_short, compressed_short, offsets_short, cotangent_short
    )
    long = Group(layout, inputs_long, memory_long, compressed_long, offsets_long, cotangent_long)
    groups = (short, long)
    triple_weight = layout.weight(jnp.concatenate([query_weight, key_weight, value_weight], 1))
    pair_weight = triple_weight[:, local_width:]
    squeeze = layout.weight(compress_weight.reshape(3 * width, local_width))
    output_weight = layout.weight(out_weight)
    up, down = layout.weight(up_weight), layout.weight(down_weight)

    before = ()
    grad_out = grad_squeeze = grad_triple = 0.0
    for group in groups:
        group.enter(attention_gain)
        group.compress(squeeze, pair_weight, attention_gain)
        group.attend(triple_weight, pair_weight)
        group.middle(output_weight, feedforward_gain)
        before = group.feed(up, down, before)
        grad_out += group.middle_back(feedforward_gain, output_weight)
        group.attend_back()
        grad_squeeze += group.compress_back(pair_weight, attention_gain)
        grad_triple += group.projection_grads()
    up_sum, down_sum = map(layout.grad, before)
    out_sum = layout.grad(grad_out)
    squeeze_sum = layout.grad(grad_squeeze).reshape(3, width, local_width)
    triple_sum = layout.grad(grad_triple)
    attention_part = (
        jnp.sum(grad_triple * triple_weight.astype(jnp.float32), 1) / attention_gain
    )
    gain_one, gain_two, square_total = lax.psum(
        (
            attention_part,
            short.feed_gain + long.feed_gain,
            short.squares + long.squares,
        ),
        AXES,
    )
    rows_all = sum(group.count * group.length for group in groups) * layout.dp
    return (
        short.leave(),
        long.leave(),
        short.enter_back(triple_weight, attention_gain),
        long.enter_back(triple_weight, attention_gain),
        short.leave_appended(),
        long.leave_appended(),
        triple_sum[:, :local_width],
        triple_sum[:, local_width : 2 * local_width],
        triple_sum[:, 2 * local_width :],
        out_sum,
        up_sum,
        down_sum,
        squeeze_sum,
        gain_one,
        gain_two,
        square_total / rows_all,
    )


def solution(mesh):
    in_specs = (
        P("dp", "tensor", None),
        P("dp", "tensor", None),
        P("dp", "tensor", None),
        P("dp"),
        P("dp", "tensor", None),
        P("dp", "tensor", None),
        P("dp", "tensor", None),
        P("dp"),
        P(None, "tensor"),
        P(None, "tensor"),
        P(None, "tensor"),
        P("tensor", None),
        P(None, "tensor"),
        P("tensor", None),
        P(None, None, "tensor"),
        P(),
        P(),
        P("dp", "tensor", None),
        P("dp", "tensor", None),
    )
    out_specs = (
        P("dp", "tensor", None),
        P("dp", "tensor", None),
        P("dp", "tensor", None),
        P("dp", "tensor", None),
        P("dp", None, "tensor"),
        P("dp", None, "tensor"),
        P(None, "tensor"),
        P(None, "tensor"),
        P(None, "tensor"),
        P("tensor", None),
        P(None, "tensor"),
        P("tensor", None),
        P(None, None, "tensor"),
        P(),
        P(),
        P(),
    )
    return jax.shard_map(
        per_device, mesh=mesh, in_specs=in_specs, out_specs=out_specs, check_vma=False
    )
```

time: 1000 us -> 841 us (0.84)
  matrix products: 269 us -> 78.1 us
  Pallas kernels: 0 us -> 128 us
  other arithmetic: 171 us -> 106 us
  local copies, waits for them, and re-layouts: 75.5 us -> 50.5 us
  waiting for transfers between devices: 270 us -> 285 us
    dot_general x74 -> x28, matrix products: 260 us -> 78.1 us  [the longest x12 35 us: matmul(): jnp.einsum('...k,kn->...n', left, right, preferred_element_type=jnp.float32)]
    pallas_call x0 -> x8, Pallas kernels: none -> 128 us  [the longest x2 44.8 us: feedforward(): pl.pallas_call(functools.partial(feedforward_kernel, min(512, hidden)), g...]
    select_n x28 -> x0, other arithmetic: 54 us -> none  [the longest x26 47.8 us: join(): jnp.where(second, jnp.concatenate([other, own], axis), jnp.concatenate([o...]
    concatenate x4 -> x20, other arithmetic: 3.29 us -> 32.3 us  [gather(): value = jnp.concatenate([value, self.flip(value, bit)], 0)]
    convert_element_type x15 -> x14, other arithmetic: 43.4 us -> 18.4 us  [the longest x8 9.99 us: scatter(): value = value.astype(jnp.bfloat16)]
    ppermute x81 -> x73, waiting for transfers between devices: 262 us -> 284 us  [permute(): return jax.tree.map(lambda part: lax.ppermute(part, AXES, pairs), value)]
    reduce_sum x12 -> x4, other arithmetic: 20.9 us -> 2.26 us  [the longest x2 1.2 us: attend(): self.squares = jnp.sum(squares)]
    unnamed x305 -> x175, local copies, waits for them, and re-layouts: 31.3 us -> 15.8 us
  transfers between devices with their start and end apart: 95 -> 86, of which waited for: 28 -> 27; matrix products, arithmetic and copies ran while one was open for 48% -> 26% of each run, Pallas kernels for 0% -> 10%
where the time goes in v2:
time: 841 us; the launch traced here: 833 us
  waiting for transfers between devices  285 us (34%)
  Pallas kernels  128 us (15%)
  starting transfers between devices  106 us (13%)
  other arithmetic  106 us (13%)
  matrix products  78.1 us (9%)
  blocking collectives  60.5 us (7%)
  local copies, waits for them, and re-layouts  50.5 us (6%)
  between operations  19.2 us (2%)
    ppermute x73, waiting for transfers between devices, permute(): return jax.tree.map(lambda part: lax.ppermute(part, AXES, pairs), value)  284 us
    ppermute x73, starting transfers between devices, permute(): return jax.tree.map(lambda part: lax.ppermute(part, AXES, pairs), value)  105 us
    pallas_call x2, Pallas kernels, feedforward(): pl.pallas_call(functools.partial(feedforward_kernel, min(512, hidden)), g...  44.8 us
    pallas_call x2, Pallas kernels, attend_back(): pl.pallas_call(functools.partial(attend_back_kernel, reduced, many, heads...  41.6 us
    psum x1, blocking collectives, per_device(): lax.psum((attention_part, short.feed_gain + long.feed_gain, short.squares...  39.2 us
    dot_general x12, matrix products, matmul(): jnp.einsum('...k,kn->...n', left, right, preferred_element_type=jnp.float32)  35 us
    pallas_call x2, Pallas kernels, attend(): pl.pallas_call(functools.partial(attend_kernel, reduced, many), grid_spec...  33.6 us
    concatenate x20, other arithmetic, gather(): value = jnp.concatenate([value, self.flip(value, bit)], 0)  32.3 us
  transfers between devices with their start and end apart: 86, of which 27 were waited for; matrix products, arithmetic and copies ran while one was open for 26% of the time, Pallas kernels for 10%

profile of v2, /device:TPU:1, one launch (start us, length us, event | category | flops | bytes accessed | tf_op | source)
XLA Modules:
  0.0 832.8 jit_solution(947351716505861002)
XLA Ops:
  8.5 5.6 collective-permute-start.4
  14.1 9.7 %collective-permute-done.4 = bf16[256,768]{1,0:T(8,128)(2,1)S(1)} collective-permute-done((bf16[256,768]{1,0:T(8,128)(2,1)S(1)}, bf16[256,768]{1,0:T(8,128)(2,1)S(1)}, u32[]{:S(2)}, u32[]{:S(2)}) %collective-permute-start.4) | collective-permute-done | bytes 393248 | tf_op jit(solution)/shard_map/ppermute | solution.py:43
  28.5 12.5 %collective-permute-done.8 = bf16[768,256]{0,1:T(8,128)(2,1)S(1)} collective-permute-done((bf16[768,256]{0,1:T(8,128)(2,1)}, bf16[768,256]{0,1:T(8,128)(2,1)S(1)}, u32[]{:S(2)}, u32[]{:S(2)}) %collective-permute-start.8) | collective-permute-done | bytes 393248 | tf_op jit(solution)/shard_map/ppermute | solution.py:43
  45.0 4.5 collective-permute-start
  49.6 19.0 %collective-permute-done.5 = bf16[2,128,1024]{2,1,0:T(8,128)(2,1)S(1)} collective-permute-done((bf16[2,128,1024]{2,1,0:T(8,128)(2,1)}, bf16[2,128,1024]{2,1,0:T(8,128)(2,1)S(1)}, u32[]{:S(2)}, u32[]{:S(2)}) %collective-permute-start.5) | collective-permute-done | bytes 524320 | tf_op jit(solution)/shard_map/ppermute | solution.py:43
  71.1 4.9 collective-permute-start.24
  77.9 6.3 collective-permute-done.6
  85.3 7.4 collective-permute-done
  92.7 21.1 %collective-permute-done.28 = bf16[1,256,1024]{2,1,0:T(8,128)(2,1)} collective-permute-done((bf16[1,256,1024]{2,1,0:T(8,128)(2,1)S(1)}, bf16[1,256,1024]{2,1,0:T(8,128)(2,1)}, u32[]{:S(2)}, u32[]{:S(2)}) %collective-permute-start.28) | collective-permute-done | bytes 524320 | tf_op jit(solution)/shard_map/ppermute | solution.py:43
  114.6 5.2 collective-permute-start.19
  124.8 23.5 %collective-permute-done.29 = bf16[1,1,256,1024]{3,2,0,1:T(8,128)(2,1)} collective-permute-done((bf16[1,1,256,1024]{3,2,0,1:T(8,128)(2,1)}, bf16[1,1,256,1024]{3,2,0,1:T(8,128)(2,1)}, u32[]{:S(2)}, u32[]{:S(2)}) %collective-permute-start.29) | collective-permute-done | bytes 524320 | tf_op jit(solution)/shard_map/ppermute | solution.py:43
  150.6 9.8 %all_gather.32 = bf16[256,1024]{1,0:T(8,128)(2,1)} all-gather(bf16[64,1024]{1,0:T(8,128)(2,1)S(1)} %collective-permute-done.11), channel_id=1, replica_groups={{0,8,16,24},{4,12,20,28},{1,9,17,25},{5,13,21,29},{2,10,18,26},{6,14,22..., dimensions={0}, use_global_device_ids=true | all-gather | bytes 655360 | tf_op jit(solution)/shard_map/all_gather | solution.py:90
  160.4 7.2 collective-permute-start.1
  171.2 4.7 collective-permute-start.20
  188.2 3.9 fusion.93.kc_ref.vc_ref
  217.0 4.2 stack_memory.3
  225.9 4.5 convolution_convert_fusion.4.q_ref.kx_ref.vx_ref
  253.3 21.0 %attend.3 = (bf16[4,1,256,256]{3,2,1,0:T(8,128)(2,1)}, bf16[4,1,256,256]{3,2,1,0:T(8,128)(2,1)}, f32[2,1,1024]{2,1,0:T(1,128)}, f32[2,1,1024]{2,1,0:T(1,128)}, f32[8,128]{1,0:T(8,128)}) custom-call(s32[1]{0:T(128)} %bitcast.3.me_ref, s32[1]{0:T(128)} %collective-permute-done.25.offsets_ref, bf16[4,1,256,768]{3,2,1,0:T(8,128)(2,1)} %fusion.88.q_ref.kx_ref.vx_ref, ...), custom_call_target="tpu_custom_call" | custom-call | flops 7247757312 | bytes 110592 | tf_op jit(solution)/shard_map/attend/pallas_call | solution.py:294
  287.7 12.6 %attend.2 = (bf16[4,2,128,256]{3,2,1,0:T(8,128)(2,1)}, bf16[4,2,128,256]{3,2,1,0:T(8,128)(2,1)}, f32[4,1,512]{2,1,0:T(1,128)}, f32[4,1,512]{2,1,0:T(1,128)}, f32[8,128]{1,0:T(8,128)}) custom-call(s32[1]{0:T(128)} %bitcast.3.me_ref, s32[2]{0:T(128)} %copy-done.77, bf16[4,2,128,768]{3,2,1,0:T(8,128)(2,1)} %convolution_convert_fusion.4.q_ref.kx_ref.vx_ref, ...), custom_call_target="tpu_custom_call" | custom-call | flops 3758096384 | bytes 57344 | tf_op jit(solution)/shard_map/attend/pallas_call | solution.py:294
  312.1 27.9 %collective-permute-done.34 = bf16[1,1,256,1024]{3,2,1,0:T(8,128)(2,1)S(1)} collective-permute-done((bf16[1,1,256,1024]{3,2,1,0:T(8,128)(2,1)S(1)}, bf16[1,1,256,1024]{3,2,1,0:T(8,128)(2,1)S(1)}, u32[]{:S(2)}, u32[]{:S(2)}) %collective-permute-start.34) | collective-permute-done | bytes 524320 | tf_op jit(solution)/shard_map/ppermute | solution.py:43
  341.5 9.7 %collective-permute-done.13 = bf16[1,2,128,1024]{3,2,1,0:T(8,128)(2,1)S(1)} collective-permute-done((bf16[1,2,128,1024]{3,2,1,0:T(8,128)(2,1)S(1)}, bf16[1,2,128,1024]{3,2,1,0:T(8,128)(2,1)S(1)}, u32[]{:S(2)}, u32[]{:S(2)}) %collective-permute-start.13) | collective-permute-done | bytes 524320 | tf_op jit(solution)/shard_map/ppermute | solution.py:43
  363.8 9.9 %collective-permute-done.14 = bf16[1,2,128,1024]{3,2,1,0:T(8,128)(2,1)S(1)} collective-permute-done((bf16[1,2,128,1024]{3,2,1,0:T(8,128)(2,1)S(1)}, bf16[1,2,128,1024]{3,2,1,0:T(8,128)(2,1)S(1)}, u32[]{:S(2)}, u32[]{:S(2)}) %collective-permute-start.14) | collective-permute-done | bytes 524320 | tf_op jit(solution)/shard_map/ppermute | solution.py:43
  383.2 21.0 %feedforward.2 = (bf16[4,2,128,1024]{3,2,1,0:T(8,128)(2,1)}, bf16[4,2,128,1024]{3,2,1,0:T(8,128)(2,1)}, f32[1024,1024]{1,0:T(8,128)}, f32[1024,1024]{1,0:T(8,128)}) custom-call(bf16[4,2,128,1024]{3,2,1,0:T(8,128)(2,1)} %pad_maximum_fusion.4.rows_ref, bf16[4,2,128,1024]{3,2,1,0:T(8,128)(2,1)} %pad_maximum_fusion.5.grad_ref, ...), custom_call_target="tpu_custom_call" | custom-call | flops 12884901888 | bytes 20971520 | tf_op jit(solution)/shard_map/feedforward/pallas_call | solution.py:531
  404.2 23.8 %feedforward.3 = (bf16[4,1,256,1024]{3,2,1,0:T(8,128)(2,1)}, bf16[4,1,256,1024]{3,2,1,0:T(8,128)(2,1)}, bf16[1024,1024]{1,0:T(8,128)(2,1)}, bf16[1024,1024]{1,0:T(8,128)(2,1)}) custom-call(bf16[4,1,256,1024]{3,2,1,0:T(8,128)(2,1)} %pad_maximum_fusion.8.rows_ref, bf16[4,1,256,1024]{3,2,1,0:T(8,128)(2,1)} %pad_maximum_fusion.9.grad_ref, ...), custom_call_target="tpu_custom_call" | custom-call | flops 12884901888 | bytes 20971520 | tf_op jit(solution)/shard_map/feedforward/pallas_call | solution.py:531
  437.9 10.6 %collective-permute-done.51 = bf16[1,1,256,1024]{3,2,1,0:T(8,128)(2,1)S(1)} collective-permute-done((bf16[1,1,256,1024]{3,2,1,0:T(8,128)(2,1)S(1)}, bf16[1,1,256,1024]{3,2,1,0:T(8,128)(2,1)S(1)}, u32[]{:S(2)}, u32[]{:S(2)}) %collective-permute-start.51) | collective-permute-done | bytes 524320 | tf_op jit(solution)/shard_map/ppermute | solution.py:43
  449.0 10.7 %collective-permute-done.41 = bf16[1,1,256,1024]{3,2,1,0:T(8,128)(2,1)S(1)} collective-permute-done((bf16[1,1,256,1024]{3,2,1,0:T(8,128)(2,1)S(1)}, bf16[1,1,256,1024]{3,2,1,0:T(8,128)(2,1)S(1)}, u32[]{:S(2)}, u32[]{:S(2)}) %collective-permute-start.41) | collective-permute-done | bytes 524320 | tf_op jit(solution)/shard_map/ppermute | solution.py:43
  462.7 8.1 collective-permute-done.44
  471.4 10.7 %collective-permute-done.52 = bf16[1,1,256,1024]{3,2,1,0:T(8,128)(2,1)S(1)} collective-permute-done((bf16[1,1,256,1024]{3,2,1,0:T(8,128)(2,1)S(1)}, bf16[1,1,256,1024]{3,2,1,0:T(8,128)(2,1)S(1)}, u32[]{:S(2)}, u32[]{:S(2)}) %collective-permute-start.52) | collective-permute-done | bytes 524320 | tf_op jit(solution)/shard_map/ppermute | solution.py:43
  486.7 12.9 %collective-permute-done.45 = bf16[1,2,128,1024]{3,2,1,0:T(8,128)(2,1)} collective-permute-done((bf16[1,2,128,1024]{3,2,1,0:T(8,128)(2,1)S(1)}, bf16[1,2,128,1024]{3,2,1,0:T(8,128)(2,1)}, u32[]{:S(2)}, u32[]{:S(2)}) %collective-permute-start.45) | collective-permute-done | bytes 524320 | tf_op jit(solution)/shard_map/ppermute | solution.py:43
  505.2 26.2 %attend_back.3 = (bf16[4,1,256,768]{3,2,1,0:T(8,128)(2,1)}, bf16[4,1,256,512]{3,2,1,0:T(8,128)(2,1)}, bf16[4,1,256,512]{3,2,1,0:T(8,128)(2,1)}, bf16[1,384,512]{2,1,0:T(8,128)(2,1)}) custom-call(s32[1]{0:T(128)} %bitcast.3.me_ref, s32[1]{0:T(128)} %collective-permute-done.25.offsets_ref, bf16[4,1,256,768]{3,2,1,0:T(8,128)(2,1)} %fusion.88.q_ref.kx_ref.vx_ref, ...), custom_call_target="tpu_custom_call" | custom-call | flops 18119393280 | bytes 221184 | tf_op jit(solution)/shard_map/attend_back/pallas_call | solution.py:440
  537.3 15.4 %attend_back.2 = (bf16[4,2,128,768]{3,2,1,0:T(8,128)(2,1)}, bf16[4,2,128,512]{3,2,1,0:T(8,128)(2,1)}, bf16[4,2,128,512]{3,2,1,0:T(8,128)(2,1)}, bf16[2,256,512]{2,1,0:T(8,128)(2,1)}) custom-call(s32[1]{0:T(128)} %bitcast.3.me_ref, s32[2]{0:T(128)} %copy-done.77, bf16[4,2,128,768]{3,2,1,0:T(8,128)(2,1)} %convolution_convert_fusion.4.q_ref.kx_ref.vx_ref, ...), custom_call_target="tpu_custom_call" | custom-call | flops 9395240960 | bytes 114688 | tf_op jit(solution)/shard_map/attend_back/pallas_call | solution.py:440
  572.5 4.1 multiply_reduce_fusion
  580.1 11.6 %collective-permute-done.70 = bf16[1,384,1024]{2,1,0:T(8,128)(2,1)} collective-permute-done((bf16[1,384,1024]{2,1,0:T(8,128)(2,1)}, bf16[1,384,1024]{2,1,0:T(8,128)(2,1)}, u32[]{:S(2)}, u32[]{:S(2)}) %collective-permute-start.70) | collective-permute-done | bytes 786464 | tf_op jit(solution)/shard_map/ppermute | solution.py:43
  595.3 18.7 %collective-permute-done.68 = bf16[2,256,1024]{2,1,0:T(8,128)(2,1)S(1)} collective-permute-done((bf16[2,256,1024]{2,1,0:T(8,128)(2,1)S(1)}, bf16[2,256,1024]{2,1,0:T(8,128)(2,1)S(1)}, u32[]{:S(2)}, u32[]{:S(2)}) %collective-permute-start.68) | collective-permute-done | bytes 1048608 | tf_op jit(solution)/shard_map/ppermute | solution.py:43
  629.3 10.6 %collective-permute-done.63 = bf16[128,1024]{1,0:T(8,128)(2,1)S(1)} collective-permute-done((bf16[128,1024]{1,0:T(8,128)(2,1)S(1)}, bf16[128,1024]{1,0:T(8,128)(2,1)S(1)}, u32[]{:S(2)}, u32[]{:S(2)}) %collective-permute-start.63) | collective-permute-done | bytes 262176 | tf_op jit(solution)/shard_map/ppermute | solution.py:43
  645.1 9.6 %collective-permute-done.65 = bf16[128,1024]{1,0:T(8,128)(2,1)S(1)} collective-permute-done((bf16[128,1024]{1,0:T(8,128)(2,1)S(1)}, bf16[128,1024]{1,0:T(8,128)(2,1)S(1)}, u32[]{:S(2)}, u32[]{:S(2)}) %collective-permute-start.65) | collective-permute-done | bytes 262176 | tf_op jit(solution)/shard_map/ppermute | solution.py:43
  659.7 4.1 collective-permute-start.57
  667.6 5.0 collective-permute-done.59
  674.4 3.8 convolution_convert_fusion.3
  689.6 3.7 collective-permute-start.71
  697.0 4.9 collective-permute-done.72
  704.0 5.5 collective-permute-start.42
  712.2 11.4 %collective-permute-done.22 = bf16[1,2,128,1024]{3,2,1,0:T(8,128)(2,1)} collective-permute-done((bf16[1,2,128,1024]{3,2,1,0:T(8,128)(2,1)}, bf16[1,2,128,1024]{3,2,1,0:T(8,128)(2,1)}, u32[]{:S(2)}, u32[]{:S(2)}) %collective-permute-start.22) | collective-permute-done | bytes 524320 | tf_op jit(solution)/shard_map/ppermute | solution.py:43
  728.9 5.4 collective-permute-done.55
  752.8 39.2 %all-reduce.2 = (f32[1024]{0:T(1024)}, f32[1024]{0:T(1024)}, f32[]{:T(128)}) all-reduce(f32[1024]{0:T(1024)S(1)} %div.171, f32[1024]{0:T(1024)S(1)} %add.431, f32[]{:T(128)S(6)} %add.432), channel_id=1, replica_groups=mesh['dp'=8,'tensor'=4] {'dp','tensor'}, use_global_device_ids=true, to_apply=%region_42.43 | all-reduce | flops 2049 | bytes 16392 | tf_op jit(solution)/shard_map/psum | solution.py:760
  792.6 11.5 %all_gather.36 = bf16[256,1024]{1,0:T(8,128)(2,1)S(1)} all-gather(bf16[32,1024]{1,0:T(8,128)(2,1)S(1)} %add_convert_fusion.12), channel_id=1, replica_groups=mesh['dp'=8,'tensor'=4] {'dp'}, dimensions={0}, use_global_device_ids=true | all-gather | bytes 589824 | tf_op jit(solution)/shard_map/all_gather | solution.py:113
  807.5 4.1 convert_element_type.712
  811.6 4.1 convert_element_type.716
  (503 shorter events, 281.8 us)
Async XLA Ops:
  7.2 181.0 %all-gather.9.cloned.1.call-start = ((), (), s32[]{:S(2)}) async-start(), calls=%async_computation.5 | async-start | bytes 1966080 | tf_op jit(solution)/shard_map/all_gather | solution.py:90
  24.6 186.8 %all-gather.11.cloned.1.call-start = ((), (), s32[]{:S(2)}) async-start(), calls=%async_computation.6 | async-start | bytes 1966080 | tf_op jit(solution)/shard_map/all_gather | solution.py:90
  41.8 341.4 %all-gather.13.cloned.1.call-start = ((), (), s32[]{:S(2)}) async-start(), calls=%async_computation.7 | async-start | bytes 2621440 | tf_op jit(solution)/shard_map/all_gather | solution.py:90
  41.9 26.7 %collective-permute-start.5 = (bf16[2,128,1024]{2,1,0:T(8,128)(2,1)}, bf16[2,128,1024]{2,1,0:T(8,128)(2,1)S(1)}, u32[]{:S(2)}, u32[]{:S(2)}) collective-permute-start(bf16[2,128,1024]{2,1,0:T(8,128)(2,1)} %param.21), channel_id=1, source_target_pairs={{0,0},{1,1},{2,4},{3,5},{4,2},{5,3},{6,6},{7,7},{8,8},{9,9},{10,12... | collective-permute-start | bytes 1572872 | tf_op jit(solution)/shard_map/ppermute | solution.py:43
  45.0 47.7 %collective-permute-start = (bf16[2,2,128,1024]{3,2,1,0:T(8,128)(2,1)S(1)}, bf16[2,2,128,1024]{3,2,1,0:T(8,128)(2,1)}, u32[]{:S(2)}, u32[]{:S(2)}) collective-permute-start(bf16[2,2,128,1024]{3,2,1,0:T(8,128)(2,1)S(1)} %pad_maximum_fusion.11), channel_id=1, source_target_pairs={{0,0},{1,1},{2,4},{3,5},{4,2},{5,3},{6,6},{7,7},{8,8},{9,9},{10,12... | collective-permute-start | bytes 3145736 | tf_op jit(solution)/shard_map/ppermute | solution.py:43
  71.1 51.8 %collective-permute-start.24 = (bf16[2,1,256,1024]{3,2,1,0:T(8,128)(2,1)}, bf16[2,1,256,1024]{3,2,1,0:T(8,128)(2,1)S(1)}, u32[]{:S(2)}, u32[]{:S(2)}) collective-permute-start(bf16[2,1,256,1024]{3,2,1,0:T(8,128)(2,1)} %pad_maximum_fusion.17), channel_id=1, source_target_pairs={{0,0},{1,1},{2,4},{3,5},{4,2},{5,3},{6,6},{7,7},{8,8},{9,9},{10,12... | collective-permute-start | bytes 3145736 | tf_op jit(solution)/shard_map/ppermute | solution.py:43
  76.0 37.8 %collective-permute-start.28 = (bf16[1,256,1024]{2,1,0:T(8,128)(2,1)S(1)}, bf16[1,256,1024]{2,1,0:T(8,128)(2,1)}, u32[]{:S(2)}, u32[]{:S(2)}) collective-permute-start(bf16[1,256,1024]{2,1,0:T(8,128)(2,1)S(1)} %copy-done.75), channel_id=1, source_target_pairs={{0,0},{1,1},{2,4},{3,5},{4,2},{5,3},{6,6},{7,7},{8,8},{9,9},{10,12... | collective-permute-start | bytes 1572872 | tf_op jit(solution)/shard_map/ppermute | solution.py:43
  85.3 82.3 %collective-permute-start.7 = (bf16[2,2,128,1024]{3,2,1,0:T(8,128)(2,1)}, bf16[2,2,128,1024]{3,2,1,0:T(8,128)(2,1)}, u32[]{:S(2)}, u32[]{:S(2)}) collective-permute-start(bf16[2,2,128,1024]{3,2,1,0:T(8,128)(2,1)} %pad_maximum_fusion.12), channel_id=1, source_target_pairs={{0,4},{1,5},{2,6},{3,7},{4,0},{5,1},{6,2},{7,3},{8,12},{9,13},{10,... | collective-permute-start | bytes 3145736 | tf_op jit(solution)/shard_map/ppermute | solution.py:43
  92.7 78.5 %collective-permute-start.2 = (bf16[1,2,2,128,1024]{4,3,2,1,0:T(8,128)(2,1)}, bf16[1,2,2,128,1024]{4,3,2,1,0:T(8,128)(2,1)}, u32[]{:S(2)}, u32[]{:S(2)}) collective-permute-start(bf16[1,2,2,128,1024]{4,3,2,1,0:T(8,128)(2,1)} %bitcast.4), channel_id=1, source_target_pairs={{0,1},{1,0},{2,3},{3,2},{4,5},{5,4},{6,7},{7,6},{8,9},{9,8},{10,11... | collective-permute-start | bytes 3145736 | tf_op jit(solution)/shard_map/ppermute | solution.py:43
  113.8 34.5 %collective-permute-start.29 = (bf16[1,1,256,1024]{3,2,0,1:T(8,128)(2,1)}, bf16[1,1,256,1024]{3,2,0,1:T(8,128)(2,1)}, u32[]{:S(2)}, u32[]{:S(2)}) collective-permute-start(bf16[1,1,256,1024]{3,2,0,1:T(8,128)(2,1)} %bitcast.37), channel_id=1, source_target_pairs={{0,1},{1,0},{2,3},{3,2},{4,5},{5,4},{6,7},{7,6},{8,9},{9,8},{10,11... | collective-permute-start | bytes 1572872 | tf_op jit(solution)/shard_map/ppermute | solution.py:43
  114.6 45.7 %collective-permute-start.19 = (bf16[256,1024]{1,0:T(8,128)(2,1)}, bf16[256,1024]{1,0:T(8,128)(2,1)}, u32[]{:S(2)}, u32[]{:S(2)}) collective-permute-start(bf16[256,1024]{1,0:T(8,128)(2,1)} %constant_dynamic-slice_fusion.15), channel_id=1, source_target_pairs={{0,0},{1,1},{2,4},{3,5},{4,2},{5,3},{6,6},{7,7},{8,8},{9,9},{10,12... | collective-permute-start | bytes 1572872 | tf_op jit(solution)/shard_map/ppermute | solution.py:43
  122.8 27.7 %collective-permute-start.11 = (bf16[64,1024]{1,0:T(8,128)(2,1)S(1)}, bf16[64,1024]{1,0:T(8,128)(2,1)S(1)}, u32[]{:S(2)}, u32[]{:S(2)}) collective-permute-start(bf16[64,1024]{1,0:T(8,128)(2,1)S(1)} %constant_dynamic-slice_fusion.16), channel_id=1, source_target_pairs={{0,0},{1,1},{2,4},{3,5},{4,2},{5,3},{6,6},{7,7},{8,8},{9,9},{10,12... | collective-permute-start | bytes 393224 | tf_op jit(solution)/shard_map/ppermute | solution.py:43
  148.3 32.6 %collective-permute-start.26 = (bf16[1,2,1,256,1024]{4,3,1,2,0:T(8,128)(2,1)S(1)}, bf16[1,2,1,256,1024]{4,3,1,2,0:T(8,128)(2,1)}, u32[]{:S(2)}, u32[]{:S(2)}) collective-permute-start(bf16[1,2,1,256,1024]{4,3,1,2,0:T(8,128)(2,1)S(1)} %bitcast.398), channel_id=1, source_target_pairs={{0,1},{1,0},{2,3},{3,2},{4,5},{5,4},{6,7},{7,6},{8,9},{9,8},{10,11... | collective-permute-start | bytes 3145736 | tf_op jit(solution)/shard_map/ppermute | solution.py:43
  150.6 33.2 %collective-permute-start.30 = (bf16[2,1,256,1024]{3,2,0,1:T(8,128)(2,1)}, bf16[2,1,256,1024]{3,2,0,1:T(8,128)(2,1)S(1)}, u32[]{:S(2)}, u32[]{:S(2)}) collective-permute-start(bf16[2,1,256,1024]{3,2,0,1:T(8,128)(2,1)} %pad_maximum_fusion.18), channel_id=1, source_target_pairs={{0,4},{1,5},{2,6},{3,7},{4,0},{5,1},{6,2},{7,3},{8,12},{9,13},{10,... | collective-permute-start | bytes 3145736 | tf_op jit(solution)/shard_map/ppermute | solution.py:43
  160.4 126.8 %collective-permute-start.1 = (s32[2]{0:T(128)S(1)}, s32[2]{0:T(128)S(1)}, u32[]{:S(2)}, u32[]{:S(2)}) collective-permute-start(s32[2]{0:T(128)S(1)} %copy-done.76), channel_id=1, source_target_pairs={{0,0},{1,1},{2,4},{3,5},{4,2},{5,3},{6,6},{7,7},{8,8},{9,9},{10,12... | collective-permute-start | bytes 32 | tf_op jit(solution)/shard_map/ppermute | solution.py:43
  167.6 215.6 %all-gather.15.cloned.1.call-start = ((), (), s32[]{:S(2)}) async-start(), calls=%async_computation.8 | async-start | bytes 2621440 | tf_op jit(solution)/shard_map/all_gather | solution.py:90
  167.7 136.1 %collective-permute-start.16 = (bf16[2,128,1024]{2,1,0:T(8,128)(2,1)}, bf16[2,128,1024]{2,1,0:T(8,128)(2,1)}, u32[]{:S(2)}, u32[]{:S(2)}) collective-permute-start(bf16[2,128,1024]{2,1,0:T(8,128)(2,1)} %param.36), channel_id=1, source_target_pairs={{0,0},{1,1},{2,4},{3,5},{4,2},{5,3},{6,6},{7,7},{8,8},{9,9},{10,12... | collective-permute-start | bytes 1572872 | tf_op jit(solution)/shard_map/ppermute | solution.py:43
  171.2 134.0 %collective-permute-start.20 = (bf16[256,1024]{1,0:T(8,128)(2,1)}, bf16[256,1024]{1,0:T(8,128)(2,1)}, u32[]{:S(2)}, u32[]{:S(2)}) collective-permute-start(bf16[256,1024]{1,0:T(8,128)(2,1)} %constant_dynamic-slice_fusion.14), channel_id=1, source_target_pairs={{0,0},{1,1},{2,4},{3,5},{4,2},{5,3},{6,6},{7,7},{8,8},{9,9},{10,12... | collective-permute-start | bytes 1572872 | tf_op jit(solution)/shard_map/ppermute | solution.py:43
  214.9 25.0 %collective-permute-start.9 = (bf16[1,2,256,256]{2,3,1,0:T(8,128)(2,1)S(1)}, bf16[1,2,256,256]{2,3,1,0:T(8,128)(2,1)S(1)}, u32[]{:S(2)}, u32[]{:S(2)}) collective-permute-start(bf16[1,2,256,256]{2,3,1,0:T(8,128)(2,1)S(1)} %bitcast.438), channel_id=1, source_target_pairs={{0,1},{1,0},{2,3},{3,2},{4,5},{5,4},{6,7},{7,6},{8,9},{9,8},{10,11... | collective-permute-start | bytes 786440 | tf_op jit(solution)/shard_map/ppermute | solution.py:43
  244.4 59.6 %collective-permute-start.37 = (bf16[1,256,1024]{2,1,0:T(8,128)(2,1)}, bf16[1,256,1024]{2,1,0:T(8,128)(2,1)}, u32[]{:S(2)}, u32[]{:S(2)}) collective-permute-start(bf16[1,256,1024]{2,1,0:T(8,128)(2,1)} %param.37), channel_id=1, source_target_pairs={{0,0},{1,1},{2,4},{3,5},{4,2},{5,3},{6,6},{7,7},{8,8},{9,9},{10,12... | collective-permute-start | bytes 1572872 | tf_op jit(solution)/shard_map/ppermute | solution.py:43
  252.4 24.9 %collective-permute-start.10 = (bf16[2,2,256,256]{2,3,1,0:T(8,128)(2,1)}, bf16[2,2,256,256]{2,3,1,0:T(8,128)(2,1)}, u32[]{:S(2)}, u32[]{:S(2)}) collective-permute-start(bf16[2,2,256,256]{2,3,1,0:T(8,128)(2,1)} %pad_maximum_fusion.27), channel_id=1, source_target_pairs={{0,4},{1,5},{2,6},{3,7},{4,0},{5,1},{6,2},{7,3},{8,12},{9,13},{10,... | collective-permute-start | bytes 1572872 | tf_op jit(solution)/shard_map/ppermute | solution.py:43
  277.4 29.5 %collective-permute-start.33 = (bf16[2,1,256,1024]{3,2,1,0:T(8,128)(2,1)}, bf16[2,1,256,1024]{3,2,1,0:T(8,128)(2,1)}, u32[]{:S(2)}, u32[]{:S(2)}) collective-permute-start(bf16[2,1,256,1024]{3,2,1,0:T(8,128)(2,1)} %slice_bitcast_fusion.5), channel_id=1, source_target_pairs={{0,4},{1,5},{2,6},{3,7},{4,0},{5,1},{6,2},{7,3},{8,12},{9,13},{10,... | collective-permute-start | bytes 3145736 | tf_op jit(solution)/shard_map/ppermute | solution.py:43
  303.8 50.9 %collective-permute-start.17 = (bf16[1,2,128,1024]{3,2,1,0:T(8,128)(2,1)}, bf16[1,2,128,1024]{3,2,1,0:T(8,128)(2,1)}, u32[]{:S(2)}, u32[]{:S(2)}) collective-permute-start(bf16[1,2,128,1024]{3,2,1,0:T(8,128)(2,1)} %bitcast.24), channel_id=1, source_target_pairs={{0,1},{1,0},{2,3},{3,2},{4,5},{5,4},{6,7},{7,6},{8,9},{9,8},{10,11... | collective-permute-start | bytes 1572872 | tf_op jit(solution)/shard_map/ppermute | solution.py:43
  304.1 53.5 %collective-permute-start.38 = (bf16[1,1,256,1024]{3,2,1,0:T(8,128)(2,1)}, bf16[1,1,256,1024]{3,2,1,0:T(8,128)(2,1)}, u32[]{:S(2)}, u32[]{:S(2)}) collective-permute-start(bf16[1,1,256,1024]{3,2,1,0:T(8,128)(2,1)} %bitcast.59), channel_id=1, source_target_pairs={{0,1},{1,0},{2,3},{3,2},{4,5},{5,4},{6,7},{7,6},{8,9},{9,8},{10,11... | collective-permute-start | bytes 1572872 | tf_op jit(solution)/shard_map/ppermute | solution.py:43
  305.3 317.6 %reduce-scatter.10.cloned.1.call-start = ((), (), s32[]{:S(2)}) async-start(), calls=%async_computation.12 | async-start | bytes 2621440 | tf_op jit(solution)/shard_map/reduce_scatter | solution.py:95
  308.8 31.2 %collective-permute-start.34 = (bf16[1,1,256,1024]{3,2,1,0:T(8,128)(2,1)S(1)}, bf16[1,1,256,1024]{3,2,1,0:T(8,128)(2,1)S(1)}, u32[]{:S(2)}, u32[]{:S(2)}) collective-permute-start(bf16[1,1,256,1024]{3,2,1,0:T(8,128)(2,1)S(1)} %slice.206), channel_id=1, source_target_pairs={{0,1},{1,0},{2,3},{3,2},{4,5},{5,4},{6,7},{7,6},{8,9},{9,8},{10,11... | collective-permute-start | bytes 1572872 | tf_op jit(solution)/shard_map/ppermute | solution.py:43
  310.9 40.4 %collective-permute-start.13 = (bf16[1,2,128,1024]{3,2,1,0:T(8,128)(2,1)S(1)}, bf16[1,2,128,1024]{3,2,1,0:T(8,128)(2,1)S(1)}, u32[]{:S(2)}, u32[]{:S(2)}) collective-permute-start(bf16[1,2,128,1024]{3,2,1,0:T(8,128)(2,1)S(1)} %slice.197), channel_id=1, source_target_pairs={{0,1},{1,0},{2,3},{3,2},{4,5},{5,4},{6,7},{7,6},{8,9},{9,8},{10,11... | collective-permute-start | bytes 1572872 | tf_op jit(solution)/shard_map/ppermute | solution.py:43
  430.3 210.3 %reduce-scatter.12.cloned.1.call-start = ((), (), s32[]{:S(2)}) async-start(), calls=%async_computation.14 | async-start | bytes 2621440 | tf_op jit(solution)/shard_map/reduce_scatter | solution.py:95
  437.5 33.3 %collective-permute-start.44 = (bf16[1,2,128,1024]{3,2,1,0:T(8,128)(2,1)S(1)}, bf16[1,2,128,1024]{3,2,1,0:T(8,128)(2,1)S(1)}, u32[]{:S(2)}, u32[]{:S(2)}) collective-permute-start(bf16[1,2,128,1024]{3,2,1,0:T(8,128)(2,1)S(1)} %slice.210), channel_id=1, source_target_pairs={{0,1},{1,0},{2,3},{3,2},{4,5},{5,4},{6,7},{7,6},{8,9},{9,8},{10,11... | collective-permute-start | bytes 1572872 | tf_op jit(solution)/shard_map/ppermute | solution.py:43
  486.2 169.4 %reduce-scatter.6.cloned.1.call-start = ((), (), s32[]{:S(2)}) async-start(), calls=%async_computation.9 | async-start | bytes 1966080 | tf_op jit(solution)/shard_map/reduce_scatter | solution.py:95
  501.6 32.7 %collective-permute-start.46 = (bf16[2,2,128,1024]{3,2,1,0:T(8,128)(2,1)}, bf16[2,2,128,1024]{3,2,1,0:T(8,128)(2,1)}, u32[]{:S(2)}, u32[]{:S(2)}) collective-permute-start(bf16[2,2,128,1024]{3,2,1,0:T(8,128)(2,1)} %pad_maximum_fusion.21), channel_id=1, source_target_pairs={{0,4},{1,5},{2,6},{3,7},{4,0},{5,1},{6,2},{7,3},{8,12},{9,13},{10,... | collective-permute-start | bytes 3145736 | tf_op jit(solution)/shard_map/ppermute | solution.py:43
  534.3 35.2 %collective-permute-start.69 = (bf16[1,384,1024]{2,1,0:T(8,128)(2,1)}, bf16[1,384,1024]{2,1,0:T(8,128)(2,1)}, u32[]{:S(2)}, u32[]{:S(2)}) collective-permute-start(bf16[1,384,1024]{2,1,0:T(8,128)(2,1)} %fusion.113), channel_id=1, source_target_pairs={{0,4},{1,5},{2,6},{3,7},{4,0},{5,1},{6,2},{7,3},{8,12},{9,13},{10,... | collective-permute-start | bytes 2359304 | tf_op jit(solution)/shard_map/ppermute | solution.py:43
  576.6 111.8 %reduce-scatter.14.cloned.1.call-start = ((), (), s32[]{:S(2)}) async-start(), calls=%async_computation.16 | async-start | bytes 1966080 | tf_op jit(solution)/shard_map/reduce_scatter | solution.py:95
  578.8 35.2 %collective-permute-start.68 = (bf16[2,256,1024]{2,1,0:T(8,128)(2,1)S(1)}, bf16[2,256,1024]{2,1,0:T(8,128)(2,1)S(1)}, u32[]{:S(2)}, u32[]{:S(2)}) collective-permute-start(bf16[2,256,1024]{2,1,0:T(8,128)(2,1)S(1)} %add_convert_fusion), channel_id=1, source_target_pairs={{0,1},{1,0},{2,3},{3,2},{4,5},{5,4},{6,7},{7,6},{8,9},{9,8},{10,11... | collective-permute-start | bytes 3145736 | tf_op jit(solution)/shard_map/ppermute | solution.py:43
  617.4 125.3 %reduce-scatter.8.cloned.1.call-start = ((), (), s32[]{:S(2)}) async-start(), calls=%async_computation.11 | async-start | bytes 655360 | tf_op jit(solution)/shard_map/reduce_scatter | solution.py:95
  622.7 184.8 %all-gather.19.cloned.1.call-start = ((), (), s32[]{:S(2)}) async-start(), calls=%async_computation.13 | async-start | bytes 2359296 | tf_op jit(solution)/shard_map/all_gather | solution.py:113
  640.6 171.0 %all-gather.21.cloned.1.call-start = ((), (), s32[]{:S(2)}) async-start(), calls=%async_computation.15 | async-start | bytes 2359296 | tf_op jit(solution)/shard_map/all_gather | solution.py:113
  655.5 160.2 %all-gather.17.cloned.1.call-start = ((), (), s32[]{:S(2)}) async-start(), calls=%async_computation.10 | async-start | bytes 1769472 | tf_op jit(solution)/shard_map/all_gather | solution.py:113
  659.7 83.8 %collective-permute-start.57 = (bf16[2,256,256]{1,2,0:T(8,128)(2,1)S(1)}, bf16[2,256,256]{1,2,0:T(8,128)(2,1)}, u32[]{:S(2)}, u32[]{:S(2)}) collective-permute-start(bf16[2,256,256]{1,2,0:T(8,128)(2,1)S(1)} %copy-done.51), channel_id=1, source_target_pairs={{0,0},{1,1},{2,4},{3,5},{4,2},{5,3},{6,6},{7,7},{8,8},{9,9},{10,12... | collective-permute-start | bytes 786440 | tf_op jit(solution)/shard_map/ppermute | solution.py:43
  663.9 75.4 %collective-permute-start.58 = (bf16[1,384,256]{1,2,0:T(8,128)(2,1)}, bf16[1,384,256]{1,2,0:T(8,128)(2,1)}, u32[]{:S(2)}, u32[]{:S(2)}) collective-permute-start(bf16[1,384,256]{1,2,0:T(8,128)(2,1)} %bitcast.75), channel_id=1, source_target_pairs={{0,0},{1,1},{2,4},{3,5},{4,2},{5,3},{6,6},{7,7},{8,8},{9,9},{10,12... | collective-permute-start | bytes 589832 | tf_op jit(solution)/shard_map/ppermute | solution.py:43
  674.4 144.4 %all-gather.23.cloned.1.call-start = ((), (), s32[]{:S(2)}) async-start(), calls=%async_computation.17 | async-start | bytes 1769472 | tf_op jit(solution)/shard_map/all_gather | solution.py:113
  704.0 39.6 %collective-permute-start.42 = (bf16[1,256,1024]{2,1,0:T(8,128)(2,1)}, bf16[1,256,1024]{2,1,0:T(8,128)(2,1)}, u32[]{:S(2)}, u32[]{:S(2)}) collective-permute-start(bf16[1,256,1024]{2,1,0:T(8,128)(2,1)} %get-tuple-element.136), channel_id=1, source_target_pairs={{0,0},{1,1},{2,4},{3,5},{4,2},{5,3},{6,6},{7,7},{8,8},{9,9},{10,12... | collective-permute-start | bytes 1572872 | tf_op jit(solution)/shard_map/ppermute | solution.py:43
  710.3 24.1 %collective-permute-start.55 = (bf16[1,1,256,1024]{3,2,1,0:T(8,128)(2,1)}, bf16[1,1,256,1024]{3,2,1,0:T(8,128)(2,1)S(1)}, u32[]{:S(2)}, u32[]{:S(2)}) collective-permute-start(bf16[1,1,256,1024]{3,2,1,0:T(8,128)(2,1)} %slice.220), channel_id=1, source_target_pairs={{0,1},{1,0},{2,3},{3,2},{4,5},{5,4},{6,7},{7,6},{8,9},{9,8},{10,11... | collective-permute-start | bytes 1572872 | tf_op jit(solution)/shard_map/ppermute | solution.py:43
  726.9 78.4 %collective-permute-start.23 = (bf16[2,128,1024]{2,1,0:T(8,128)(2,1)}, bf16[2,128,1024]{2,1,0:T(8,128)(2,1)S(1)}, u32[]{:S(2)}, u32[]{:S(2)}) collective-permute-start(bf16[2,128,1024]{2,1,0:T(8,128)(2,1)} %get-tuple-element.138), channel_id=1, source_target_pairs={{0,0},{1,1},{2,4},{3,5},{4,2},{5,3},{6,6},{7,7},{8,8},{9,9},{10,12... | collective-permute-start | bytes 1572872 | tf_op jit(solution)/shard_map/ppermute | solution.py:43
  734.4 70.9 %collective-permute-start.49 = (bf16[2,128,1024]{2,1,0:T(8,128)(2,1)}, bf16[2,128,1024]{2,1,0:T(8,128)(2,1)S(1)}, u32[]{:S(2)}, u32[]{:S(2)}) collective-permute-start(bf16[2,128,1024]{2,1,0:T(8,128)(2,1)} %get-tuple-element.137), channel_id=1, source_target_pairs={{0,0},{1,1},{2,4},{3,5},{4,2},{5,3},{6,6},{7,7},{8,8},{9,9},{10,12... | collective-permute-start | bytes 1572872 | tf_op jit(solution)/shard_map/ppermute | solution.py:43
  739.3 67.1 %collective-permute-start.56 = (bf16[1,256,1024]{2,1,0:T(8,128)(2,1)}, bf16[1,256,1024]{2,1,0:T(8,128)(2,1)S(1)}, u32[]{:S(2)}, u32[]{:S(2)}) collective-permute-start(bf16[1,256,1024]{2,1,0:T(8,128)(2,1)} %fusion.140), channel_id=1, source_target_pairs={{0,0},{1,1},{2,4},{3,5},{4,2},{5,3},{6,6},{7,7},{8,8},{9,9},{10,12... | collective-permute-start | bytes 1572872 | tf_op jit(solution)/shard_map/ppermute | solution.py:43
  743.6 49.0 %collective-permute-start.62 = (bf16[32,1024]{1,0:T(8,128)(2,1)S(1)}, bf16[32,1024]{1,0:T(8,128)(2,1)S(1)}, u32[]{:S(2)}, u32[]{:S(2)}) collective-permute-start(bf16[32,1024]{1,0:T(8,128)(2,1)S(1)} %get-tuple-element.158), channel_id=1, source_target_pairs={{0,4},{1,5},{2,0},{3,1},{4,6},{5,7},{6,2},{7,3},{8,12},{9,13},{10,... | collective-permute-start | bytes 196616 | tf_op jit(solution)/shard_map/ppermute | solution.py:43
  743.7 49.0 %collective-permute-start.61 = (bf16[32,1024]{1,0:T(8,128)(2,1)S(1)}, bf16[32,1024]{1,0:T(8,128)(2,1)S(1)}, u32[]{:S(2)}, u32[]{:S(2)}) collective-permute-start(bf16[32,1024]{1,0:T(8,128)(2,1)S(1)} %get-tuple-element.157), channel_id=1, source_target_pairs={{0,0},{1,1},{2,4},{3,5},{4,2},{5,3},{6,6},{7,7},{8,8},{9,9},{10,12... | collective-permute-start | bytes 196616 | tf_op jit(solution)/shard_map/ppermute | solution.py:43
  (123 other events, 1546.4 us)
Sparse Core Ops, SparseCore 0:
  24.7 31.8 all-gather.8
  59.1 30.9 all-gather.10
  167.7 32.0 all-gather.12
  305.4 34.4 all-gather.14
  430.5 33.7 reduce-scatter.9
  486.3 34.4 reduce-scatter.11
  576.7 30.2 reduce-scatter.5
  617.5 29.8 reduce-scatter.13
  650.8 24.6 reduce-scatter.7
  677.4 28.4 all-gather.18
  707.9 27.8 all-gather.20
  737.7 26.2 all-gather.16
  766.6 26.2 all-gather.22

commit v3 on v2

--- a/solution.py
+++ b/solution.py
@@ -68,11 +68,12 @@
         return value[0]
 
     def total(self, value):
-        bit = self.half
-        while bit:
-            value = value.astype(jnp.bfloat16)
-            value = value.astype(jnp.float32) + self.flip(value, bit).astype(jnp.float32)
-            bit //= 2
+        for axis, extent in zip(AXES, (self.dp, self.tensor)):
+            bit = 1
+            while bit < extent:
+                pairs = [(i, i ^ bit) for i in range(extent)]
+                value = value + lax.ppermute(value, axis, pairs)
+                bit *= 2
         return value
 
     def ordered(self, pieces, axis):
@@ -110,7 +111,15 @@
         )
         own = self.permute(eighth(self.upper), lambda p, c, h, a: (p, h, c, a))
         summed = (own.astype(jnp.float32) + other.astype(jnp.float32)).astype(jnp.bfloat16)
-        return lax.all_gather(summed, "dp", axis=0, tiled=True).astype(jnp.float32)
+        mine = lax.all_gather(summed, "dp", axis_index_groups=self.groups)
+        other = self.flip(mine, self.half)
+        first = jnp.where(self.core == 0, mine, other)
+        second = jnp.where(self.core == 0, other, mine)
+        return jnp.stack([first, second], 1).reshape(value.shape).astype(jnp.float32)
+
+
+def after(value, *done):
+    return lax.optimization_barrier((value, done))[0]
 
 
 def normalize(rows):
@@ -192,12 +201,14 @@
     ka_ref,
     va_ref,
     o_ref,
-    push_ref,
     lse_ref,
-    alse_ref,
+    da_ref,
     square_ref,
+    ka_acc,
+    va_acc,
 ):
     seq, head, block = pl.program_id(0), pl.program_id(1), pl.program_id(2)
+    heads = da_ref.shape[2] // (2 * HEAD_SIZE)
     pieces, _, rows, _ = q_ref.shape
     length, tile = pieces * rows, many * rows
     tiles = Tiles(me_ref[0], pieces, rows, many)
@@ -249,7 +260,7 @@
         empty(), jnp.where(place < reduced, scores, masked_value), va_ref[0]
     )
     differ = memory[2] / memory[1] - aacc / atotal
-    tiles.store(push_ref, block, (-2.0 * rebuild_weight * differ).astype(jnp.bfloat16), 0)
+    push = (-2.0 * rebuild_weight * differ).astype(jnp.bfloat16)
 
     @pl.when((seq == 0) & (head == 0) & (block == 0))
     def _():
@@ -261,20 +272,35 @@
         return jnp.transpose(jnp.broadcast_to(column, (tile, HEAD_SIZE)))[:1]
 
     lse_ref[0] = row(top + jnp.log(total))
-    alse_ref[0] = row(atop + jnp.log(atotal))
-
-
-def attention_specs(pieces, rows, heads, padded, tile):
+
+    @pl.when(block == 0)
+    def _():
+        ka_acc[...] = jnp.zeros_like(ka_acc)
+        va_acc[...] = jnp.zeros_like(va_acc)
+
+    place = lax.broadcasted_iota(jnp.int32, (ka_ref.shape[1], 1), 0)
+    scores = jnp.where(place < reduced, dot(ka_ref[0], q, NT) * SCALE, masked_value)
+    probs = jnp.exp(scores - row(atop + jnp.log(atotal)))
+    va_acc[...] += dot(probs.astype(jnp.bfloat16), push)
+    dp = dot(va_ref[0], push, NT)
+    shift = jnp.sum(probs * dp, 0, keepdims=True)
+    ka_acc[...] += dot((probs * (dp - shift)).astype(jnp.bfloat16), q)
+
+    @pl.when(block == pl.num_programs(2) - 1)
+    def _():
+        for kind, value in ((0, ka_acc[...] * SCALE), (1, va_acc[...])):
+            start = pl.multiple_of((kind * heads + head) * HEAD_SIZE, HEAD_SIZE)
+            da_ref[0, :, pl.ds(start, HEAD_SIZE)] = value.astype(jnp.bfloat16)
+
+
+def attention_specs(pieces, rows, heads, tile):
     def whole(shift):
         return pl.BlockSpec(
             (pieces, 1, rows, HEAD_SIZE), lambda s, h, b, *_: (0, s, 0, h + shift * heads)
         )
 
-    def added(shift):
-        return pl.BlockSpec((1, padded, HEAD_SIZE), lambda s, h, b, *_: (s, 0, h + shift * heads))
-
     stat = pl.BlockSpec((1, 1, tile), lambda s, h, b, *_: (s * heads + h, 0, b))
-    keys = [whole(0), whole(1), whole(2)] + [whole(0), whole(1)] * 2 + [added(0), added(1)]
+    keys = [whole(0), whole(1), whole(2)] + [whole(0), whole(1)] * 2
     return whole, stat, keys
 
 
@@ -287,7 +313,11 @@
     heads = memory.shape[-1] // (2 * HEAD_SIZE)
     padded, length = added.shape[1], pieces * rows
     many = tile_pieces(pieces, rows)
-    whole, stat, keys = attention_specs(pieces, rows, heads, padded, many * rows)
+    whole, stat, keys = attention_specs(pieces, rows, heads, many * rows)
+    for shift in (0, heads):
+        keys.append(
+            pl.BlockSpec((1, padded, HEAD_SIZE), lambda s, h, b, *_, shift=shift: (s, 0, h + shift))
+        )
     tokens = jax.ShapeDtypeStruct((pieces, count, rows, heads * HEAD_SIZE), jnp.bfloat16)
     stats = jax.ShapeDtypeStruct((count * heads, 1, length), jnp.float32)
     work = count * heads * length * (3 * length + padded)
@@ -299,13 +329,18 @@
             in_specs=keys,
             out_specs=[
                 whole(0),
-                whole(0),
                 stat,
-                stat,
+                pl.BlockSpec((1, *added.shape[1:]), lambda s, h, b, *_: (s, 0, 0)),
                 pl.BlockSpec((8, HEAD_SIZE), lambda *_: (0, 0)),
             ],
+            scratch_shapes=[pltpu.VMEM((padded, HEAD_SIZE), jnp.float32)] * 2,
         ),
-        out_shape=[tokens, tokens, stats, stats, jax.ShapeDtypeStruct((8, HEAD_SIZE), jnp.float32)],
+        out_shape=[
+            tokens,
+            stats,
+            jax.ShapeDtypeStruct(added.shape, jnp.bfloat16),
+            jax.ShapeDtypeStruct((8, HEAD_SIZE), jnp.float32),
+        ],
         cost_estimate=pl.CostEstimate(
             flops=work * 4 * HEAD_SIZE * 2, bytes_accessed=work // 64, transcendentals=work
         ),
@@ -314,7 +349,6 @@
 
 
 def attend_back_kernel(
-    reduced,
     many,
     heads,
     me_ref,
@@ -326,25 +360,18 @@
     vm_ref,
     kc_ref,
     vc_ref,
-    ka_ref,
-    va_ref,
     o_ref,
     do_ref,
-    push_ref,
     lse_ref,
-    alse_ref,
     dx_ref,
     dm_ref,
     dc_ref,
-    da_ref,
     kx_acc,
     vx_acc,
     km_acc,
     vm_acc,
     kc_acc,
     vc_acc,
-    ka_acc,
-    va_acc,
 ):
     seq, head, block = pl.program_id(0), pl.program_id(1), pl.program_id(2)
     pieces, _, rows, _ = q_ref.shape
@@ -355,7 +382,7 @@
 
     @pl.when(block == 0)
     def _():
-        for ref in (kx_acc, vx_acc, km_acc, vm_acc, kc_acc, vc_acc, ka_acc, va_acc):
+        for ref in (kx_acc, vx_acc, km_acc, vm_acc, kc_acc, vc_acc):
             ref[...] = jnp.zeros_like(ref)
 
     lse = lse_ref[0]
@@ -400,15 +427,6 @@
 
     tiles.store(dx_ref, block, (dq * SCALE).astype(jnp.bfloat16), 0, slice(None), columns(0))
 
-    push = tiles.load(push_ref, block, 0)
-    place = lax.broadcasted_iota(jnp.int32, (ka_ref.shape[1], 1), 0)
-    scores = jnp.where(place < reduced, dot(ka_ref[0], q, NT) * SCALE, masked_value)
-    probs = jnp.exp(scores - alse_ref[0])
-    va_acc[...] += dot(probs.astype(jnp.bfloat16), push)
-    dp = dot(va_ref[0], push, NT)
-    shift = jnp.sum(probs * dp, 0, keepdims=True)
-    ka_acc[...] += dot((probs * (dp - shift)).astype(jnp.bfloat16), q)
-
     @pl.when(block == pl.num_programs(2) - 1)
     def _():
         dx_ref[:, 0, :, columns(1)] = (kx_acc[...] * SCALE).astype(jnp.bfloat16)
@@ -417,35 +435,28 @@
         dm_ref[:, 0, :, columns(1)] = vm_acc[...].astype(jnp.bfloat16)
         dc_ref[:, 0, :, columns(0)] = (kc_acc[...] * SCALE).astype(jnp.bfloat16)
         dc_ref[:, 0, :, columns(1)] = vc_acc[...].astype(jnp.bfloat16)
-        da_ref[0, :, columns(0)] = (ka_acc[...] * SCALE).astype(jnp.bfloat16)
-        da_ref[0, :, columns(1)] = va_acc[...].astype(jnp.bfloat16)
-
-
-def attend_back(
-    me, offsets, triples, memory, older, added, out, grad, push, lse, alse, reduced
-):
+
+
+def attend_back(me, offsets, triples, memory, older, out, grad, lse):
     pieces, count, rows, _ = triples.shape
     heads = memory.shape[-1] // (2 * HEAD_SIZE)
-    padded, length = added.shape[1], pieces * rows
+    length = pieces * rows
     many = tile_pieces(pieces, rows)
-    whole, stat, keys = attention_specs(pieces, rows, heads, padded, many * rows)
+    whole, stat, keys = attention_specs(pieces, rows, heads, many * rows)
 
     def result(like):
-        if like.ndim == 3:
-            return pl.BlockSpec((1, *like.shape[1:]), lambda s, h, b, *_: (s, 0, 0))
         return pl.BlockSpec((pieces, 1, rows, like.shape[-1]), lambda s, h, b, *_: (0, s, 0, 0))
 
-    outputs = [triples, memory, older, added]
-    work = count * heads * length * (3 * length + padded)
+    outputs = [triples, memory, older]
+    work = count * heads * length * 3 * length
     return pl.pallas_call(
-        functools.partial(attend_back_kernel, reduced, many, heads),
+        functools.partial(attend_back_kernel, many, heads),
         grid_spec=pltpu.PrefetchScalarGridSpec(
             num_scalar_prefetch=2,
             grid=(count, heads, pieces // many),
-            in_specs=keys + [whole(0)] * 3 + [stat, stat],
+            in_specs=keys + [whole(0), whole(0), stat],
             out_specs=[result(like) for like in outputs],
-            scratch_shapes=[pltpu.VMEM((pieces, rows, HEAD_SIZE), jnp.float32)] * 6
-            + [pltpu.VMEM((padded, HEAD_SIZE), jnp.float32)] * 2,
+            scratch_shapes=[pltpu.VMEM((pieces, rows, HEAD_SIZE), jnp.float32)] * 6,
         ),
         out_shape=[jax.ShapeDtypeStruct(like.shape, jnp.bfloat16) for like in outputs],
         cost_estimate=pl.CostEstimate(
@@ -462,13 +473,9 @@
         memory,
         older,
         older,
-        added,
-        added,
         out,
         grad,
-        push,
         lse,
-        alse,
     )
 
 
@@ -589,25 +596,201 @@
     )(me, memory)
 
 
+def fetch_kernel(dp, tensor, activations, weights, *refs):
+    half, columns = tensor // 2, dp // 2
+    count = len(activations) + len(weights)
+    inputs, outputs = refs[:count], refs[count : 2 * count]
+    staged, (send, recv, stage_sem) = refs[2 * count : -3], refs[-3:]
+    place, plane = lax.axis_index("dp"), lax.axis_index("tensor")
+    core, column = place % 2, place // 2
+    upper, lower = plane // half, plane % half
+    stays = core == upper
+
+    def other(column, core, upper, lower):
+        return (2 * column + core, upper * half + lower)
+
+    swapped = other(column, upper, core, lower)
+    row_bits = [1 << i for i in range(half.bit_length() - 1)] + [half]
+    column_bits = [1 << i for i in range(columns.bit_length() - 1)]
+
+    def row_partner(bit):
+        if bit == half:
+            return other(column, 1 - core, upper, lower)
+        return other(column, core, upper, lower ^ bit)
+
+    def column_partner(bit):
+        return other(column ^ bit, core, upper, lower)
+
+    partners = [row_partner(bit) for bit in row_bits] + [column_partner(b) for b in column_bits]
+
+    loads = []
+    for i in range(len(weights)):
+        source = inputs[len(activations) + i]
+        rows = staged[i].shape[0]
+        load = pltpu.make_async_copy(
+            source.at[pl.ds(pl.multiple_of(column * rows, rows), rows)], staged[i], stage_sem.at[i]
+        )
+        load.start()
+        loads.append(load)
+
+    barrier = pltpu.get_barrier_semaphore()
+    for partner in partners:
+        pl.semaphore_signal(barrier, 1, device_id=partner, device_id_type=pl.DeviceIdType.MESH)
+
+    @pl.when(stays)
+    def _():
+        pl.semaphore_wait(barrier, len(partners))
+
+    @pl.when(jnp.logical_not(stays))
+    def _():
+        pl.semaphore_signal(barrier, 1, device_id=swapped, device_id_type=pl.DeviceIdType.MESH)
+        pl.semaphore_wait(barrier, len(partners) + 1)
+
+    for load in loads:
+        load.wait()
+
+    transfers = []
+    for item in range(count):
+        if item < len(activations):
+            source, where, bits, partner = inputs[item], 0, row_bits, row_partner
+        else:
+            source, where = staged[item - len(activations)], column
+            bits, partner = column_bits, column_partner
+        transfers.append((item, source, where, bits, partner))
+    ranks = activations + weights
+    order = sorted(range(count), key=lambda item: ranks[item])
+
+    def keep(item):
+        _, source, where, _, _ = transfers[item]
+        return pltpu.make_async_copy(source, outputs[item].at[where], recv.at[item, 0])
+
+    def swap(item):
+        _, source, where, _, _ = transfers[item]
+        return pltpu.make_async_remote_copy(
+            source,
+            outputs[item].at[where],
+            send.at[item, 0],
+            recv.at[item, 0],
+            device_id=swapped,
+            device_id_type=pl.DeviceIdType.MESH,
+        )
+
+    def exchange(item, stage):
+        _, _, where, bits, partner = transfers[item]
+        bit = bits[stage - 1]
+        if item < len(activations):
+            source, target = outputs[item].at[pl.ds(0, bit)], outputs[item].at[pl.ds(bit, bit)]
+        else:
+            block = pl.ds(column // bit * bit, bit)
+            source = target = outputs[item].at[block]
+        return pltpu.make_async_remote_copy(
+            source,
+            target,
+            send.at[item, stage],
+            recv.at[item, stage],
+            device_id=partner(bit),
+            device_id_type=pl.DeviceIdType.MESH,
+        )
+
+    def begin(item):
+        @pl.when(stays)
+        def _():
+            keep(item).start()
+
+        @pl.when(jnp.logical_not(stays))
+        def _():
+            swap(item).start()
+
+    ahead = 2
+    for item in order[:ahead]:
+        begin(item)
+
+    depth = max(len(row_bits), len(column_bits))
+    for tick in range(len(order) + depth):
+        if tick + ahead < len(order):
+            begin(order[tick + ahead])
+        for stage in range(1, depth + 2):
+            index = tick - stage + 1
+            if not 0 <= index < len(order):
+                continue
+            item = order[index]
+            bits = transfers[item][3]
+            if stage == 1:
+
+                @pl.when(stays)
+                def _(item=item):
+                    keep(item).wait()
+
+                @pl.when(jnp.logical_not(stays))
+                def _(item=item):
+                    swap(item).wait_recv()
+
+            elif stage <= len(bits) + 1:
+                exchange(item, stage - 1).wait_recv()
+            if stage <= len(bits):
+                exchange(item, stage).start()
+
+    @pl.when(jnp.logical_not(stays))
+    def _():
+        for item in order:
+            swap(item).wait_send()
+
+    for item in order:
+        for stage in range(1, len(transfers[item][3]) + 1):
+            exchange(item, stage).wait_send()
+
+
+def fetch(layout, activations, weights):
+    columns, tensor = layout.columns, layout.tensor
+    arrays = [value for _, value in activations + weights]
+    slices = [(value.shape[0] // columns, *value.shape[1:]) for _, value in weights]
+    shapes = [(tensor, *value.shape) for _, value in activations] + [
+        (columns, *part) for part in slices
+    ]
+    stages = tensor.bit_length() + columns.bit_length()
+    results = pl.pallas_call(
+        functools.partial(
+            fetch_kernel,
+            layout.dp,
+            tensor,
+            [rank for rank, _ in activations],
+            [rank for rank, _ in weights],
+        ),
+        in_specs=[pl.BlockSpec(memory_space=pltpu.VMEM)] * len(activations)
+        + [pl.BlockSpec(memory_space=pl.ANY)] * len(weights),
+        out_specs=[pl.BlockSpec(memory_space=pl.ANY)] * len(arrays),
+        out_shape=[jax.ShapeDtypeStruct(shape, jnp.bfloat16) for shape in shapes],
+        scratch_shapes=[pltpu.VMEM(part, jnp.bfloat16) for part in slices]
+        + [
+            pltpu.SemaphoreType.DMA((len(arrays), stages)),
+            pltpu.SemaphoreType.DMA((len(arrays), stages)),
+            pltpu.SemaphoreType.DMA((len(weights),)),
+        ],
+        compiler_params=pltpu.CompilerParams(collective_id=0, has_side_effects=True),
+        name="fetch",
+    )(*arrays)
+    whole = results[len(activations) :]
+    return results[: len(activations)], [
+        part.reshape(value.shape) for part, (_, value) in zip(whole, weights)
+    ]
+
+
 class Group:
-    def __init__(self, layout, inputs, memory, older, offsets, cotangent):
+    def __init__(self, layout, tokens, memory, older, cotangent, offsets):
         self.layout, self.offsets = layout, layout.swap(offsets)
         self.me = layout.shard.reshape(1).astype(jnp.int32)
-        self.count = inputs.shape[0]
-        self.length = inputs.shape[1] * layout.tensor
+        self.count = tokens.shape[1]
+        self.length = tokens.shape[2] * layout.tensor
         self.reduced = self.length // 3
         self.padded = -(-self.reduced // 128) * 128
-        self.raw = layout.swap(jnp.stack([inputs, memory]))
-        self.older = layout.swap(older)
-        self.cotangent = layout.swap(cotangent)
+        self.token_rows, self.memory_rows, self.older_rows = tokens, memory, older
+        self.grad_rows = cotangent
+        self.raw, self.cotangent = tokens[0], cotangent[0]
 
     def enter(self, gain):
-        layout = self.layout
-        whole = layout.gather(self.raw)
-        self.memory_rows = whole[:, 1]
-        self.token_z = normed(whole[:, 0], gain)
-        self.memory_z = normed(whole[:, 1], gain)
-        self.older_z = normed(layout.gather(self.older), gain)
+        self.token_z = normed(self.token_rows, gain)
+        self.memory_z = normed(self.memory_rows, gain)
+        self.older_z = normed(self.older_rows, gain)
         self.stacked = stack(self.me, self.memory_rows, self.reduced, self.padded)
 
     def compress(self, squeeze, pair_weight, gain):
@@ -622,7 +805,7 @@
         self.triples = matmul(self.token_z, triple_weight).astype(jnp.bfloat16)
         self.memory_pairs = matmul(self.memory_z, pair_weight).astype(jnp.bfloat16)
         self.older_pairs = matmul(self.older_z, pair_weight).astype(jnp.bfloat16)
-        self.attention, self.push, self.lse, self.added_lse, squares = attend(
+        self.attention, self.lse, self.grad_added, squares = attend(
             self.me,
             self.offsets,
             self.triples,
@@ -636,10 +819,9 @@
     def middle(self, out_weight, gain):
         layout = self.layout
         branch = layout.scatter(matmul(self.attention, out_weight))
-        self.hidden = self.raw[0].astype(jnp.float32) + branch
+        self.hidden = self.raw.astype(jnp.float32) + branch
         self.hidden_unit, self.hidden_inverse = normalize(self.hidden)
         self.feed_rows = layout.gather((self.hidden_unit * gain).astype(jnp.bfloat16))
-        self.grad_rows = layout.gather(self.cotangent)
 
     def feed(self, up_weight, down_weight, before):
         out, back, grad_up, grad_down = feedforward(
@@ -664,33 +846,34 @@
         return outer(self.attention, whole)
 
     def attend_back(self):
-        self.grad_triples, self.grad_memory, self.grad_older, self.grad_added = attend_back(
+        self.grad_triples, self.grad_memory, self.grad_older = attend_back(
             self.me,
             self.offsets,
             self.triples,
             self.memory_pairs,
             self.older_pairs,
-            self.added,
             self.attention,
             self.grad_attention,
-            self.push,
             self.lse,
-            self.added_lse,
-            self.reduced,
         )
 
     def compress_back(self, pair_weight, gain):
         layout = self.layout
-        grad = layout.total(matmul_back(self.grad_added, pair_weight))
+        grad = matmul_back(self.grad_added, pair_weight)
         grad = norm_back(grad, gain, self.added_unit, self.added_inverse).astype(jnp.bfloat16)
         extent = self.appended.shape[2]
-        mine = lax.dynamic_slice_in_dim(grad, layout.shard * extent, extent, 2)
-        return outer(self.stacked, mine)
+        pieces = jnp.stack(
+            [
+                lax.dynamic_slice_in_dim(grad, (layout.shard ^ j) * extent, extent, 2)
+                for j in range(layout.tensor)
+            ]
+        )
+        return outer(self.stacked, layout.scatter(pieces).astype(jnp.bfloat16))
 
     def enter_back(self, triple_weight, gain):
         layout = self.layout
         grad = layout.scatter(matmul_back(self.grad_triples, triple_weight))
-        unit, inverse = normalize(self.raw[0].astype(jnp.float32))
+        unit, inverse = normalize(self.raw.astype(jnp.float32))
         full = self.grad_hidden + norm_back(grad, gain, unit, inverse)
         return layout.swap(full.astype(jnp.bfloat16)).astype(jnp.float32)
 
@@ -727,16 +910,34 @@
 ):
     layout = Layout()
     width, local_width = query_weight.shape
-    short = Group(
-        layout, inputs_short, memory_short, compressed_short, offsets_short, cotangent_short
-    )
-    long = Group(layout, inputs_long, memory_long, compressed_long, offsets_long, cotangent_long)
+    rows, whole = fetch(
+        layout,
+        [
+            (0, inputs_short),
+            (1, memory_short),
+            (2, compressed_short),
+            (8, cotangent_short),
+            (3, inputs_long),
+            (4, memory_long),
+            (5, compressed_long),
+            (9, cotangent_long),
+        ],
+        [
+            (1.1, query_weight),
+            (1.2, key_weight),
+            (1.3, value_weight),
+            (2.1, compress_weight.reshape(3 * width, local_width)),
+            (3.1, out_weight),
+            (4.1, up_weight),
+            (5.1, down_weight),
+        ],
+    )
+    triple_weight = jnp.concatenate(whole[:3], 1)
+    pair_weight = triple_weight[:, local_width:]
+    squeeze, output_weight, up, down = whole[3:]
+    short = Group(layout, *rows[:4], offsets_short)
+    long = Group(layout, *rows[4:], offsets_long)
     groups = (short, long)
-    triple_weight = layout.weight(jnp.concatenate([query_weight, key_weight, value_weight], 1))
-    pair_weight = triple_weight[:, local_width:]
-    squeeze = layout.weight(compress_weight.reshape(3 * width, local_width))
-    output_weight = layout.weight(out_weight)
-    up, down = layout.weight(up_weight), layout.weight(down_weight)
 
     before = ()
     grad_out = grad_squeeze = grad_triple = 0.0
@@ -744,27 +945,29 @@
         group.enter(attention_gain)
         group.compress(squeeze, pair_weight, attention_gain)
         group.attend(triple_weight, pair_weight)
+        grad_squeeze += group.compress_back(pair_weight, attention_gain)
         group.middle(output_weight, feedforward_gain)
         before = group.feed(up, down, before)
         grad_out += group.middle_back(feedforward_gain, output_weight)
         group.attend_back()
-        grad_squeeze += group.compress_back(pair_weight, attention_gain)
         grad_triple += group.projection_grads()
     up_sum, down_sum = map(layout.grad, before)
+    squeeze_sum = layout.grad(grad_squeeze).reshape(3, width, local_width)
     out_sum = layout.grad(grad_out)
-    squeeze_sum = layout.grad(grad_squeeze).reshape(3, width, local_width)
     triple_sum = layout.grad(grad_triple)
     attention_part = (
         jnp.sum(grad_triple * triple_weight.astype(jnp.float32), 1) / attention_gain
     )
-    gain_one, gain_two, square_total = lax.psum(
-        (
-            attention_part,
-            short.feed_gain + long.feed_gain,
-            short.squares + long.squares,
-        ),
-        AXES,
-    )
+    sums = layout.total(
+        jnp.concatenate(
+            [
+                attention_part,
+                short.feed_gain + long.feed_gain,
+                jnp.full((128,), short.squares + long.squares),
+            ]
+        ).reshape(-1, 128)
+    ).reshape(-1)
+    gain_one, gain_two, square_total = sums[:width], sums[width : 2 * width], sums[2 * width]
     rows_all = sum(group.count * group.length for group in groups) * layout.dp
     return (
         short.leave(),

time: 841 us -> 772 us (0.918)
  Pallas kernels: 128 us -> 300 us
  waiting for transfers between devices: 285 us -> 138 us
  other arithmetic: 106 us -> 67.2 us
  starting transfers between devices: 106 us -> 78.8 us
  blocking collectives: 60.5 us -> 37 us
  matrix products: 78.1 us -> 69.6 us
    pallas_call x2 -> x3, Pallas kernels: 41.6 us -> 208 us  [the longest x1 170 us: fetch(): pl.pallas_call(functools.partial(fetch_kernel, layout.dp, tensor, [rank f...]
    ppermute x73 -> x55, waiting for transfers between devices: 284 us -> 127 us  [permute(): return jax.tree.map(lambda part: lax.ppermute(part, AXES, pairs), value)]
    psum x1 -> x0, blocking collectives: 39.2 us -> none  [per_device(): lax.psum((attention_part, short.feed_gain + long.feed_gain, short.squares...]
    ppermute x73 -> x55, starting transfers between devices: 105 us -> 73.6 us  [permute(): return jax.tree.map(lambda part: lax.ppermute(part, AXES, pairs), value)]
    concatenate x20 -> x10, other arithmetic: 32.3 us -> 12.2 us  [gather(): value = jnp.concatenate([value, self.flip(value, bit)], 0)]
    all_gather x2 -> x3, blocking collectives: 21.3 us -> 37 us  [grad(): mine = lax.all_gather(summed, 'dp', axis_index_groups=self.groups)]
    ppermute x0 -> x5, waiting for transfers between devices: none -> 11.5 us  [total(): value = value + lax.ppermute(value, axis, pairs)]
    unnamed x175 -> x266, local copies, waits for them, and re-layouts: 15.8 us -> 17.3 us
  transfers between devices with their start and end apart: 86 -> 67, of which waited for: 27 -> 25; matrix products, arithmetic and copies ran while one was open for 26% -> 23% of each run, Pallas kernels for 10% -> 39%
where the time goes in v3:
time: 772 us; the launch traced here: 767 us
  Pallas kernels  300 us (39%)
  waiting for transfers between devices  138 us (18%)
  starting transfers between devices  78.8 us (10%)
  matrix products  69.6 us (9%)
  other arithmetic  67.2 us (9%)
  local copies, waits for them, and re-layouts  55.6 us (7%)
  blocking collectives  37 us (5%)
  between operations  20 us (3%)
    pallas_call x1, Pallas kernels, fetch(): pl.pallas_call(functools.partial(fetch_kernel, layout.dp, tensor, [rank f...  170 us
    ppermute x55, waiting for transfers between devices, permute(): return jax.tree.map(lambda part: lax.ppermute(part, AXES, pairs), value)  127 us
    ppermute x55, starting transfers between devices, permute(): return jax.tree.map(lambda part: lax.ppermute(part, AXES, pairs), value)  73.6 us
    pallas_call x2, Pallas kernels, feedforward(): pl.pallas_call(functools.partial(feedforward_kernel, min(512, hidden)), g...  45.2 us
    pallas_call x2, Pallas kernels, attend(): pl.pallas_call(functools.partial(attend_kernel, reduced, many), grid_spec...  39.1 us
    pallas_call x2, Pallas kernels, attend_back(): pl.pallas_call(functools.partial(attend_back_kernel, many, heads), grid_s...  37.8 us
    all_gather x3, blocking collectives, grad(): mine = lax.all_gather(summed, 'dp', axis_index_groups=self.groups)  37 us
    dot_general x12, matrix products, matmul(): jnp.einsum('...k,kn->...n', left, right, preferred_element_type=jnp.float32)  29.3 us
  transfers between devices with their start and end apart: 67, of which 25 were waited for; matrix products, arithmetic and copies ran while one was open for 23% of the time, Pallas kernels for 39%

profile of v3, /device:TPU:1, one launch (start us, length us, event | category | flops | bytes accessed | tf_op | source)
XLA Modules:
  0.0 766.7 jit_solution(9939228627332433704)
XLA Ops:
  7.2 5.6 collective-permute-start
  12.9 170.4 %fetch.1 = (bf16[4,2,128,1024]{3,2,1,0:T(8,128)(2,1)}, bf16[4,2,128,1024]{3,2,1,0:T(8,128)(2,1)}, bf16[4,2,128,1024]{3,2,1,0:T(8,128)(2,1)}, bf16[4,2,128,1024]{...) custom-call(bf16[2,128,1024]{2,1,0:T(8,128)(2,1)} %refs_0_.1, ...), custom_call_target="tpu_custom_call" | custom-call | tf_op jit(solution)/shard_map/fetch/pallas_call | solution.py:751
  183.3 3.7 stack_memory.2
  190.0 3.5 collective-permute-start.10
  193.5 4.1 stack_memory.3
  211.9 3.1 convolution_convert_fusion.5.q_ref.kx_ref.vx_ref
  237.3 24.1 %attend.3 = (bf16[4,1,256,256]{3,2,1,0:T(8,128)(2,1)}, f32[2,1,1024]{2,1,0:T(1,128)}, bf16[1,384,512]{2,1,0:T(8,128)(2,1)}, f32[8,128]{1,0:T(8,128)}) custom-call(s32[1]{0:T(128)} %bitcast.2.me_ref, s32[1]{0:T(128)} %collective-permute-done.10.offsets_ref, bf16[4,1,256,768]{3,2,1,0:T(8,128)(2,1)} %fusion.61.q_ref.kx_ref.vx_ref, ...), custom_call_target="tpu_custom_call" | custom-call | flops 7247757312 | bytes 110592 | tf_op jit(solution)/shard_map/attend/pallas_call | solution.py:324
  278.4 15.1 %attend.2 = (bf16[4,2,128,256]{3,2,1,0:T(8,128)(2,1)}, f32[4,1,512]{2,1,0:T(1,128)}, bf16[2,256,512]{2,1,0:T(8,128)(2,1)}, f32[8,128]{1,0:T(8,128)}) custom-call(s32[1]{0:T(128)} %bitcast.2.me_ref, s32[2]{0:T(128)} %collective-permute-done.offsets_ref, bf16[4,2,128,768]{3,2,1,0:T(8,128)(2,1)} %convolution_convert_fusion.5.q_ref.kx_ref.vx_ref, ...), custom_call_target="tpu_custom_call" | custom-call | flops 3758096384 | bytes 57344 | tf_op jit(solution)/shard_map/attend/pallas_call | solution.py:324
  303.0 10.5 %collective-permute-done.14 = bf16[1,1,256,1024]{3,2,1,0:T(8,128)(2,1)S(1)} collective-permute-done((bf16[1,1,256,1024]{3,2,1,0:T(8,128)(2,1)S(1)}, bf16[1,1,256,1024]{3,2,1,0:T(8,128)(2,1)S(1)}, u32[]{:S(2)}, u32[]{:S(2)}) %collective-permute-start.14) | collective-permute-done | bytes 524320 | tf_op jit(solution)/shard_map/ppermute | solution.py:43
  314.8 9.9 %collective-permute-done.4 = bf16[1,2,128,1024]{3,2,1,0:T(8,128)(2,1)S(1)} collective-permute-done((bf16[1,2,128,1024]{3,2,1,0:T(8,128)(2,1)S(1)}, bf16[1,2,128,1024]{3,2,1,0:T(8,128)(2,1)S(1)}, u32[]{:S(2)}, u32[]{:S(2)}) %collective-permute-start.4) | collective-permute-done | bytes 524320 | tf_op jit(solution)/shard_map/ppermute | solution.py:43
  330.6 5.3 collective-permute-done.15
  339.3 7.9 %collective-permute-done.5 = bf16[1,2,128,1024]{3,2,1,0:T(8,128)(2,1)S(1)} collective-permute-done((bf16[1,2,128,1024]{3,2,1,0:T(8,128)(2,1)S(1)}, bf16[1,2,128,1024]{3,2,1,0:T(8,128)(2,1)S(1)}, u32[]{:S(2)}, u32[]{:S(2)}) %collective-permute-start.5) | collective-permute-done | bytes 524320 | tf_op jit(solution)/shard_map/ppermute | solution.py:43
  352.4 5.6 collective-permute-done.49
  366.3 21.2 %feedforward.2 = (bf16[4,2,128,1024]{3,2,1,0:T(8,128)(2,1)}, bf16[4,2,128,1024]{3,2,1,0:T(8,128)(2,1)}, f32[1024,1024]{1,0:T(8,128)}, f32[1024,1024]{1,0:T(8,128)}) custom-call(bf16[4,2,128,1024]{3,2,1,0:T(8,128)(2,1)} %pad_maximum_fusion.rows_ref, bf16[4,2,128,1024]{3,2,1,0:T(8,128)(2,1)} %get-tuple-element.62.grad_ref, bf16[1024,1024]{1,0:T(8,128)(2,1)} %bitcast.439, ...), custom_call_target="tpu_custom_call" | custom-call | flops 12884901888 | bytes 20971520 | tf_op jit(solution)/shard_map/feedforward/pallas_call | solution.py:538
  387.5 24.0 %feedforward.3 = (bf16[4,1,256,1024]{3,2,1,0:T(8,128)(2,1)}, bf16[4,1,256,1024]{3,2,1,0:T(8,128)(2,1)}, bf16[1024,1024]{1,0:T(8,128)(2,1)}, bf16[1024,1024]{1,0:T(8,128)(2,1)}) custom-call(bf16[4,1,256,1024]{3,2,1,0:T(8,128)(2,1)} %pad_maximum_fusion.1.rows_ref, bf16[4,1,256,1024]{3,2,1,0:T(8,128)(2,1)} %get-tuple-element.70.grad_ref, ...), custom_call_target="tpu_custom_call" | custom-call | flops 12884901888 | bytes 20971520 | tf_op jit(solution)/shard_map/feedforward/pallas_call | solution.py:538
  422.5 9.3 %collective-permute-done.28 = bf16[1,1,256,1024]{3,2,1,0:T(8,128)(2,1)} collective-permute-done((bf16[1,1,256,1024]{3,2,1,0:T(8,128)(2,1)}, bf16[1,1,256,1024]{3,2,1,0:T(8,128)(2,1)}, u32[]{:S(2)}, u32[]{:S(2)}) %collective-permute-start.28) | collective-permute-done | bytes 524320 | tf_op jit(solution)/shard_map/ppermute | solution.py:43
  435.7 7.2 collective-permute-done.21
  445.7 8.5 %collective-permute-done.29 = bf16[1,1,256,1024]{3,2,1,0:T(8,128)(2,1)S(1)} collective-permute-done((bf16[1,1,256,1024]{3,2,1,0:T(8,128)(2,1)S(1)}, bf16[1,1,256,1024]{3,2,1,0:T(8,128)(2,1)S(1)}, u32[]{:S(2)}, u32[]{:S(2)}) %collective-permute-start.29) | collective-permute-done | bytes 524320 | tf_op jit(solution)/shard_map/ppermute | solution.py:43
  456.3 9.0 %collective-permute-done.22 = bf16[1,2,128,1024]{3,2,1,0:T(8,128)(2,1)S(1)} collective-permute-done((bf16[1,2,128,1024]{3,2,1,0:T(8,128)(2,1)S(1)}, bf16[1,2,128,1024]{3,2,1,0:T(8,128)(2,1)S(1)}, u32[]{:S(2)}, u32[]{:S(2)}) %collective-permute-start.22) | collective-permute-done | bytes 524320 | tf_op jit(solution)/shard_map/ppermute | solution.py:43
  471.6 3.9 collective-permute-start.34
  480.4 6.9 collective-permute-done.35
  500.5 5.0 collective-permute-done.52
  506.6 19.4 %all-gather.4 = bf16[1536,256]{1,0:T(8,128)(2,1)} all-gather(bf16[384,256]{1,0:T(8,128)(2,1)S(1)} %add_convert_fusion.11), channel_id=6, replica_groups={{0,8,16,24},{4,12,20,28},{1,9,17,25},{5,13,21,29},{2,10,18,26},{6,14,22..., dimensions={0}, use_global_device_ids=true | all-gather | bytes 983040 | tf_op jit(solution)/shard_map/all_gather | solution.py:114
  530.7 14.4 %attend_back.2 = (bf16[4,2,128,768]{3,2,1,0:T(8,128)(2,1)}, bf16[4,2,128,512]{3,2,1,0:T(8,128)(2,1)}, bf16[4,2,128,512]{3,2,1,0:T(8,128)(2,1)}) custom-call(s32[1]{0:T(128)} %bitcast.2.me_ref, s32[2]{0:T(128)} %collective-permute-done.offsets_ref, bf16[4,2,128,768]{3,2,1,0:T(8,128)(2,1)} %convolution_convert_fusion.5.q_ref.kx_ref.vx_ref, ...), custom_call_target="tpu_custom_call" | custom-call | flops 8053063680 | bytes 98304 | tf_op jit(solution)/shard_map/attend_back/pallas_call | solution.py:452
  545.2 3.4 fusion.91.do_ref
  553.3 4.0 fusion.73
  557.3 23.3 %attend_back.3 = (bf16[4,1,256,768]{3,2,1,0:T(8,128)(2,1)}, bf16[4,1,256,512]{3,2,1,0:T(8,128)(2,1)}, bf16[4,1,256,512]{3,2,1,0:T(8,128)(2,1)}) custom-call(s32[1]{0:T(128)} %bitcast.2.me_ref, s32[1]{0:T(128)} %collective-permute-done.10.offsets_ref, bf16[4,1,256,768]{3,2,1,0:T(8,128)(2,1)} %fusion.61.q_ref.kx_ref.vx_ref, ...), custom_call_target="tpu_custom_call" | custom-call | flops 16106127360 | bytes 196608 | tf_op jit(solution)/shard_map/attend_back/pallas_call | solution.py:452
  582.8 3.8 collective-permute-start.42
  586.7 4.6 fusion.68
  591.3 5.9 collective-permute-done.42
  598.4 4.1 bitcast_add_fusion.2
  603.5 4.0 multiply_reduce_fusion
  607.5 3.1 convolution_convert_fusion.3
  610.8 3.8 convolution_convert_fusion.2
  627.2 9.7 %collective-permute-done.58 = f32[17,128]{1,0:T(8,128)S(1)} collective-permute-done((f32[17,128]{1,0:T(8,128)S(1)}, f32[17,128]{1,0:T(8,128)S(1)}, u32[]{:S(2)}, u32[]{:S(2)}) %collective-permute-start.58) | collective-permute-done | bytes 8736 | tf_op jit(solution)/shard_map/ppermute | solution.py:75
  642.2 5.2 collective-permute-start.39
  653.7 3.7 collective-permute-start.45
  657.4 5.7 all-gather.1
  669.1 3.6 fusion.109
  672.7 3.4 collective-permute-start.9
  679.1 3.3 fusion.104
  682.3 4.5 collective-permute-start.19
  690.9 4.5 collective-permute-start.33
  699.7 15.0 %collective-permute-done.19 = bf16[1,256,1024]{2,1,0:T(8,128)(2,1)} collective-permute-done((bf16[1,256,1024]{2,1,0:T(8,128)(2,1)}, bf16[1,256,1024]{2,1,0:T(8,128)(2,1)}, u32[]{:S(2)}, u32[]{:S(2)}) %collective-permute-start.19) | collective-permute-done | bytes 524320 | tf_op jit(solution)/shard_map/ppermute | solution.py:43
  717.5 4.7 collective-permute-done.26
  724.5 3.4 collective-permute-done.33
  728.9 3.2 collective-permute-done.36
  733.2 11.8 %all-gather = bf16[512,768]{1,0:T(8,128)(2,1)S(1)} all-gather(bf16[128,768]{1,0:T(8,128)(2,1)S(1)} %add_convert_fusion.13), channel_id=2, replica_groups={{0,8,16,24},{4,12,20,28},{1,9,17,25},{5,13,21,29},{2,10,18,26},{6,14,22..., dimensions={0}, use_global_device_ids=true | all-gather | bytes 983040 | tf_op jit(solution)/shard_map/all_gather | solution.py:114
  (560 shorter events, 207.3 us)
Async XLA Ops:
  7.2 486.7 %reduce-scatter.14.cloned.1.call-start = ((), (), s32[]{:S(2)}) async-start(), calls=%async_computation.9 | async-start | bytes 1966080 | tf_op jit(solution)/shard_map/reduce_scatter | solution.py:96
  7.2 271.2 %collective-permute-start = (s32[2]{0:T(128)}, s32[2]{0:T(128)}, u32[]{:S(2)}, u32[]{:S(2)}) collective-permute-start(s32[2]{0:T(128)} %param.22), channel_id=1, source_target_pairs={{0,0},{1,1},{2,4},{3,5},{4,2},{5,3},{6,6},{7,7},{8,8},{9,9},{10,12... | collective-permute-start | bytes 32 | tf_op jit(solution)/shard_map/ppermute | solution.py:43
  189.9 36.5 %collective-permute-start.1 = (bf16[1,2,256,256]{2,3,1,0:T(8,128)(2,1)S(1)}, bf16[1,2,256,256]{2,3,1,0:T(8,128)(2,1)S(1)}, u32[]{:S(2)}, u32[]{:S(2)}) collective-permute-start(bf16[1,2,256,256]{2,3,1,0:T(8,128)(2,1)S(1)} %bitcast.419), channel_id=1, source_target_pairs={{0,1},{1,0},{2,3},{3,2},{4,5},{5,4},{6,7},{7,6},{8,9},{9,8},{10,11... | collective-permute-start | bytes 786440 | tf_op jit(solution)/shard_map/ppermute | solution.py:43
  190.0 47.3 %collective-permute-start.10 = (s32[1]{0:T(128)}, s32[1]{0:T(128)}, u32[]{:S(2)}, u32[]{:S(2)}) collective-permute-start(s32[1]{0:T(128)} %param.26), channel_id=1, source_target_pairs={{0,0},{1,1},{2,4},{3,5},{4,2},{5,3},{6,6},{7,7},{8,8},{9,9},{10,12... | collective-permute-start | bytes 20 | tf_op jit(solution)/shard_map/ppermute | solution.py:43
  200.5 24.9 %collective-permute-start.11 = (bf16[1,1,384,256]{2,3,1,0:T(8,128)(2,1)S(1)}, bf16[1,1,384,256]{2,3,1,0:T(8,128)(2,1)S(1)}, u32[]{:S(2)}, u32[]{:S(2)}) collective-permute-start(bf16[1,1,384,256]{2,3,1,0:T(8,128)(2,1)S(1)} %bitcast.434), channel_id=1, source_target_pairs={{0,1},{1,0},{2,3},{3,2},{4,5},{5,4},{6,7},{7,6},{8,9},{9,8},{10,11... | collective-permute-start | bytes 589832 | tf_op jit(solution)/shard_map/ppermute | solution.py:43
  227.3 42.9 %collective-permute-start.2 = (bf16[2,2,256,256]{2,3,1,0:T(8,128)(2,1)}, bf16[2,2,256,256]{2,3,1,0:T(8,128)(2,1)}, u32[]{:S(2)}, u32[]{:S(2)}) collective-permute-start(bf16[2,2,256,256]{2,3,1,0:T(8,128)(2,1)} %pad_maximum_fusion.16), channel_id=1, source_target_pairs={{0,4},{1,5},{2,6},{3,7},{4,0},{5,1},{6,2},{7,3},{8,12},{9,13},{10,... | collective-permute-start | bytes 1572872 | tf_op jit(solution)/shard_map/ppermute | solution.py:43
  265.7 32.0 %collective-permute-start.13 = (bf16[2,1,256,1024]{3,2,1,0:T(8,128)(2,1)}, bf16[2,1,256,1024]{3,2,1,0:T(8,128)(2,1)}, u32[]{:S(2)}, u32[]{:S(2)}) collective-permute-start(bf16[2,1,256,1024]{3,2,1,0:T(8,128)(2,1)} %slice_bitcast_fusion.2), channel_id=1, source_target_pairs={{0,4},{1,5},{2,6},{3,7},{4,0},{5,1},{6,2},{7,3},{8,12},{9,13},{10,... | collective-permute-start | bytes 3145736 | tf_op jit(solution)/shard_map/ppermute | solution.py:43
  269.8 58.3 %collective-permute-start.50 = (bf16[2,1,384,256]{3,2,1,0:T(8,128)(2,1)}, bf16[2,1,384,256]{3,2,1,0:T(8,128)(2,1)}, u32[]{:S(2)}, u32[]{:S(2)}) collective-permute-start(bf16[2,1,384,256]{3,2,1,0:T(8,128)(2,1)} %pad_maximum_fusion.19), channel_id=1, source_target_pairs={{0,4},{1,5},{2,6},{3,7},{4,0},{5,1},{6,2},{7,3},{8,12},{9,13},{10,... | collective-permute-start | bytes 1179656 | tf_op jit(solution)/shard_map/ppermute | solution.py:43
  300.0 13.4 %collective-permute-start.14 = (bf16[1,1,256,1024]{3,2,1,0:T(8,128)(2,1)S(1)}, bf16[1,1,256,1024]{3,2,1,0:T(8,128)(2,1)S(1)}, u32[]{:S(2)}, u32[]{:S(2)}) collective-permute-start(bf16[1,1,256,1024]{3,2,1,0:T(8,128)(2,1)S(1)} %slice.229), channel_id=1, source_target_pairs={{0,1},{1,0},{2,3},{3,2},{4,5},{5,4},{6,7},{7,6},{8,9},{9,8},{10,11... | collective-permute-start | bytes 1572872 | tf_op jit(solution)/shard_map/ppermute | solution.py:43
  301.6 23.1 %collective-permute-start.4 = (bf16[1,2,128,1024]{3,2,1,0:T(8,128)(2,1)S(1)}, bf16[1,2,128,1024]{3,2,1,0:T(8,128)(2,1)S(1)}, u32[]{:S(2)}, u32[]{:S(2)}) collective-permute-start(bf16[1,2,128,1024]{3,2,1,0:T(8,128)(2,1)S(1)} %slice.223), channel_id=1, source_target_pairs={{0,1},{1,0},{2,3},{3,2},{4,5},{5,4},{6,7},{7,6},{8,9},{9,8},{10,11... | collective-permute-start | bytes 1572872 | tf_op jit(solution)/shard_map/ppermute | solution.py:43
  314.6 21.4 %collective-permute-start.15 = (bf16[1,1,256,1024]{3,2,1,0:T(8,128)(2,1)S(1)}, bf16[1,1,256,1024]{3,2,1,0:T(8,128)(2,1)S(1)}, u32[]{:S(2)}, u32[]{:S(2)}) collective-permute-start(bf16[1,1,256,1024]{3,2,1,0:T(8,128)(2,1)S(1)} %multiply_convert_fusion.2), channel_id=1, source_target_pairs={{0,1},{1,0},{2,3},{3,2},{4,5},{5,4},{6,7},{7,6},{8,9},{9,8},{10,11... | collective-permute-start | bytes 1572872 | tf_op jit(solution)/shard_map/ppermute | solution.py:43
  325.8 21.4 %collective-permute-start.5 = (bf16[1,2,128,1024]{3,2,1,0:T(8,128)(2,1)S(1)}, bf16[1,2,128,1024]{3,2,1,0:T(8,128)(2,1)S(1)}, u32[]{:S(2)}, u32[]{:S(2)}) collective-permute-start(bf16[1,2,128,1024]{3,2,1,0:T(8,128)(2,1)S(1)} %multiply_convert_fusion.3), channel_id=1, source_target_pairs={{0,1},{1,0},{2,3},{3,2},{4,5},{5,4},{6,7},{7,6},{8,9},{9,8},{10,11... | collective-permute-start | bytes 1572872 | tf_op jit(solution)/shard_map/ppermute | solution.py:43
  326.3 23.6 %collective-permute-start.48 = (bf16[2,2,256,256]{3,2,1,0:T(8,128)(2,1)S(1)}, bf16[2,2,256,256]{3,2,1,0:T(8,128)(2,1)S(1)}, u32[]{:S(2)}, u32[]{:S(2)}) collective-permute-start(bf16[2,2,256,256]{3,2,1,0:T(8,128)(2,1)S(1)} %pad_maximum_fusion.17), channel_id=1, source_target_pairs={{0,4},{1,5},{2,6},{3,7},{4,0},{5,1},{6,2},{7,3},{8,12},{9,13},{10,... | collective-permute-start | bytes 1572872 | tf_op jit(solution)/shard_map/ppermute | solution.py:43
  329.3 22.1 %collective-permute-start.51 = (bf16[1,1,384,256]{3,2,1,0:T(8,128)(2,1)S(1)}, bf16[1,1,384,256]{3,2,1,0:T(8,128)(2,1)S(1)}, u32[]{:S(2)}, u32[]{:S(2)}) collective-permute-start(bf16[1,1,384,256]{3,2,1,0:T(8,128)(2,1)S(1)} %slice.252), channel_id=1, source_target_pairs={{0,1},{1,0},{2,3},{3,2},{4,5},{5,4},{6,7},{7,6},{8,9},{9,8},{10,11... | collective-permute-start | bytes 589832 | tf_op jit(solution)/shard_map/ppermute | solution.py:43
  337.8 22.6 %collective-permute-start.16 = (bf16[2,1,256,1024]{3,2,1,0:T(8,128)(2,1)}, bf16[2,1,256,1024]{3,2,1,0:T(8,128)(2,1)}, u32[]{:S(2)}, u32[]{:S(2)}) collective-permute-start(bf16[2,1,256,1024]{3,2,1,0:T(8,128)(2,1)} %pad_maximum_fusion.8), channel_id=1, source_target_pairs={{0,4},{1,5},{2,6},{3,7},{4,0},{5,1},{6,2},{7,3},{8,12},{9,13},{10,... | collective-permute-start | bytes 3145736 | tf_op jit(solution)/shard_map/ppermute | solution.py:43
  348.3 15.2 %collective-permute-start.6 = (bf16[2,2,128,1024]{3,2,1,0:T(8,128)(2,1)}, bf16[2,2,128,1024]{3,2,1,0:T(8,128)(2,1)}, u32[]{:S(2)}, u32[]{:S(2)}) collective-permute-start(bf16[2,2,128,1024]{3,2,1,0:T(8,128)(2,1)} %pad_maximum_fusion.7), channel_id=1, source_target_pairs={{0,4},{1,5},{2,6},{3,7},{4,0},{5,1},{6,2},{7,3},{8,12},{9,13},{10,... | collective-permute-start | bytes 3145736 | tf_op jit(solution)/shard_map/ppermute | solution.py:43
  360.3 220.4 %reduce-scatter.10.cloned.1.call-start = ((), (), s32[]{:S(2)}) async-start(), calls=%async_computation.7 | async-start | bytes 2621440 | tf_op jit(solution)/shard_map/reduce_scatter | solution.py:96
  418.3 13.5 %collective-permute-start.28 = (bf16[1,1,256,1024]{3,2,1,0:T(8,128)(2,1)}, bf16[1,1,256,1024]{3,2,1,0:T(8,128)(2,1)}, u32[]{:S(2)}, u32[]{:S(2)}) collective-permute-start(bf16[1,1,256,1024]{3,2,1,0:T(8,128)(2,1)} %slice.239), channel_id=1, source_target_pairs={{0,1},{1,0},{2,3},{3,2},{4,5},{5,4},{6,7},{7,6},{8,9},{9,8},{10,11... | collective-permute-start | bytes 1572872 | tf_op jit(solution)/shard_map/ppermute | solution.py:43
  418.6 222.3 %reduce-scatter.8.cloned.1.call-start = ((), (), s32[]{:S(2)}) async-start(), calls=%async_computation.6 | async-start | bytes 655360 | tf_op jit(solution)/shard_map/reduce_scatter | solution.py:96
  421.2 21.7 %collective-permute-start.21 = (bf16[1,2,128,1024]{3,2,1,0:T(8,128)(2,1)S(1)}, bf16[1,2,128,1024]{3,2,1,0:T(8,128)(2,1)S(1)}, u32[]{:S(2)}, u32[]{:S(2)}) collective-permute-start(bf16[1,2,128,1024]{3,2,1,0:T(8,128)(2,1)S(1)} %slice.233), channel_id=1, source_target_pairs={{0,1},{1,0},{2,3},{3,2},{4,5},{5,4},{6,7},{7,6},{8,9},{9,8},{10,11... | collective-permute-start | bytes 1572872 | tf_op jit(solution)/shard_map/ppermute | solution.py:43
  435.5 18.7 %collective-permute-start.29 = (bf16[1,1,256,1024]{3,2,1,0:T(8,128)(2,1)S(1)}, bf16[1,1,256,1024]{3,2,1,0:T(8,128)(2,1)S(1)}, u32[]{:S(2)}, u32[]{:S(2)}) collective-permute-start(bf16[1,1,256,1024]{3,2,1,0:T(8,128)(2,1)S(1)} %fusion.115), channel_id=1, source_target_pairs={{0,1},{1,0},{2,3},{3,2},{4,5},{5,4},{6,7},{7,6},{8,9},{9,8},{10,11... | collective-permute-start | bytes 1572872 | tf_op jit(solution)/shard_map/ppermute | solution.py:43
  445.4 20.0 %collective-permute-start.22 = (bf16[1,2,128,1024]{3,2,1,0:T(8,128)(2,1)S(1)}, bf16[1,2,128,1024]{3,2,1,0:T(8,128)(2,1)S(1)}, u32[]{:S(2)}, u32[]{:S(2)}) collective-permute-start(bf16[1,2,128,1024]{3,2,1,0:T(8,128)(2,1)S(1)} %fusion.113), channel_id=1, source_target_pairs={{0,1},{1,0},{2,3},{3,2},{4,5},{5,4},{6,7},{7,6},{8,9},{9,8},{10,11... | collective-permute-start | bytes 1572872 | tf_op jit(solution)/shard_map/ppermute | solution.py:43
  471.6 175.8 %reduce-scatter.12.cloned.1.call-start = ((), (), s32[]{:S(2)}) async-start(), calls=%async_computation.8 | async-start | bytes 2621440 | tf_op jit(solution)/shard_map/reduce_scatter | solution.py:96
  471.6 17.4 %collective-permute-start.34 = (bf16[2,256,256]{1,2,0:T(8,128)(2,1)S(1)}, bf16[2,256,256]{1,2,0:T(8,128)(2,1)}, u32[]{:S(2)}, u32[]{:S(2)}) collective-permute-start(bf16[2,256,256]{1,2,0:T(8,128)(2,1)S(1)} %copy-done.59), channel_id=1, source_target_pairs={{0,0},{1,1},{2,4},{3,5},{4,2},{5,3},{6,6},{7,7},{8,8},{9,9},{10,12... | collective-permute-start | bytes 786440 | tf_op jit(solution)/shard_map/ppermute | solution.py:43
  480.4 45.7 %collective-permute-start.7 = (bf16[2,2,128,1024]{3,2,1,0:T(8,128)(2,1)}, bf16[2,2,128,1024]{3,2,1,0:T(8,128)(2,1)}, u32[]{:S(2)}, u32[]{:S(2)}) collective-permute-start(bf16[2,2,128,1024]{3,2,1,0:T(8,128)(2,1)} %slice.174), channel_id=1, source_target_pairs={{0,4},{1,5},{2,6},{3,7},{4,0},{5,1},{6,2},{7,3},{8,12},{9,13},{10,... | collective-permute-start | bytes 3145736 | tf_op jit(solution)/shard_map/ppermute | solution.py:43
  500.4 118.9 %collective-permute-start.17 = (bf16[2,1,256,1024]{3,2,1,0:T(8,128)(2,1)}, bf16[2,1,256,1024]{3,2,1,0:T(8,128)(2,1)}, u32[]{:S(2)}, u32[]{:S(2)}) collective-permute-start(bf16[2,1,256,1024]{3,2,1,0:T(8,128)(2,1)} %slice.184), channel_id=1, source_target_pairs={{0,4},{1,5},{2,6},{3,7},{4,0},{5,1},{6,2},{7,3},{8,12},{9,13},{10,... | collective-permute-start | bytes 3145736 | tf_op jit(solution)/shard_map/ppermute | solution.py:43
  500.4 195.1 %all-gather.8.cloned.1.call-start = ((), (), s32[]{:S(2)}) async-start(), calls=%async_computation.10 | async-start | bytes 1310720 | tf_op jit(solution)/shard_map/all_gather | solution.py:114
  526.0 97.1 %collective-permute-start.54 = (bf16[4,384,256]{2,1,0:T(8,128)(2,1)}, bf16[4,384,256]{2,1,0:T(8,128)(2,1)}, u32[]{:S(2)}, u32[]{:S(2)}) collective-permute-start(bf16[4,384,256]{2,1,0:T(8,128)(2,1)} %bitcast.108), channel_id=1, source_target_pairs={{0,4},{1,5},{2,6},{3,7},{4,0},{5,1},{6,2},{7,3},{8,12},{9,13},{10,... | collective-permute-start | bytes 2359304 | tf_op jit(solution)/shard_map/ppermute | solution.py:43
  529.1 139.9 %collective-permute-start.8 = (bf16[1,2,128,1024]{3,2,1,0:T(8,128)(2,1)}, bf16[1,2,128,1024]{3,2,1,0:T(8,128)(2,1)}, u32[]{:S(2)}, u32[]{:S(2)}) collective-permute-start(bf16[1,2,128,1024]{3,2,1,0:T(8,128)(2,1)} %slice.225), channel_id=1, source_target_pairs={{0,1},{1,0},{2,3},{3,2},{4,5},{5,4},{6,7},{7,6},{8,9},{9,8},{10,11... | collective-permute-start | bytes 1572872 | tf_op jit(solution)/shard_map/ppermute | solution.py:43
  582.8 14.4 %collective-permute-start.42 = (bf16[128,1024]{1,0:T(8,128)(2,1)S(1)}, bf16[128,1024]{1,0:T(8,128)(2,1)S(1)}, u32[]{:S(2)}, u32[]{:S(2)}) collective-permute-start(bf16[128,1024]{1,0:T(8,128)(2,1)S(1)} %get-tuple-element.177), channel_id=1, source_target_pairs={{0,0},{1,1},{2,4},{3,5},{4,2},{5,3},{6,6},{7,7},{8,8},{9,9},{10,12... | collective-permute-start | bytes 786440 | tf_op jit(solution)/shard_map/ppermute | solution.py:43
  598.0 100.5 %reduce-scatter.6.cloned.1.call-start = ((), (), s32[]{:S(2)}) async-start(), calls=%async_computation.5 | async-start | bytes 1966080 | tf_op jit(solution)/shard_map/reduce_scatter | solution.py:96
  610.6 111.6 %all-gather.10.cloned.1.call-start = ((), (), s32[]{:S(2)}) async-start(), calls=%async_computation.11 | async-start | bytes 1310720 | tf_op jit(solution)/shard_map/all_gather | solution.py:114
  614.7 22.3 %collective-permute-start.24 = (bf16[2,2,128,1024]{3,2,1,0:T(8,128)(2,1)S(1)}, bf16[2,2,128,1024]{3,2,1,0:T(8,128)(2,1)S(1)}, u32[]{:S(2)}, u32[]{:S(2)}) collective-permute-start(bf16[2,2,128,1024]{3,2,1,0:T(8,128)(2,1)S(1)} %slice.235), channel_id=1, source_target_pairs={{0,4},{1,5},{2,6},{3,7},{4,0},{5,1},{6,2},{7,3},{8,12},{9,13},{10,... | collective-permute-start | bytes 3145736 | tf_op jit(solution)/shard_map/ppermute | solution.py:43
  618.2 20.4 %collective-permute-start.31 = (bf16[2,1,256,1024]{3,2,1,0:T(8,128)(2,1)S(1)}, bf16[2,1,256,1024]{3,2,1,0:T(8,128)(2,1)S(1)}, u32[]{:S(2)}, u32[]{:S(2)}) collective-permute-start(bf16[2,1,256,1024]{3,2,1,0:T(8,128)(2,1)S(1)} %slice_bitcast_fusion), channel_id=1, source_target_pairs={{0,4},{1,5},{2,6},{3,7},{4,0},{5,1},{6,2},{7,3},{8,12},{9,13},{10,... | collective-permute-start | bytes 3145736 | tf_op jit(solution)/shard_map/ppermute | solution.py:43
  623.2 55.9 %collective-permute-start.18 = (bf16[1,1,256,1024]{3,2,1,0:T(8,128)(2,1)}, bf16[1,1,256,1024]{3,2,1,0:T(8,128)(2,1)}, u32[]{:S(2)}, u32[]{:S(2)}) collective-permute-start(bf16[1,1,256,1024]{3,2,1,0:T(8,128)(2,1)} %slice.231), channel_id=1, source_target_pairs={{0,1},{1,0},{2,3},{3,2},{4,5},{5,4},{6,7},{7,6},{8,9},{9,8},{10,11... | collective-permute-start | bytes 1572872 | tf_op jit(solution)/shard_map/ppermute | solution.py:43
  623.2 13.8 %collective-permute-start.58 = (f32[17,128]{1,0:T(8,128)S(1)}, f32[17,128]{1,0:T(8,128)S(1)}, u32[]{:S(2)}, u32[]{:S(2)}) collective-permute-start(f32[17,128]{1,0:T(8,128)S(1)} %add.472), channel_id=1, source_target_pairs={{0,1},{1,0},{2,3},{3,2},{4,5},{5,4},{6,7},{7,6},{8,9},{9,8},{10,11... | collective-permute-start | bytes 26120 | tf_op jit(solution)/shard_map/ppermute | solution.py:75
  638.3 27.5 %collective-permute-start.25 = (bf16[1,2,128,1024]{3,2,1,0:T(8,128)(2,1)}, bf16[1,2,128,1024]{3,2,1,0:T(8,128)(2,1)}, u32[]{:S(2)}, u32[]{:S(2)}) collective-permute-start(bf16[1,2,128,1024]{3,2,1,0:T(8,128)(2,1)} %slice.237), channel_id=1, source_target_pairs={{0,1},{1,0},{2,3},{3,2},{4,5},{5,4},{6,7},{7,6},{8,9},{9,8},{10,11... | collective-permute-start | bytes 1572872 | tf_op jit(solution)/shard_map/ppermute | solution.py:43
  663.2 25.8 %collective-permute-start.59 = (f32[17,128]{1,0:T(8,128)S(1)}, f32[17,128]{1,0:T(8,128)S(1)}, u32[]{:S(2)}, u32[]{:S(2)}) collective-permute-start(f32[17,128]{1,0:T(8,128)S(1)} %add.473), channel_id=1, source_target_pairs={{0,2},{1,3},{2,0},{3,1},{4,6},{5,7},{6,4},{7,5},{8,10},{9,11},{10,... | collective-permute-start | bytes 26120 | tf_op jit(solution)/shard_map/ppermute | solution.py:75
  665.0 12.5 %collective-permute-start.32 = (bf16[1,1,256,1024]{3,2,1,0:T(8,128)(2,1)}, bf16[1,1,256,1024]{3,2,1,0:T(8,128)(2,1)}, u32[]{:S(2)}, u32[]{:S(2)}) collective-permute-start(bf16[1,1,256,1024]{3,2,1,0:T(8,128)(2,1)} %slice.243), channel_id=1, source_target_pairs={{0,1},{1,0},{2,3},{3,2},{4,5},{5,4},{6,7},{7,6},{8,9},{9,8},{10,11... | collective-permute-start | bytes 1572872 | tf_op jit(solution)/shard_map/ppermute | solution.py:43
  665.8 29.7 %collective-permute-start.41 = (bf16[4,32,1024]{2,1,0:T(8,128)(2,1)S(1)}, bf16[4,32,1024]{2,1,0:T(8,128)(2,1)}, u32[]{:S(2)}, u32[]{:S(2)}) collective-permute-start(bf16[4,32,1024]{2,1,0:T(8,128)(2,1)S(1)} %bitcast.417), channel_id=1, source_target_pairs={{0,4},{1,5},{2,6},{3,7},{4,0},{5,1},{6,2},{7,3},{8,12},{9,13},{10,... | collective-permute-start | bytes 786440 | tf_op jit(solution)/shard_map/ppermute | solution.py:43
  672.7 26.9 %collective-permute-start.9 = (bf16[2,128,1024]{2,1,0:T(8,128)(2,1)}, bf16[2,128,1024]{2,1,0:T(8,128)(2,1)}, u32[]{:S(2)}, u32[]{:S(2)}) collective-permute-start(bf16[2,128,1024]{2,1,0:T(8,128)(2,1)} %get-tuple-element.162), channel_id=1, source_target_pairs={{0,0},{1,1},{2,4},{3,5},{4,2},{5,3},{6,6},{7,7},{8,8},{9,9},{10,12... | collective-permute-start | bytes 1572872 | tf_op jit(solution)/shard_map/ppermute | solution.py:43
  682.3 32.3 %collective-permute-start.19 = (bf16[1,256,1024]{2,1,0:T(8,128)(2,1)}, bf16[1,256,1024]{2,1,0:T(8,128)(2,1)}, u32[]{:S(2)}, u32[]{:S(2)}) collective-permute-start(bf16[1,256,1024]{2,1,0:T(8,128)(2,1)} %get-tuple-element.160), channel_id=1, source_target_pairs={{0,0},{1,1},{2,4},{3,5},{4,2},{5,3},{6,6},{7,7},{8,8},{9,9},{10,12... | collective-permute-start | bytes 1572872 | tf_op jit(solution)/shard_map/ppermute | solution.py:43
  689.0 33.2 %collective-permute-start.26 = (bf16[2,128,1024]{2,1,0:T(8,128)(2,1)}, bf16[2,128,1024]{2,1,0:T(8,128)(2,1)S(1)}, u32[]{:S(2)}, u32[]{:S(2)}) collective-permute-start(bf16[2,128,1024]{2,1,0:T(8,128)(2,1)} %get-tuple-element.161), channel_id=1, source_target_pairs={{0,0},{1,1},{2,4},{3,5},{4,2},{5,3},{6,6},{7,7},{8,8},{9,9},{10,12... | collective-permute-start | bytes 1572872 | tf_op jit(solution)/shard_map/ppermute | solution.py:43
  690.9 36.9 %collective-permute-start.33 = (bf16[1,256,1024]{2,1,0:T(8,128)(2,1)}, bf16[1,256,1024]{2,1,0:T(8,128)(2,1)S(1)}, u32[]{:S(2)}, u32[]{:S(2)}) collective-permute-start(bf16[1,256,1024]{2,1,0:T(8,128)(2,1)} %get-tuple-element.159), channel_id=1, source_target_pairs={{0,0},{1,1},{2,4},{3,5},{4,2},{5,3},{6,6},{7,7},{8,8},{9,9},{10,12... | collective-permute-start | bytes 1572872 | tf_op jit(solution)/shard_map/ppermute | solution.py:43
  695.5 49.9 %collective-permute-start.44 = (bf16[4,128,1024]{2,1,0:T(8,128)(2,1)}, bf16[4,128,1024]{2,1,0:T(8,128)(2,1)}, u32[]{:S(2)}, u32[]{:S(2)}) collective-permute-start(bf16[4,128,1024]{2,1,0:T(8,128)(2,1)} %bitcast.412), channel_id=1, source_target_pairs={{0,4},{1,5},{2,6},{3,7},{4,0},{5,1},{6,2},{7,3},{8,12},{9,13},{10,... | collective-permute-start | bytes 3145736 | tf_op jit(solution)/shard_map/ppermute | solution.py:43
  699.6 29.4 %collective-permute-start.37 = (bf16[128,768]{1,0:T(8,128)(2,1)S(1)}, bf16[128,768]{1,0:T(8,128)(2,1)}, u32[]{:S(2)}, u32[]{:S(2)}) collective-permute-start(bf16[128,768]{1,0:T(8,128)(2,1)S(1)} %get-tuple-element.184), channel_id=1, source_target_pairs={{0,4},{1,5},{2,0},{3,1},{4,6},{5,7},{6,2},{7,3},{8,12},{9,13},{10,... | collective-permute-start | bytes 589832 | tf_op jit(solution)/shard_map/ppermute | solution.py:43
  714.6 17.6 %collective-permute-start.36 = (bf16[128,768]{1,0:T(8,128)(2,1)S(1)}, bf16[128,768]{1,0:T(8,128)(2,1)}, u32[]{:S(2)}, u32[]{:S(2)}) collective-permute-start(bf16[128,768]{1,0:T(8,128)(2,1)S(1)} %get-tuple-element.183), channel_id=1, source_target_pairs={{0,0},{1,1},{2,4},{3,5},{4,2},{5,3},{6,6},{7,7},{8,8},{9,9},{10,12... | collective-permute-start | bytes 589832 | tf_op jit(solution)/shard_map/ppermute | solution.py:43
  722.2 27.2 %collective-permute-start.47 = (bf16[4,128,1024]{2,1,0:T(8,128)(2,1)}, bf16[4,128,1024]{2,1,0:T(8,128)(2,1)S(1)}, u32[]{:S(2)}, u32[]{:S(2)}) collective-permute-start(bf16[4,128,1024]{2,1,0:T(8,128)(2,1)} %bitcast.414), channel_id=1, source_target_pairs={{0,4},{1,5},{2,6},{3,7},{4,0},{5,1},{6,2},{7,3},{8,12},{9,13},{10,... | collective-permute-start | bytes 3145736 | tf_op jit(solution)/shard_map/ppermute | solution.py:43
  (150 other events, 1128.6 us)
Sparse Core Ops, SparseCore 0:
  360.5 29.4 reduce-scatter.13
  418.7 34.7 reduce-scatter.9
  471.7 23.0 reduce-scatter.7
  500.6 39.6 reduce-scatter.11
  598.1 24.1 all-gather.7
  626.0 30.9 reduce-scatter.5
  665.9 26.4 all-gather.9

commit v4 on v3

--- a/solution.py
+++ b/solution.py
@@ -67,15 +67,6 @@
             bit //= 2
         return value[0]
 
-    def total(self, value):
-        for axis, extent in zip(AXES, (self.dp, self.tensor)):
-            bit = 1
-            while bit < extent:
-                pairs = [(i, i ^ bit) for i in range(extent)]
-                value = value + lax.ppermute(value, axis, pairs)
-                bit *= 2
-        return value
-
     def ordered(self, pieces, axis):
         return jnp.concatenate(
             [
@@ -85,41 +76,11 @@
             axis,
         )
 
-    def weight(self, value):
-        rows = value.shape[0] // self.columns
-        mine = lax.dynamic_slice_in_dim(value, self.column * rows, rows, 0)
-        return lax.all_gather(
-            self.swap(mine), "dp", axis=0, tiled=True, axis_index_groups=self.groups
-        )
-
-    def grad(self, value):
-        part = lax.psum_scatter(
-            value.astype(jnp.bfloat16),
-            "dp",
-            scatter_dimension=0,
-            tiled=True,
-            axis_index_groups=self.groups,
-        )
-        rows = part.shape[0] // 2
-
-        def eighth(index):
-            return lax.dynamic_slice_in_dim(part, index * rows, rows, 0)
-
-        other = self.permute(
-            eighth(1 - self.upper),
-            lambda p, c, h, a: (p, c, c, a) if c != h else (p, 1 - c, h, a),
-        )
-        own = self.permute(eighth(self.upper), lambda p, c, h, a: (p, h, c, a))
-        summed = (own.astype(jnp.float32) + other.astype(jnp.float32)).astype(jnp.bfloat16)
-        mine = lax.all_gather(summed, "dp", axis_index_groups=self.groups)
-        other = self.flip(mine, self.half)
-        first = jnp.where(self.core == 0, mine, other)
-        second = jnp.where(self.core == 0, other, mine)
-        return jnp.stack([first, second], 1).reshape(value.shape).astype(jnp.float32)
-
-
-def after(value, *done):
-    return lax.optimization_barrier((value, done))[0]
+    def split(self, grad):
+        return grad.astype(jnp.bfloat16).reshape(self.columns, -1, grad.shape[1])
+
+    def eighths(self, grad):
+        return (self.columns, 2, grad.shape[0] // (2 * self.columns), grad.shape[1])
 
 
 def normalize(rows):
@@ -775,6 +736,451 @@
     ]
 
 
+class Links:
+    def __init__(self, dp, tensor, send, recv):
+        self.half, self.columns = tensor // 2, dp // 2
+        self.send, self.recv, self.used, self.sent = send, recv, 0, []
+        place, plane = lax.axis_index("dp"), lax.axis_index("tensor")
+        self.core, self.column = place % 2, place // 2
+        self.upper, self.lower = plane // self.half, plane % self.half
+        self.stays = self.core == self.upper
+        self.row_bits = [1 << i for i in range(self.half.bit_length() - 1)] + [self.half]
+        self.column_bits = [1 << i for i in range(self.columns.bit_length() - 1)]
+
+    def at(self, column=None, core=None, upper=None, lower=None):
+        column = self.column if column is None else column
+        core = self.core if core is None else core
+        upper = self.upper if upper is None else upper
+        lower = self.lower if lower is None else lower
+        return (2 * column + core, upper * self.half + lower)
+
+    def row(self, bit):
+        if bit == self.half:
+            return self.at(core=1 - self.core)
+        return self.at(lower=self.lower ^ bit)
+
+    def swapped(self):
+        return self.at(core=self.upper, upper=self.core)
+
+    def greet(self):
+        partners = [self.row(bit) for bit in self.row_bits]
+        partners += [self.at(column=self.column ^ bit) for bit in self.column_bits]
+        partners.append(self.at(upper=1 - self.upper))
+        barrier = pltpu.get_barrier_semaphore()
+
+        def signal(partner):
+            pl.semaphore_signal(barrier, 1, device_id=partner, device_id_type=pl.DeviceIdType.MESH)
+
+        for partner in partners:
+            signal(partner)
+
+        @pl.when(self.stays)
+        def _():
+            pl.semaphore_wait(barrier, len(partners))
+
+        @pl.when(jnp.logical_not(self.stays))
+        def _():
+            signal(self.swapped())
+            pl.semaphore_wait(barrier, len(partners) + 1)
+
+    def slot(self):
+        self.used += 1
+        return self.used - 1
+
+    def copy(self, source, target, partner, slot=None):
+        slot = self.slot() if slot is None else slot
+        return pltpu.make_async_remote_copy(
+            source,
+            target,
+            self.send.at[slot],
+            self.recv.at[slot],
+            device_id=partner,
+            device_id_type=pl.DeviceIdType.MESH,
+        )
+
+    def put(self, source, target, partner):
+        copy = self.copy(source, target, partner)
+        copy.start()
+        self.sent.append(copy)
+        return copy
+
+    def finish(self):
+        for copy in self.sent:
+            copy.wait_send()
+
+
+def reduce_rows(links, partial, received, work, result):
+    arrived = []
+    for step, bit in enumerate(reversed(links.row_bits)):
+        source = partial
+        if step:
+            source = work
+            for piece in range(bit, 2 * bit):
+                value = partial[piece].astype(jnp.float32)
+                for other in arrived:
+                    value += other[piece].astype(jnp.float32)
+                work[piece] = value.astype(jnp.bfloat16)
+        copy = links.put(source.at[pl.ds(bit, bit)], received[step], links.row(bit))
+        yield
+        copy.wait_recv()
+        arrived.append(received[step])
+    value = partial[0].astype(jnp.float32)
+    for other in arrived:
+        value += other[0].astype(jnp.float32)
+    result.append(value)
+
+
+def gather_rows(links, whole):
+    for bit in links.row_bits:
+        copy = links.put(whole.at[pl.ds(0, bit)], whole.at[pl.ds(bit, bit)], links.row(bit))
+        yield
+        copy.wait_recv()
+
+
+def return_rows(links, value, mine, target):
+    copy = links.copy(mine, target, links.swapped())
+
+    @pl.when(links.stays)
+    def _():
+        target[...] = value
+
+    @pl.when(jnp.logical_not(links.stays))
+    def _():
+        mine[...] = value
+        copy.start()
+
+    yield
+
+    @pl.when(jnp.logical_not(links.stays))
+    def _():
+        copy.wait_recv()
+        copy.wait_send()
+
+
+def reduce_columns(links, bits, grad, received, work, quarter, across, store):
+    left = list(bits)
+    arrived = []
+
+    def relative(some):
+        found = [0]
+        for bit in some:
+            found += [value | bit for value in found]
+        return found
+
+    def value_of(place):
+        value = grad[links.column ^ place].astype(jnp.float32)
+        for other, slots in arrived:
+            value += other[slots.index(place)].astype(jnp.float32)
+        return value
+
+    for step, bit in enumerate(bits):
+        left.remove(bit)
+        slots = relative(left)
+        copies = []
+        for slot, place in enumerate(slots):
+            if step:
+                work[slot] = value_of(place | bit).astype(jnp.bfloat16)
+                source = work.at[slot]
+            else:
+                source = grad.at[links.column ^ (place | bit)]
+            copies.append(
+                links.put(
+                    source, received[step].at[slot], links.at(column=links.column ^ bit)
+                )
+            )
+        yield
+        for copy in copies:
+            copy.wait_recv()
+        arrived.append((received[step], slots))
+    value = value_of(0)
+    rows = value.shape[0] // 2
+    quarter[0] = value[:rows].astype(jnp.bfloat16)
+    quarter[1] = value[rows:].astype(jnp.bfloat16)
+    first, slot = quarter.at[1 - links.upper], links.slot()
+    to_core = links.copy(first, across.at[0], links.at(core=1 - links.core), slot)
+    to_half = links.copy(first, across.at[0], links.at(upper=1 - links.upper), slot)
+    to_swapped = links.copy(quarter.at[links.upper], across.at[1], links.swapped())
+
+    @pl.when(links.stays)
+    def _():
+        to_core.start()
+
+    @pl.when(jnp.logical_not(links.stays))
+    def _():
+        to_half.start()
+        to_swapped.start()
+
+    yield
+    to_core.wait()
+
+    @pl.when(links.stays)
+    def _():
+        total = quarter[links.upper].astype(jnp.float32) + across[0].astype(jnp.float32)
+        store(total.astype(jnp.bfloat16))
+
+    @pl.when(jnp.logical_not(links.stays))
+    def _():
+        to_swapped.wait()
+        total = across[1].astype(jnp.float32) + across[0].astype(jnp.float32)
+        store(total.astype(jnp.bfloat16))
+
+
+def gather_columns(links, bits, result):
+    places = [0]
+    for bit in bits:
+        copies = []
+        for place in places:
+            part = result.at[links.column ^ place, links.core]
+            copies.append(links.put(part, part, links.at(column=links.column ^ bit)))
+        yield
+        for copy in copies:
+            copy.wait_recv()
+        places += [place | bit for place in places]
+    part = result.at[:, links.core]
+    copy = links.put(part, part, links.at(core=1 - links.core))
+    yield
+    copy.wait_recv()
+
+
+def sum_all(links, source, slots, result):
+    value = source[...]
+    partners = [links.row(bit) for bit in links.row_bits] + [links.at(upper=1 - links.upper)]
+    partners += [links.at(column=links.column ^ bit) for bit in links.column_bits]
+    for step, partner in enumerate(partners):
+        slots[2 * step] = value
+        copy = links.put(slots.at[2 * step], slots.at[2 * step + 1], partner)
+        yield
+        copy.wait_recv()
+        value = value + slots[2 * step + 1]
+    result[...] = value
+
+
+def run_streams(links, streams, order):
+    alive = dict(enumerate(streams))
+
+    def advance(index):
+        if index in alive:
+            try:
+                next(alive[index])
+            except StopIteration:
+                del alive[index]
+
+    for index in order:
+        advance(index)
+    while alive:
+        for index in list(alive):
+            advance(index)
+    links.finish()
+
+
+def row_buffers(shape):
+    pieces, *rest = shape
+    sizes, bit = [], pieces // 2
+    while bit:
+        sizes.append(bit)
+        bit //= 2
+    return [pltpu.VMEM((size, *rest), jnp.bfloat16) for size in sizes + [pieces // 2]]
+
+
+def column_buffers(shape):
+    columns, rows, width = shape
+    sizes, count = [], columns // 2
+    while count:
+        sizes.append(count)
+        count //= 2
+    return [pltpu.VMEM((size, rows, width), jnp.bfloat16) for size in sizes] + [
+        pltpu.VMEM((max(1, columns // 4), rows, width), jnp.bfloat16),
+        pltpu.VMEM((2, rows // 2, width), jnp.bfloat16),
+        pltpu.VMEM((2, rows // 2, width), jnp.bfloat16),
+    ]
+
+
+def take(refs, count):
+    taken = refs[:count]
+    del refs[:count]
+    return taken
+
+
+def exchange(kernel, layout, collective_id, inputs, outputs, scratch, copies, name):
+    vmem = pl.BlockSpec(memory_space=pltpu.VMEM)
+    return pl.pallas_call(
+        functools.partial(kernel, layout.dp, layout.tensor),
+        in_specs=[vmem] * len(inputs),
+        out_specs=[vmem] * len(outputs),
+        out_shape=[jax.ShapeDtypeStruct(*each) for each in outputs],
+        scratch_shapes=scratch
+        + [pltpu.SemaphoreType.DMA((copies,)), pltpu.SemaphoreType.DMA((copies,))],
+        compiler_params=pltpu.CompilerParams(collective_id=collective_id, has_side_effects=True),
+        name=name,
+    )(*inputs)
+
+
+def middle_kernel(dp, tensor, *refs):
+    refs = list(refs)
+    links = Links(dp, tensor, *refs[-2:])
+    gain = refs.pop(0)
+    groups = [take(refs, 3) for _ in range(2)]
+    outputs = [take(refs, 3) for _ in range(2)]
+    count = len(links.row_bits) + 1
+    buffers = [take(refs, 2 * count) for _ in range(2)]
+    links.greet()
+
+    def stream(inputs, results, spare):
+        (partial, raw, _), (hidden, whole, _) = inputs, results
+        found = []
+        yield from reduce_rows(links, partial, spare[: count - 1], spare[count - 1], found)
+        value = raw[...].astype(jnp.float32) + found[0]
+        hidden[...] = value
+        whole[0] = (normalize(value)[0] * gain[...]).astype(jnp.bfloat16)
+        yield from gather_rows(links, whole)
+
+    def appended(inputs, results, spare):
+        found = []
+        yield from reduce_rows(links, inputs[2], spare[count:-1], spare[-1], found)
+        results[2][...] = found[0].astype(jnp.bfloat16)
+
+    each = list(zip(groups, outputs, buffers))
+    streams = [stream(*one) for one in each] + [appended(*one) for one in each]
+    run_streams(links, streams, [0, 1, 2, 3, 0, 1, 0, 2, 3, 1, 0, 1])
+
+
+def middle(layout, gain, partials, raws, pieces):
+    inputs = [gain.reshape(1, -1)]
+    outputs, scratch = [], []
+    for partial, raw, piece in zip(partials, raws, pieces):
+        inputs += [partial, raw, piece]
+        outputs += [
+            (raw.shape, jnp.float32),
+            (partial.shape, jnp.bfloat16),
+            (piece.shape[1:], jnp.bfloat16),
+        ]
+        scratch += row_buffers(partial.shape) + row_buffers(piece.shape)
+    copies = 6 * layout.tensor.bit_length()
+    return exchange(middle_kernel, layout, 1, inputs, outputs, scratch, copies, "middle")
+
+
+def middle_back_kernel(dp, tensor, *refs):
+    refs = list(refs)
+    links = Links(dp, tensor, *refs[-2:])
+    gain = refs.pop(0)
+    groups = [take(refs, 3) for _ in range(2)]
+    grads = take(refs, 3)
+    gain_sum = refs.pop(0)
+    outputs = [take(refs, 2) for _ in range(2)]
+    results = take(refs, 3)
+    buffers = [take(refs, len(links.row_bits) + 1) for _ in range(2)]
+    spares = [take(refs, len(links.column_bits) + 3) for _ in range(3)]
+    links.greet()
+    gain_sum[...] = jnp.zeros_like(gain_sum)
+
+    def stream(inputs, results, spare):
+        (partial, hidden, cotangent), (grad_hidden, whole) = inputs, results
+        found = []
+        yield from reduce_rows(links, partial, spare[:-1], spare[-1], found)
+        unit, inverse = normalize(hidden[...])
+        width = unit.shape[-1]
+        gain_sum[...] += jnp.sum((found[0] * unit).reshape(-1, 8, width), 0)
+        value = cotangent[...].astype(jnp.float32) + norm_back(
+            found[0], gain[...], unit, inverse
+        )
+        grad_hidden[...] = value
+        whole[0] = value.astype(jnp.bfloat16)
+        yield from gather_rows(links, whole)
+
+    def column(bits, grad, result, spare):
+        def store(value):
+            result[...] = value
+
+        yield from reduce_columns(links, bits, grad, spare[:-3], *spare[-3:], store)
+
+    bits = links.column_bits
+    streams = [stream(*each) for each in zip(groups, outputs, buffers)] + [
+        column(order, *each)
+        for order, each in zip((bits, bits[::-1], bits), zip(grads, results, spares))
+    ]
+    run_streams(links, streams, [0, 1, 4, 2, 3, 0, 1, 0, 4, 1, 2, 3, 4, 2, 3, 0, 1])
+
+
+def middle_back(layout, gain, partials, hiddens, cotangents, grads):
+    inputs = [gain.reshape(1, -1)]
+    outputs, scratch = [((8, gain.shape[0]), jnp.float32)], []
+    for partial, hidden, cotangent in zip(partials, hiddens, cotangents):
+        inputs += [partial, hidden, cotangent]
+        outputs += [(hidden.shape, jnp.float32), (partial.shape, jnp.bfloat16)]
+        scratch += row_buffers(partial.shape)
+    for grad in grads:
+        split = layout.split(grad)
+        inputs.append(split)
+        outputs.append((layout.eighths(grad)[2:], jnp.bfloat16))
+        scratch += column_buffers(split.shape)
+    copies = 4 * layout.tensor.bit_length() + 3 * (layout.columns + 4)
+    return exchange(middle_back_kernel, layout, 2, inputs, outputs, scratch, copies, "middle_back")
+
+
+def leave_kernel(dp, tensor, *refs):
+    refs = list(refs)
+    links = Links(dp, tensor, *refs[-2:])
+    gain, sums = take(refs, 2)
+    tokens = [take(refs, 3) for _ in range(2)]
+    outs = [take(refs, 2) for _ in range(2)]
+    grads = take(refs, 2)
+    total = refs.pop(0)
+    targets, results = take(refs, 4), take(refs, 2)
+    slots = refs.pop(0)
+    buffers = [take(refs, len(links.row_bits) + 2) for _ in range(4)]
+    spares = [take(refs, len(links.column_bits) + 3) for _ in range(2)]
+    links.greet()
+
+    def token_stream(inputs, target, spare):
+        partial, raw, grad_hidden = inputs
+        found = []
+        yield from reduce_rows(links, partial, spare[:-2], spare[-2], found)
+        unit, inverse = normalize(raw[...].astype(jnp.float32))
+        value = grad_hidden[...] + norm_back(found[0], gain[...], unit, inverse)
+        yield from return_rows(links, value.astype(jnp.bfloat16), spare[-1], target)
+
+    def out_stream(inputs, target, spare):
+        partial, hidden = inputs
+        found = []
+        yield from reduce_rows(links, partial, spare[:-2], spare[-2], found)
+        value = (hidden[...] + found[0]).astype(jnp.bfloat16)
+        yield from return_rows(links, value, spare[-1], target)
+
+    def column(bits, grad, result, spare):
+        def store(value):
+            result[links.column, links.core] = value
+
+        yield from reduce_columns(links, bits, grad, spare[:-3], *spare[-3:], store)
+        yield from gather_columns(links, bits, result)
+
+    bits = links.column_bits
+    streams = [token_stream(*each) for each in zip(tokens, targets[:2], buffers[:2])]
+    streams += [out_stream(*each) for each in zip(outs, targets[2:], buffers[2:])]
+    streams += [column(*each) for each in zip((bits, bits[::-1]), grads, results, spares)]
+    streams.append(sum_all(links, sums, slots, total))
+    order = [0, 1, 4, 5, 2, 3, 6, 0, 1, 6, 5, 0, 2, 6, 4, 5, 1, 4, 5, 3, 6, 2, 4, 5, 6, 4, 5, 3]
+    run_streams(links, streams, order)
+
+
+def leave(layout, gain, sums, tokens, outs, grads):
+    inputs = [gain.reshape(1, -1), sums]
+    steps = (layout.dp * layout.tensor).bit_length() - 1
+    outputs, scratch = [(sums.shape, jnp.float32)], [
+        pltpu.VMEM((2 * steps, *sums.shape), jnp.float32)
+    ]
+    for each in tokens + outs:
+        inputs += each
+        owned = each[1].shape
+        outputs.append((owned, jnp.bfloat16))
+        scratch += row_buffers(each[0].shape) + [pltpu.VMEM(owned, jnp.bfloat16)]
+    for grad in grads:
+        inputs.append(layout.split(grad))
+        outputs.append((layout.eighths(grad), jnp.bfloat16))
+        scratch += column_buffers(inputs[-1].shape)
+    copies = 4 * (layout.tensor.bit_length() + 1) + steps + 4 * (layout.columns + 4)
+    return exchange(leave_kernel, layout, 3, inputs, outputs, scratch, copies, "leave")
+
+
 class Group:
     def __init__(self, layout, tokens, memory, older, cotangent, offsets):
         self.layout, self.offsets = layout, layout.swap(offsets)
@@ -816,32 +1222,13 @@
         )
         self.squares = jnp.sum(squares)
 
-    def middle(self, out_weight, gain):
-        layout = self.layout
-        branch = layout.scatter(matmul(self.attention, out_weight))
-        self.hidden = self.raw.astype(jnp.float32) + branch
-        self.hidden_unit, self.hidden_inverse = normalize(self.hidden)
-        self.feed_rows = layout.gather((self.hidden_unit * gain).astype(jnp.bfloat16))
-
     def feed(self, up_weight, down_weight, before):
-        out, back, grad_up, grad_down = feedforward(
+        self.feed_out, self.feed_back, grad_up, grad_down = feedforward(
             self.feed_rows, self.grad_rows, up_weight, down_weight, before
         )
-        self.feed_out, self.feed_back = out, back
         return grad_up, grad_down
 
-    def leave(self):
-        layout = self.layout
-        return layout.swap((self.hidden + layout.scatter(self.feed_out)).astype(jnp.bfloat16))
-
-    def middle_back(self, gain, out_weight):
-        layout = self.layout
-        grad = layout.scatter(self.feed_back)
-        self.feed_gain = jnp.sum(grad * self.hidden_unit, (0, 1))
-        self.grad_hidden = self.cotangent.astype(jnp.float32) + norm_back(
-            grad, gain, self.hidden_unit, self.hidden_inverse
-        )
-        whole = layout.gather(self.grad_hidden.astype(jnp.bfloat16))
+    def branch_back(self, whole, out_weight):
         self.grad_attention = matmul_back(whole, out_weight).astype(jnp.bfloat16)
         return outer(self.attention, whole)
 
@@ -862,20 +1249,13 @@
         grad = matmul_back(self.grad_added, pair_weight)
         grad = norm_back(grad, gain, self.added_unit, self.added_inverse).astype(jnp.bfloat16)
         extent = self.appended.shape[2]
-        pieces = jnp.stack(
+        return jnp.stack(
             [
                 lax.dynamic_slice_in_dim(grad, (layout.shard ^ j) * extent, extent, 2)
                 for j in range(layout.tensor)
             ]
         )
-        return outer(self.stacked, layout.scatter(pieces).astype(jnp.bfloat16))
-
-    def enter_back(self, triple_weight, gain):
-        layout = self.layout
-        grad = layout.scatter(matmul_back(self.grad_triples, triple_weight))
-        unit, inverse = normalize(self.raw.astype(jnp.float32))
-        full = self.grad_hidden + norm_back(grad, gain, unit, inverse)
-        return layout.swap(full.astype(jnp.bfloat16)).astype(jnp.float32)
+
 
     def projection_grads(self):
         width = self.grad_triples.shape[-1] // 3
@@ -939,41 +1319,75 @@
     long = Group(layout, *rows[4:], offsets_long)
     groups = (short, long)
 
-    before = ()
     grad_out = grad_squeeze = grad_triple = 0.0
-    for group in groups:
+    pieces = []
+    for group in groups[::-1]:
         group.enter(attention_gain)
         group.compress(squeeze, pair_weight, attention_gain)
         group.attend(triple_weight, pair_weight)
-        grad_squeeze += group.compress_back(pair_weight, attention_gain)
-        group.middle(output_weight, feedforward_gain)
+        pieces.append(group.compress_back(pair_weight, attention_gain))
+    long.hidden, long.feed_rows, long_added, short.hidden, short.feed_rows, short_added = middle(
+        layout,
+        feedforward_gain,
+        [matmul(group.attention, output_weight).astype(jnp.bfloat16) for group in (long, short)],
+        [long.raw, short.raw],
+        pieces,
+    )
+    grad_squeeze = outer(long.stacked, long_added) + outer(short.stacked, short_added)
+    before = ()
+    for group in groups:
         before = group.feed(up, down, before)
-        grad_out += group.middle_back(feedforward_gain, output_weight)
+    feed_gain, long.grad_hidden, long_back, short.grad_hidden, short_back, *early = middle_back(
+        layout,
+        feedforward_gain,
+        [long.feed_back, short.feed_back],
+        [long.hidden, short.hidden],
+        [long.cotangent, short.cotangent],
+        [*before, grad_squeeze],
+    )
+    up_sum, down_sum, squeeze_sum = (
+        lax.all_gather(eighth, "dp", axis=0, tiled=True).astype(jnp.float32) for eighth in early
+    )
+    for group, whole in ((long, long_back), (short, short_back)):
+        grad_out += group.branch_back(whole, output_weight)
         group.attend_back()
         grad_triple += group.projection_grads()
-    up_sum, down_sum = map(layout.grad, before)
-    squeeze_sum = layout.grad(grad_squeeze).reshape(3, width, local_width)
-    out_sum = layout.grad(grad_out)
-    triple_sum = layout.grad(grad_triple)
     attention_part = (
         jnp.sum(grad_triple * triple_weight.astype(jnp.float32), 1) / attention_gain
     )
-    sums = layout.total(
-        jnp.concatenate(
+    sums = jnp.concatenate(
+        [
+            attention_part,
+            jnp.sum(feed_gain, 0),
+            jnp.full((1024,), short.squares + long.squares),
+        ]
+    ).reshape(-1, 128)
+    sums, short_grad, long_grad, short_out, long_out, triple_sum, out_sum = leave(
+        layout,
+        attention_gain,
+        sums,
+        [
             [
-                attention_part,
-                short.feed_gain + long.feed_gain,
-                jnp.full((128,), short.squares + long.squares),
+                matmul_back(group.grad_triples, triple_weight).astype(jnp.bfloat16),
+                group.raw,
+                group.grad_hidden,
             ]
-        ).reshape(-1, 128)
-    ).reshape(-1)
+            for group in groups
+        ],
+        [[group.feed_out, group.hidden] for group in groups],
+        [grad_triple, grad_out],
+    )
+    sums = sums.reshape(-1)
+    triple_sum = triple_sum.reshape(triple_weight.shape).astype(jnp.float32)
+    out_sum = out_sum.reshape(out_weight.shape).astype(jnp.float32)
+    squeeze_sum = squeeze_sum.reshape(compress_weight.shape)
     gain_one, gain_two, square_total = sums[:width], sums[width : 2 * width], sums[2 * width]
     rows_all = sum(group.count * group.length for group in groups) * layout.dp
     return (
-        short.leave(),
-        long.leave(),
-        short.enter_back(triple_weight, attention_gain),
-        long.enter_back(triple_weight, attention_gain),
+        short_out,
+        long_out,
+        short_grad.astype(jnp.float32),
+        long_grad.astype(jnp.float32),
         short.leave_appended(),
         long.leave_appended(),
         triple_sum[:, :local_width],

time: 772 us -> 740 us (0.959)
  Pallas kernels: 300 us -> 560 us
  waiting for transfers between devices: 138 us -> 7.34 us
  starting transfers between devices: 78.8 us -> 16.9 us
  blocking collectives: 37 us -> 0 us
  other arithmetic: 67.2 us -> 32.8 us
  local copies, waits for them, and re-layouts: 55.6 us -> 22.8 us
    pallas_call x0 -> x3, Pallas kernels: none -> 260 us  [exchange(): pl.pallas_call(functools.partial(kernel, layout.dp, layout.tensor), in_sp...]
    ppermute x55 -> x8, waiting for transfers between devices: 127 us -> 7.29 us  [permute(): return jax.tree.map(lambda part: lax.ppermute(part, AXES, pairs), value)]
    ppermute x55 -> x8, starting transfers between devices: 73.6 us -> 16.8 us  [permute(): return jax.tree.map(lambda part: lax.ppermute(part, AXES, pairs), value)]
    all_gather x3 -> x0, blocking collectives: 37 us -> none  [grad(): mine = lax.all_gather(summed, 'dp', axis_index_groups=self.groups)]
    convert_element_type x28 -> x6, other arithmetic: 28.4 us -> 14 us  [the longest x2 8.23 us: per_device(): lax.all_gather(eighth, 'dp', axis=0, tiled=True).astype(jnp.float32)]
    slice x18 -> x0, local copies, waits for them, and re-layouts: 12.8 us -> none  [scatter(): other = self.flip(value[bit:], bit)]
    ppermute x5 -> x0, waiting for transfers between devices: 11.5 us -> none  [total(): value = value + lax.ppermute(value, axis, pairs)]
    concatenate x10 -> x4, other arithmetic: 12.2 us -> 2.13 us  [gather(): value = jnp.concatenate([value, self.flip(value, bit)], 0)]
  transfers between devices with their start and end apart: 67 -> 11, of which waited for: 25 -> 1; matrix products, arithmetic and copies ran while one was open for 23% -> 15% of each run, Pallas kernels for 39% -> 46%
where the time goes in v4:
time: 740 us; the launch traced here: 735 us
  Pallas kernels  560 us (76%)
  matrix products  77.2 us (10%)
  other arithmetic  32.8 us (4%)
  local copies, waits for them, and re-layouts  22.8 us (3%)
  between operations  18.1 us (2%)
  starting transfers between devices  16.9 us (2%)
    pallas_call x3, Pallas kernels, exchange(): pl.pallas_call(functools.partial(kernel, layout.dp, layout.tensor), in_sp...  260 us
    pallas_call x1, Pallas kernels, fetch(): pl.pallas_call(functools.partial(fetch_kernel, layout.dp, tensor, [rank f...  170 us
    pallas_call x2, Pallas kernels, feedforward(): pl.pallas_call(functools.partial(feedforward_kernel, min(512, hidden)), g...  45 us
    pallas_call x2, Pallas kernels, attend(): pl.pallas_call(functools.partial(attend_kernel, reduced, many), grid_spec...  39.2 us
    pallas_call x2, Pallas kernels, attend_back(): pl.pallas_call(functools.partial(attend_back_kernel, many, heads), grid_s...  37.8 us
    dot_general x12, matrix products, matmul(): jnp.einsum('...k,kn->...n', left, right, preferred_element_type=jnp.float32)  30.8 us
    dot_general x10, matrix products, outer(): jnp.einsum('rk,rn->kn', rows, columns, preferred_element_type=jnp.float32)  29.2 us
    dot_general x6, matrix products, matmul_back(): jnp.einsum('...n,kn->...k', left, right, preferred_element_type=jnp.float32)  17.2 us
  transfers between devices with their start and end apart: 11, of which 1 were waited for; matrix products, arithmetic and copies ran while one was open for 15% of the time, Pallas kernels for 46%

profile of v4, /device:TPU:1, one launch (start us, length us, event | category | flops | bytes accessed | tf_op | source)
XLA Modules:
  0.0 734.9 jit_solution(13816224036672491094)
XLA Ops:
  7.2 5.6 collective-permute-start.3
  12.8 1.9 collective-permute-start
  14.8 169.8 %fetch.1 = (bf16[4,2,128,1024]{3,2,1,0:T(8,128)(2,1)}, bf16[4,2,128,1024]{3,2,1,0:T(8,128)(2,1)}, bf16[4,2,128,1024]{3,2,1,0:T(8,128)(2,1)}, bf16[4,2,128,1024]{...) custom-call(bf16[2,128,1024]{2,1,0:T(8,128)(2,1)} %refs_0_.1, ...), custom_call_target="tpu_custom_call" | custom-call | tf_op jit(solution)/shard_map/fetch/pallas_call | solution.py:712
  184.7 4.2 stack_memory.2
  188.9 2.7 fusion.97
  192.4 3.8 stack_memory.3
  196.2 3.5 convolution_convert_fusion.11
  209.5 2.3 convolution_convert_fusion.4.kc_ref.vc_ref
  211.8 2.3 convolution_convert_fusion.5.km_ref.vm_ref
  214.1 2.3 fusion.69.kc_ref.vc_ref
  216.4 2.8 fusion.68.km_ref.vm_ref
  219.2 3.1 convolution_convert_fusion.2.q_ref.kx_ref.vx_ref
  222.3 3.1 fusion.62.q_ref.kx_ref.vx_ref
  225.4 2.3 slice_bitcast_fusion.1
  228.7 2.2 slice_bitcast_fusion
  235.8 2.9 fusion.96.ka_ref.va_ref
  238.8 24.3 %attend.2 = (bf16[4,1,256,256]{3,2,1,0:T(8,128)(2,1)}, f32[2,1,1024]{2,1,0:T(1,128)}, bf16[1,384,512]{2,1,0:T(8,128)(2,1)}, f32[8,128]{1,0:T(8,128)}) custom-call(s32[1]{0:T(128)} %bitcast.3.me_ref, s32[1]{0:T(128)} %collective-permute-done.offsets_ref, bf16[4,1,256,768]{3,2,1,0:T(8,128)(2,1)} %fusion.62.q_ref.kx_ref.vx_ref, ...), custom_call_target="tpu_custom_call" | custom-call | flops 7247757312 | bytes 110592 | tf_op jit(solution)/shard_map/attend/pallas_call | solution.py:285
  263.1 2.1 fusion.120
  267.0 2.0 convert_bitcast_fusion.1.refs_1_
  274.1 14.9 %attend.3 = (bf16[4,2,128,256]{3,2,1,0:T(8,128)(2,1)}, f32[4,1,512]{2,1,0:T(1,128)}, bf16[2,256,512]{2,1,0:T(8,128)(2,1)}, f32[8,128]{1,0:T(8,128)}) custom-call(s32[1]{0:T(128)} %bitcast.3.me_ref, s32[2]{0:T(128)} %copy-done.64, bf16[4,2,128,768]{3,2,1,0:T(8,128)(2,1)} %convolution_convert_fusion.2.q_ref.kx_ref.vx_ref, ...), custom_call_target="tpu_custom_call" | custom-call | flops 3758096384 | bytes 57344 | tf_op jit(solution)/shard_map/attend/pallas_call | solution.py:285
  289.0 2.3 multiply_reduce_fusion.1
  293.4 2.1 convolution_convert_fusion.refs_4_
  296.6 71.4 %middle.1 = (f32[1,256,1024]{2,1,0:T(8,128)}, bf16[4,1,256,1024]{3,2,1,0:T(8,128)(2,1)}, bf16[1,384,256]{2,1,0:T(8,128)(2,1)}, f32[2,128,1024]{2,1,0:T(8,128)}, ...) custom-call(f32[1,1024]{1,0:T(1,128)} %bitcast.299, ...), custom_call_target="tpu_custom_call" | custom-call | tf_op jit(solution)/shard_map/middle/pallas_call | solution.py:1006
  368.0 3.1 convolution_bitcast_fusion
  371.1 2.2 fusion.30
  373.3 21.0 %feedforward.2 = (bf16[4,2,128,1024]{3,2,1,0:T(8,128)(2,1)}, bf16[4,2,128,1024]{3,2,1,0:T(8,128)(2,1)}, f32[1024,1024]{1,0:T(8,128)}, f32[1024,1024]{1,0:T(8,128)}) custom-call(bf16[4,2,128,1024]{3,2,1,0:T(8,128)(2,1)} %get-tuple-element.93.rows_ref, bf16[4,2,128,1024]{3,2,1,0:T(8,128)(2,1)} %get-tuple-element.94.grad_ref, bf16[1024,1024]{1,0:T(8,128)(2,1)} %bitcast.303, ...), custom_call_target="tpu_custom_call" | custom-call | flops 12884901888 | bytes 20971520 | tf_op jit(solution)/shard_map/feedforward/pallas_call | solution.py:499
  394.3 24.1 %feedforward.3 = (bf16[4,1,256,1024]{3,2,1,0:T(8,128)(2,1)}, bf16[4,1,256,1024]{3,2,1,0:T(8,128)(2,1)}, bf16[1024,1024]{1,0:T(8,128)(2,1)}, bf16[1024,1024]{1,0:T(8,128)(2,1)}) custom-call(bf16[4,1,256,1024]{3,2,1,0:T(8,128)(2,1)} %get-tuple-element.89.rows_ref, bf16[4,1,256,1024]{3,2,1,0:T(8,128)(2,1)} %get-tuple-element.90.grad_ref, ...), custom_call_target="tpu_custom_call" | custom-call | flops 12884901888 | bytes 20971520 | tf_op jit(solution)/shard_map/feedforward/pallas_call | solution.py:499
  418.3 90.4 %middle_back.1 = (f32[8,1024]{1,0:T(8,128)}, f32[1,256,1024]{2,1,0:T(8,128)}, bf16[4,1,256,1024]{3,2,1,0:T(8,128)(2,1)}, f32[2,128,1024]{2,1,0:T(8,128)}, bf16[4...) custom-call(f32[1,1024]{1,0:T(1,128)} %bitcast.300, ...), custom_call_target="tpu_custom_call" | custom-call | tf_op jit(solution)/shard_map/middle_back/pallas_call | solution.py:1006
  508.8 1.9 collective-permute-start.6
  510.8 4.7 collective-permute-start.7
  515.5 7.3 collective-permute-done.7
  525.7 3.1 convolution_convert_fusion.8.do_ref
  528.9 3.1 fusion.93.do_ref
  534.1 23.2 %attend_back.2 = (bf16[4,1,256,768]{3,2,1,0:T(8,128)(2,1)}, bf16[4,1,256,512]{3,2,1,0:T(8,128)(2,1)}, bf16[4,1,256,512]{3,2,1,0:T(8,128)(2,1)}) custom-call(s32[1]{0:T(128)} %bitcast.3.me_ref, s32[1]{0:T(128)} %collective-permute-done.offsets_ref, bf16[4,1,256,768]{3,2,1,0:T(8,128)(2,1)} %fusion.62.q_ref.kx_ref.vx_ref, ...), custom_call_target="tpu_custom_call" | custom-call | flops 16106127360 | bytes 196608 | tf_op jit(solution)/shard_map/attend_back/pallas_call | solution.py:413
  557.2 4.7 fusion.72
  561.9 14.7 %attend_back.3 = (bf16[4,2,128,768]{3,2,1,0:T(8,128)(2,1)}, bf16[4,2,128,512]{3,2,1,0:T(8,128)(2,1)}, bf16[4,2,128,512]{3,2,1,0:T(8,128)(2,1)}) custom-call(s32[1]{0:T(128)} %bitcast.3.me_ref, s32[2]{0:T(128)} %copy-done.64, bf16[4,2,128,768]{3,2,1,0:T(8,128)(2,1)} %convolution_convert_fusion.2.q_ref.kx_ref.vx_ref, ...), custom_call_target="tpu_custom_call" | custom-call | flops 8053063680 | bytes 98304 | tf_op jit(solution)/shard_map/attend_back/pallas_call | solution.py:413
  576.6 4.2 fusion.79
  580.8 4.0 fusion.58
  584.9 3.2 bitcast_add_fusion.3
  591.8 4.1 fusion.122
  599.2 3.2 convert_bitcast_fusion.refs_5_
  602.3 3.4 convolution_convert_fusion.1.refs_2_
  605.7 98.0 %leave.1 = (f32[24,128]{1,0:T(8,128)}, bf16[2,128,1024]{2,1,0:T(8,128)(2,1)}, bf16[1,256,1024]{2,1,0:T(8,128)(2,1)}, bf16[2,128,1024]{2,1,0:T(8,128)(2,1)}, bf16...) custom-call(f32[1,1024]{1,0:T(1,128)} %bitcast.298, ...), custom_call_target="tpu_custom_call" | custom-call | tf_op jit(solution)/shard_map/leave/pallas_call | solution.py:1006
  705.0 2.2 convert_element_type.225
  707.3 2.1 convert_element_type.226
  713.9 3.3 convert.5
  717.2 4.1 convert_element_type.233
  721.3 4.2 convert_element_type.232
  (238 shorter events, 43.3 us)
Async XLA Ops:
  7.2 706.7 %all-gather.8.cloned.1.call-start = ((), (), s32[]{:S(2)}) async-start(), calls=%async_computation.2 | async-start | bytes 1769472 | tf_op jit(solution)/shard_map/all_gather | solution.py:1349
  7.2 266.4 %collective-permute-start.3 = (s32[2]{0:T(128)}, s32[2]{0:T(128)S(1)}, u32[]{:S(2)}, u32[]{:S(2)}) collective-permute-start(s32[2]{0:T(128)} %param.22), channel_id=1, source_target_pairs={{0,0},{1,1},{2,4},{3,5},{4,2},{5,3},{6,6},{7,7},{8,8},{9,9},{10,12... | collective-permute-start | bytes 32 | tf_op jit(solution)/shard_map/ppermute | solution.py:43
  12.8 225.9 %collective-permute-start = (s32[1]{0:T(128)}, s32[1]{0:T(128)}, u32[]{:S(2)}, u32[]{:S(2)}) collective-permute-start(s32[1]{0:T(128)} %param.26), channel_id=1, source_target_pairs={{0,0},{1,1},{2,4},{3,5},{4,2},{5,3},{6,6},{7,7},{8,8},{9,9},{10,12... | collective-permute-start | bytes 20 | tf_op jit(solution)/shard_map/ppermute | solution.py:43
  184.6 4.2 copy-start.55
  191.6 40.3 %copy-start.27 = (bf16[384,256]{0,1:T(8,128)(2,1)}, bf16[384,256]{0,1:T(8,128)(2,1)S(1)}, u32[]{:S(2)}) copy-start(bf16[384,256]{0,1:T(8,128)(2,1)S(1)} %fusion.97) | copy-start | bytes 589828
  191.6 36.1 %collective-permute-start.1 = (bf16[1,1,384,256]{2,3,1,0:T(8,128)(2,1)S(1)}, bf16[1,1,384,256]{2,3,1,0:T(8,128)(2,1)S(1)}, u32[]{:S(2)}, u32[]{:S(2)}) collective-permute-start(bf16[1,1,384,256]{2,3,1,0:T(8,128)(2,1)S(1)} %bitcast.292), channel_id=1, source_target_pairs={{0,1},{1,0},{2,3},{3,2},{4,5},{5,4},{6,7},{7,6},{8,9},{9,8},{10,11... | collective-permute-start | bytes 589832 | tf_op jit(solution)/shard_map/ppermute | solution.py:43
  196.2 4.4 copy-start.5
  199.8 69.3 %copy-start.21 = (bf16[2,256,256]{1,2,0:T(8,128)(2,1)}, bf16[2,256,256]{1,2,0:T(8,128)(2,1)S(1)}, u32[]{:S(2)}) copy-start(bf16[2,256,256]{1,2,0:T(8,128)(2,1)S(1)} %convolution_convert_fusion.11) | copy-start | bytes 786436
  199.8 31.2 %collective-permute-start.4 = (bf16[1,2,256,256]{2,3,1,0:T(8,128)(2,1)S(1)}, bf16[1,2,256,256]{2,3,1,0:T(8,128)(2,1)S(1)}, u32[]{:S(2)}, u32[]{:S(2)}) collective-permute-start(bf16[1,2,256,256]{2,3,1,0:T(8,128)(2,1)S(1)} %bitcast.277), channel_id=1, source_target_pairs={{0,1},{1,0},{2,3},{3,2},{4,5},{5,4},{6,7},{7,6},{8,9},{9,8},{10,11... | collective-permute-start | bytes 786440 | tf_op jit(solution)/shard_map/ppermute | solution.py:43
  201.7 20.7 %copy-start.45 = (f32[4,256]{1,0:T(4,128)}, f32[4,256]{1,0:T(4,128)S(1)}, u32[]{:S(2)}) copy-start(f32[4,256]{1,0:T(4,128)S(1)} %add_rsqrt_fusion.5) | copy-start | bytes 12292
  203.3 15.9 %copy-start.43 = (f32[4,2,128]{2,1,0:T(2,128)}, f32[4,2,128]{2,1,0:T(2,128)S(1)}, u32[]{:S(2)}) copy-start(f32[4,2,128]{2,1,0:T(2,128)S(1)} %add_rsqrt_fusion.2) | copy-start | bytes 12292
  205.0 11.3 %copy-start.39 = (f32[4,256]{1,0:T(4,128)}, f32[4,256]{1,0:T(4,128)S(1)}, u32[]{:S(2)}) copy-start(f32[4,256]{1,0:T(4,128)S(1)} %broadcast_multiply_fusion.4) | copy-start | bytes 12292
  205.8 10.6 %copy-start.53 = (f32[4,256]{1,0:T(4,128)}, f32[4,256]{1,0:T(4,128)S(1)}, u32[]{:S(2)}) copy-start(f32[4,256]{1,0:T(4,128)S(1)} %add_rsqrt_fusion.4) | copy-start | bytes 12292
  206.5 7.6 %copy-start.47 = (f32[4,256]{1,0:T(4,128)}, f32[4,256]{1,0:T(4,128)S(1)}, u32[]{:S(2)}) copy-start(f32[4,256]{1,0:T(4,128)S(1)} %add_rsqrt_fusion.3) | copy-start | bytes 12292
  207.9 3.8 copy-start.37
  227.7 4.1 collective-permute-start.2
  231.8 37.2 %collective-permute-start.5 = (bf16[2,2,256,256]{2,3,1,0:T(8,128)(2,1)}, bf16[2,2,256,256]{2,3,1,0:T(8,128)(2,1)}, u32[]{:S(2)}, u32[]{:S(2)}) collective-permute-start(bf16[2,2,256,256]{2,3,1,0:T(8,128)(2,1)} %pad_maximum_fusion.9), channel_id=1, source_target_pairs={{0,4},{1,5},{2,6},{3,7},{4,0},{5,1},{6,2},{7,3},{8,12},{9,13},{10,... | collective-permute-start | bytes 1572872 | tf_op jit(solution)/shard_map/ppermute | solution.py:43
  238.7 24.3 %copy-start.23 = (bf16[1,1,384,256]{3,2,1,0:T(8,128)(2,1)S(1)}, bf16[1,1,384,256]{3,2,1,0:T(8,128)(2,1)}, u32[]{:S(2)}) copy-start(bf16[1,1,384,256]{3,2,1,0:T(8,128)(2,1)} %copy.47) | copy-start | bytes 589828
  238.7 24.3 %copy-start.24 = (bf16[1,1,384,256]{3,2,1,0:T(8,128)(2,1)S(1)}, bf16[1,1,384,256]{3,2,1,0:T(8,128)(2,1)}, u32[]{:S(2)}) copy-start(bf16[1,1,384,256]{3,2,1,0:T(8,128)(2,1)} %copy.50) | copy-start | bytes 589828
  238.7 24.3 %copy-start.25 = (bf16[1,1,384,256]{3,2,1,0:T(8,128)(2,1)S(1)}, bf16[1,1,384,256]{3,2,1,0:T(8,128)(2,1)}, u32[]{:S(2)}) copy-start(bf16[1,1,384,256]{3,2,1,0:T(8,128)(2,1)} %copy.49) | copy-start | bytes 589828
  238.7 24.3 %copy-start.26 = (bf16[1,1,384,256]{3,2,1,0:T(8,128)(2,1)S(1)}, bf16[1,1,384,256]{3,2,1,0:T(8,128)(2,1)}, u32[]{:S(2)}) copy-start(bf16[1,1,384,256]{3,2,1,0:T(8,128)(2,1)} %copy.48) | copy-start | bytes 589828
  418.3 90.5 %copy-start.22 = (bf16[2,256,256]{1,2,0:T(8,128)(2,1)S(1)}, bf16[2,256,256]{1,2,0:T(8,128)(2,1)}, u32[]{:S(2)}) copy-start(bf16[2,256,256]{1,2,0:T(8,128)(2,1)} %copy-done.21) | copy-start | bytes 786436
  418.3 92.4 %copy-start.28 = (bf16[384,256]{0,1:T(8,128)(2,1)S(1)}, bf16[384,256]{0,1:T(8,128)(2,1)}, u32[]{:S(2)}) copy-start(bf16[384,256]{0,1:T(8,128)(2,1)} %copy-done.27) | copy-start | bytes 589828
  508.8 208.4 %all-gather.6.cloned.1.call-start = ((), (), s32[]{:S(2)}) async-start(), calls=%async_computation.1 | async-start | bytes 2359296 | tf_op jit(solution)/shard_map/all_gather | solution.py:1349
  508.8 14.7 %collective-permute-start.6 = (bf16[2,256,256]{1,2,0:T(8,128)(2,1)S(1)}, bf16[2,256,256]{1,2,0:T(8,128)(2,1)S(1)}, u32[]{:S(2)}, u32[]{:S(2)}) collective-permute-start(bf16[2,256,256]{1,2,0:T(8,128)(2,1)S(1)} %copy-done.22), channel_id=1, source_target_pairs={{0,0},{1,1},{2,4},{3,5},{4,2},{5,3},{6,6},{7,7},{8,8},{9,9},{10,12... | collective-permute-start | bytes 786440 | tf_op jit(solution)/shard_map/ppermute | solution.py:43
  510.8 12.0 %collective-permute-start.7 = (bf16[1,384,256]{1,2,0:T(8,128)(2,1)S(1)}, bf16[1,384,256]{1,2,0:T(8,128)(2,1)S(1)}, u32[]{:S(2)}, u32[]{:S(2)}) collective-permute-start(bf16[1,384,256]{1,2,0:T(8,128)(2,1)S(1)} %bitcast.295), channel_id=1, source_target_pairs={{0,0},{1,1},{2,4},{3,5},{4,2},{5,3},{6,6},{7,7},{8,8},{9,9},{10,12... | collective-permute-start | bytes 589832 | tf_op jit(solution)/shard_map/ppermute | solution.py:43
  528.8 3.8 copy-start.34
  528.9 192.4 %all-gather.4.cloned.1.call-start = ((), (), s32[]{:S(2)}) async-start(), calls=%async_computation | async-start | bytes 2359296 | tf_op jit(solution)/shard_map/all_gather | solution.py:1349
  534.1 23.2 %copy-start.40 = (f32[4,256]{1,0:T(4,128)S(1)}, f32[4,256]{1,0:T(4,128)}, u32[]{:S(2)}) copy-start(f32[4,256]{1,0:T(4,128)} %copy-done.39) | copy-start | bytes 12292
  534.1 23.2 %copy-start.54 = (f32[4,256]{1,0:T(4,128)S(1)}, f32[4,256]{1,0:T(4,128)}, u32[]{:S(2)}) copy-start(f32[4,256]{1,0:T(4,128)} %copy-done.53) | copy-start | bytes 12292
  561.9 14.7 %copy-start.38 = (f32[4,2,128]{2,1,0:T(2,128)S(1)}, f32[4,2,128]{2,1,0:T(2,128)}, u32[]{:S(2)}) copy-start(f32[4,2,128]{2,1,0:T(2,128)} %copy-done.37) | copy-start | bytes 12292
  561.9 14.7 %copy-start.52 = (f32[4,2,128]{2,1,0:T(2,128)S(1)}, f32[4,2,128]{2,1,0:T(2,128)}, u32[]{:S(2)}) copy-start(f32[4,2,128]{2,1,0:T(2,128)} %copy-done.51) | copy-start | bytes 12292
  576.6 4.2 copy-start.7
  576.6 4.2 copy-start.46
  576.6 4.2 copy-start.67
  580.8 4.1 copy-start.11
  580.8 4.1 copy-start.48
  580.8 4.1 copy-start.69
  584.9 3.3 copy-start.9
  584.9 3.3 copy-start.36
  588.3 3.5 copy-start.71
  591.8 4.8 copy-start.13
  591.8 4.8 copy-start.14
  703.8 6.3 copy-start.41
  703.8 6.9 copy-start.29
  705.0 6.8 copy-start.20
  721.3 4.2 copy-start.31
  721.3 5.0 copy-start.30
  (35 other events, 69.9 us)
Sparse Core Ops, SparseCore 0:
  508.9 23.4 all-gather.7
  534.3 27.9 all-gather.5
  585.0 26.8 all-gather.3
